TPU v7x, 32 devices: a whole 2x2x4 slice. The times are simulated.
32 devices in a mesh: seq: 8 (over z, x), tp: 4 (over y, core).
Axes of the slice: x: 2, y: 2, z: 4, core: 2. Of those that a mesh axis runs over, the one named last changes fastest.
Arguments:
- draft_q: bfloat16 [256, 4096], P('seq', 'tp'), may hold values from -48 to 48
- draft_k: bfloat16 [256, 1024], P('seq', 'tp'), may hold values from -24 to 24
- draft_v: bfloat16 [256, 1024], P('seq', 'tp'), may hold values from -6 to 6
- cache_k: bfloat16 [4, 8192, 1024], P(None, 'seq', 'tp'), may hold values from -6 to 6
- cache_v: bfloat16 [4, 8192, 1024], P(None, 'seq', 'tp'), may hold values from -6 to 6
- lengths: int32 [4], replicated, may hold values from 2 to 8184, as said below
- migrating: int32 [4], replicated, may hold values from 0 to 1, as said below
- parents: int32 [4, 64], replicated, may hold values from -1 to 62, as said below
- accepted: int32 [4, 8], replicated, may hold values from -1 to 63, as said below
- out_weight: bfloat16 [4096, 4096], P('tp'), may hold values from -0.09375 to 0.09375
Outputs:
- attn_out: bfloat16 [256, 4096], P('seq', 'tp')
- new_k: bfloat16 [4, 8192, 1024], P(None, 'seq', 'tp')
- new_v: bfloat16 [4, 8192, 1024], P(None, 'seq', 'tp')
Inputs may be any that keep to these rules, and one draw needn't show every extreme that they name: `lengths`: some request has exactly 8184 valid positions. `migrating`: exactly 2 entries are 1. parents[r, 0] = -1 and 0 <= parents[r, i] < i for i >= 1. `accepted`: each row starts with node 0, each further entry's parent is the entry before it, 1 to 8 entries are nodes and the rest are -1; some row has 8 nodes.
All inputs are finite; a program needn't handle non-finite values.
Results may differ from a plain program's by a relative error of at most 0.015.
Values may be sent and summed in bfloat16 or wider, within the bound.
No kernel may reach another device: no remote copies, remote signals or barrier semaphores. Data moves between devices by JAX's collectives and lax.ppermute only.
A program may use at most 128 MiB of HBM per device.

v0:
```python
import math

import jax
import jax.numpy as jnp
from jax import lax
from jax.sharding import PartitionSpec as P

HD = 128


def joined(x, axis, combine):
    everything = jax.tree.map(
        lambda part, kind: lax.all_gather(part.astype(kind), axis),
        x,
        (jnp.bfloat16, jnp.bfloat16, jnp.bfloat16),
    )

    def take(k):
        return jax.tree.map(lambda part, own: part[k].astype(own.dtype), everything, x)

    return lax.fori_loop(
        1, lax.axis_size(axis), lambda k, so_far: combine(so_far, take(k)), take(0)
    )


def ancestry(parents):
    count = parents.shape[1]
    node = jnp.arange(count, dtype=jnp.int32)
    anc = (
        (node[None, :, None] == node[None, None, :]) | (parents[:, :, None] == node[None, None, :])
    ).astype(jnp.float32)
    for step in range(max(1, (count - 1).bit_length())):
        reach = jnp.einsum("rij,rjk->rik", anc, anc, precision=lax.Precision.HIGHEST)
        anc = jnp.where(anc + reach > 0.5, 1.0, 0.0).astype(jnp.float32)
    return anc


def combine(first, second):
    top_one, total_one, sum_one = first
    top_two, total_two, sum_two = second
    top = jnp.maximum(top_one, top_two)
    factor_one = jnp.exp(top_one - top)
    factor_two = jnp.exp(top_two - top)
    return (
        top,
        total_one * factor_one + total_two * factor_two,
        sum_one * factor_one[..., None] + sum_two * factor_two[..., None],
    )


def per_device(
    draft_q, draft_k, draft_v, cache_k, cache_v, lengths, migrating, parents, accepted, out_weight
):
    seq_count = lax.axis_size("seq")
    me_seq = lax.axis_index("seq")
    rows_dev, q_width = draft_q.shape
    requests, drafts = parents.shape
    cache_dev, kv_width = (cache_k.shape[1], cache_k.shape[2])
    kv_local = kv_width // HD
    group = q_width // kv_width
    heads_local = kv_local * group
    block = cache_dev // seq_count
    scale = 1.0 / math.sqrt(HD)
    accept_most = accepted.shape[1]
    q_all, k_all, v_all = (
        lax.all_gather(draft_q, "seq", axis=0, tiled=True),
        lax.all_gather(draft_k, "seq", axis=0, tiled=True),
        lax.all_gather(draft_v, "seq", axis=0, tiled=True),
    )
    order = jnp.argsort(1 - migrating, stable=True)[: requests // 2]
    half = requests // 2
    moved_k, moved_v = (
        lax.all_to_all(
            cache_k[order].reshape(half, seq_count, block, kv_width),
            "seq",
            split_axis=1,
            concat_axis=1,
            tiled=True,
        ),
        lax.all_to_all(
            cache_v[order].reshape(half, seq_count, block, kv_width),
            "seq",
            split_axis=1,
            concat_axis=1,
            tiled=True,
        ),
    )
    canon_k = cache_k.at[order].set(moved_k.reshape(half, cache_dev, kv_width))
    canon_v = cache_v.at[order].set(moved_v.reshape(half, cache_dev, kv_width))
    local = jnp.arange(cache_dev, dtype=jnp.int32)
    canon_pos = me_seq * cache_dev + local
    keys, values = (canon_k, canon_v)
    positions = jnp.broadcast_to(canon_pos[None, :], (requests, cache_dev))
    queries = q_all.reshape(requests, drafts, kv_local, group, HD)

    def partial_attend(operands):
        rows, key_rows, value_rows, live = operands
        scores = (
            jnp.einsum(
                "qkgd,pkd->kgqp",
                rows,
                key_rows.reshape(cache_dev, kv_local, HD),
                preferred_element_type=jnp.float32,
            )
            * scale
        )
        scores = jnp.where(live, scores, -1e30)
        top = jnp.max(scores, axis=-1)
        weights = jnp.where(live, jnp.exp(scores - top[..., None]), 0.0)
        total = jnp.sum(weights, axis=-1)
        summed = jnp.einsum(
            "kgqp,pkd->qkgd",
            weights.astype(jnp.bfloat16),
            value_rows.reshape(cache_dev, kv_local, HD),
            preferred_element_type=jnp.float32,
        )
        return (
            jnp.transpose(top, (2, 0, 1)).reshape(drafts, heads_local),
            jnp.transpose(total, (2, 0, 1)).reshape(drafts, heads_local),
            summed.reshape(drafts, heads_local, HD),
        )

    def nothing(operands):
        return (
            jnp.full((drafts, heads_local), -1e30, jnp.float32),
            jnp.zeros((drafts, heads_local), jnp.float32),
            jnp.zeros((drafts, heads_local, HD), jnp.float32),
        )

    tops, totals, sums = ([], [], [])
    for request in range(requests):
        live = positions[request] < lengths[request]
        top, total, summed = lax.cond(
            jnp.any(live),
            partial_attend,
            nothing,
            (queries[request], keys[request], values[request], live),
        )
        tops.append(top)
        totals.append(total)
        sums.append(summed)
    part_top = jnp.concatenate(tops, axis=0)
    part_total = jnp.concatenate(totals, axis=0)
    part_sum = jnp.concatenate(sums, axis=0)
    first_row = me_seq * rows_dev
    top_all, total_all, sum_all = joined((part_top, part_total, part_sum), "seq", combine)
    top = lax.dynamic_slice_in_dim(top_all, first_row, rows_dev, 0)
    total = lax.dynamic_slice_in_dim(total_all, first_row, rows_dev, 0)
    summed = lax.dynamic_slice_in_dim(sum_all, first_row, rows_dev, 0)
    anc = ancestry(parents).reshape(requests * drafts, drafts)
    anc_rows = lax.dynamic_slice_in_dim(anc, first_row, rows_dev, 0)
    mine = first_row + jnp.arange(rows_dev, dtype=jnp.int32)
    key_index = jnp.arange(requests * drafts, dtype=jnp.int32)
    allowed = (mine[:, None] // drafts == key_index[None, :] // drafts) & (
        jnp.tile(anc_rows, (1, requests)) > 0.5
    )
    own_q = draft_q.reshape(rows_dev, kv_local, group, HD)
    draft_scores = (
        jnp.einsum(
            "rkgd,nkd->rkgn",
            own_q,
            k_all.reshape(requests * drafts, kv_local, HD),
            preferred_element_type=jnp.float32,
        )
        * scale
    )
    draft_scores = jnp.where(allowed[:, None, None, :], draft_scores, -1e30)
    top = top.reshape(rows_dev, kv_local, group)
    new_top = jnp.maximum(top, jnp.max(draft_scores, axis=-1))
    keep = jnp.exp(top - new_top)
    draft_weights = jnp.where(
        allowed[:, None, None, :], jnp.exp(draft_scores - new_top[..., None]), 0.0
    )
    total = total.reshape(rows_dev, kv_local, group) * keep + jnp.sum(draft_weights, axis=-1)
    summed = summed.reshape(rows_dev, kv_local, group, HD) * keep[..., None]
    summed = summed + jnp.einsum(
        "rkgn,nkd->rkgd",
        draft_weights.astype(jnp.bfloat16),
        v_all.reshape(requests * drafts, kv_local, HD),
        preferred_element_type=jnp.float32,
    )
    attention = (summed / total[..., None]).astype(jnp.bfloat16).reshape(rows_dev, q_width)
    partial_out = jnp.dot(attention, out_weight, preferred_element_type=jnp.float32)
    attn_out = lax.psum_scatter(
        partial_out.astype(jnp.bfloat16), "tp", scatter_dimension=1, tiled=True
    )
    valid = accepted >= 0
    node = jnp.maximum(accepted, 0)
    slot = lengths[:, None] + jnp.arange(accept_most, dtype=jnp.int32)[None, :] - me_seq * cache_dev
    slot = jnp.where(valid & (slot >= 0) & (slot < cache_dev), slot, cache_dev)
    request_index = jnp.broadcast_to(jnp.arange(requests, dtype=jnp.int32)[:, None], slot.shape)
    rows_k = jnp.take_along_axis(k_all.reshape(requests, drafts, kv_width), node[..., None], axis=1)
    rows_v = jnp.take_along_axis(v_all.reshape(requests, drafts, kv_width), node[..., None], axis=1)
    new_k = canon_k.at[request_index, slot].set(rows_k, mode="drop")
    new_v = canon_v.at[request_index, slot].set(rows_v, mode="drop")
    return (attn_out, new_k, new_v)


def solution(mesh):
    in_specs = (
        P("seq", "tp"),
        P("seq", "tp"),
        P("seq", "tp"),
        P(None, "seq", "tp"),
        P(None, "seq", "tp"),
        P(),
        P(),
        P(),
        P(),
        P("tp", None),
    )
    out_specs = (P("seq", "tp"), P(None, "seq", "tp"), P(None, "seq", "tp"))
    return jax.shard_map(
        per_device, mesh=mesh, in_specs=in_specs, out_specs=out_specs, check_vma=False
    )
```

profile of v0, /device:TPU:0, one launch (start us, length us, event | category | flops | bytes accessed | tf_op | source)
XLA Modules:
  0.0 364.6 jit_solution(6048291003265357870)
XLA Ops:
  7.2 3.2 copy.235
  11.8 2.2 gather_fusion.1
  15.1 7.3 %all-to-all-start.1 = ((bf16[2,8,128,256]{3,2,0,1:T(8,128)(2,1)}), bf16[2,8,128,256]{3,2,0,1:T(8,128)(2,1)}, u32[]{:S(2)}, u32[]{:S(2)}) async-start(bf16[2,8,128,256]{3,2,0,1:T(8,128)(2,1)} %copy.105), calls=%async_computation.1 | async-start | bytes 2097152 | tf_op jit(solution)/shard_map/all_to_all | solution.py:80
  24.1 24.2 %all-to-all-done.1 = bf16[2,8,128,256]{3,2,0,1:T(8,128)(2,1)} async-done(((bf16[2,8,128,256]{3,2,0,1:T(8,128)(2,1)}), bf16[2,8,128,256]{3,2,0,1:T(8,128)(2,1)}, u32[]{:S(2)}, u32[]{:S(2)}) %all-to-all-start.1) | async-done | bytes 1048608 | tf_op jit(solution)/shard_map/all_to_all | solution.py:80
  48.2 3.6 all-to-all-start
  56.4 1.4 fusion.151
  63.0 38.2 %all_gather.21 = bf16[256,1024]{1,0:T(8,128)(2,1)} all-gather(bf16[32,1024]{1,0:T(8,128)(2,1)S(1)} %copy-done.12), channel_id=1, replica_groups=mesh['seq'=8,'tp'=4] {'seq'}, dimensions={0}, use_global_device_ids=true | all-gather | bytes 589824 | tf_op jit(solution)/shard_map/all_gather | solution.py:66
  101.2 2.4 copy.106
  103.6 3.1 scatter_fusion.1
  107.8 1.9 scatter_fusion
  109.7 13.5 %conditional.4 = (bf16[1,64,8]{1,2,0:T(8,128)(2,1)S(1)}, bf16[1,64,8]{1,2,0:T(8,128)(2,1)S(1)}, bf16[1,64,8,128]{3,2,1,0:T(8,128)(2,1)S(1)}) conditional(s32[]{:T(128)} %convert_element_type.117, () %tuple.87, (pred[1024]{0:T(1024)(128)(4,1)S(1)}, bf16[4,1024,256]{2,1,0:T(8,128)(2,1)S(1)}, bf16[256,1024]{1,0:T(8,128)(2,1)S(1)}, ...), branch_computations={%region_4.5_spmd, %region_5.8_spmd} | conditional | flops 275316224 | bytes 27276340 | solution.py:133
  109.7 2.4 copy.107
  113.3 1.8 bitcast_reduce_fusion
  115.1 4.0 %copy.108 = bf16[4,1024,256]{1,2,0:T(8,128)(2,1)} copy(bf16[4,1024,256]{2,1,0:T(8,128)(2,1)} %get-tuple-element.334) | data formatting | bytes 4194304 | tf_op jit(solution)/shard_map
  120.1 2.4 convolution_convert_fusion
  123.8 14.1 %conditional.5 = (bf16[1,64,8]{1,2,0:T(8,128)(2,1)S(1)}, bf16[1,64,8]{1,2,0:T(8,128)(2,1)}, bf16[1,64,8,128]{3,2,1,0:T(8,128)(2,1)S(1)}) conditional(s32[]{:T(128)} %convert_element_type.118, () %tuple.89, (pred[1024]{0:T(1024)(128)(4,1)S(1)}, bf16[4,1024,256]{2,1,0:T(8,128)(2,1)S(1)}, bf16[256,1024]{1,0:T(8,128)(2,1)S(1)}, ...), branch_computations={%region_9.10_spmd, %region_10.13_spmd} | conditional | flops 275316224 | bytes 27276340 | solution.py:133
  123.8 2.4 copy.109
  127.4 1.8 bitcast_reduce_fusion.1
  129.1 4.0 %copy.110 = bf16[4,1024,256]{1,2,0:T(8,128)(2,1)} copy(bf16[4,1024,256]{2,1,0:T(8,128)(2,1)} %get-tuple-element.338) | data formatting | bytes 4194304 | tf_op jit(solution)/shard_map
  134.2 2.4 convolution_convert_fusion.1
  138.5 14.1 %conditional.6 = (bf16[1,64,8]{1,2,0:T(8,128)(2,1)S(1)}, bf16[1,64,8]{1,2,0:T(8,128)(2,1)}, bf16[1,64,8,128]{3,2,1,0:T(8,128)(2,1)S(1)}) conditional(s32[]{:T(128)} %convert_element_type.119, () %tuple.91, (pred[1024]{0:T(1024)(128)(4,1)S(1)}, bf16[4,1024,256]{2,1,0:T(8,128)(2,1)S(1)}, bf16[256,1024]{1,0:T(8,128)(2,1)S(1)}, ...), branch_computations={%region_14.15_spmd, %region_15.18_spmd} | conditional | flops 275316224 | bytes 27276340 | solution.py:133
  138.5 2.4 copy.111
  142.1 1.8 bitcast_reduce_fusion.2
  143.8 4.0 %copy.112 = bf16[4,1024,256]{1,2,0:T(8,128)(2,1)} copy(bf16[4,1024,256]{2,1,0:T(8,128)(2,1)} %get-tuple-element.342) | data formatting | bytes 4194304 | tf_op jit(solution)/shard_map
  148.9 2.4 convolution_convert_fusion.2
  153.3 14.1 %conditional.7 = (bf16[1,64,8]{1,2,0:T(8,128)(2,1)S(1)}, bf16[1,64,8]{1,2,0:T(8,128)(2,1)}, bf16[1,64,8,128]{3,2,1,0:T(8,128)(2,1)S(1)}) conditional(s32[]{:T(128)} %convert_element_type.120, () %tuple.93, (pred[1024]{0:T(1024)(128)(4,1)S(1)}, bf16[4,1024,256]{2,1,0:T(8,128)(2,1)S(1)}, bf16[256,1024]{1,0:T(8,128)(2,1)S(1)}, ...), branch_computations={%region_19.20_spmd, %region_20.23_spmd} | conditional | flops 275316224 | bytes 27276340 | solution.py:133
  153.3 2.4 copy.113
  156.8 1.8 bitcast_reduce_fusion.3
  158.6 4.0 %copy.114 = bf16[4,1024,256]{1,2,0:T(8,128)(2,1)} copy(bf16[4,1024,256]{2,1,0:T(8,128)(2,1)} %get-tuple-element.346) | data formatting | bytes 4194304 | tf_op jit(solution)/shard_map
  163.6 2.4 convolution_convert_fusion.3
  167.3 1.8 pad_maximum_fusion
  172.8 31.0 %all_gather.25 = bf16[256,256]{1,0:T(8,128)(2,1)S(1)} all-gather(bf16[32,256]{1,0:T(8,128)(2,1)S(1)} %copy-done.14), channel_id=1, replica_groups=mesh['seq'=8,'tp'=4] {'seq'}, dimensions={0}, use_global_device_ids=true | all-gather | bytes 147456 | tf_op jit(solution)/shard_map/all_gather | solution.py:67
  204.0 31.6 %all_gather.26 = bf16[256,256]{1,0:T(8,128)(2,1)S(1)} all-gather(bf16[32,256]{1,0:T(8,128)(2,1)S(1)} %copy-done.15), channel_id=1, replica_groups=mesh['seq'=8,'tp'=4] {'seq'}, dimensions={0}, use_global_device_ids=true | all-gather | bytes 147456 | tf_op jit(solution)/shard_map/all_gather | solution.py:68
  236.4 1.5 fusion.155
  238.7 31.9 %all_gather.23 = bf16[8,256,8]{1,2,0:T(8,128)(2,1)} all-gather(bf16[1,256,8]{1,2,0:T(8,128)(2,1)S(1)} %pad_maximum_fusion.2), channel_id=1, replica_groups=mesh['seq'=8,'tp'=4] {'seq'}, dimensions={0}, use_global_device_ids=true | all-gather | bytes 36864 | tf_op jit(solution)/shard_map/all_gather | solution.py:13
  270.6 32.1 %all_gather.22 = bf16[8,256,8]{1,2,0:T(8,128)(2,1)} all-gather(bf16[1,256,8]{1,2,0:T(8,128)(2,1)S(1)} %pad_maximum_fusion.1), channel_id=1, replica_groups=mesh['seq'=8,'tp'=4] {'seq'}, dimensions={0}, use_global_device_ids=true | all-gather | bytes 36864 | tf_op jit(solution)/shard_map/all_gather | solution.py:13
  305.8 24.8 %while.19 = (s32[]{:T(128)}, f32[256,8]{0,1:T(8,128)}, f32[256,8]{0,1:T(8,128)S(1)}, f32[256,8,128]{2,1,0:T(8,128)S(1)}, bf16[8,256,8]{1,2,0:T(8,128)(2,1)}, /*i...) while((s32[]{:T(128)}, f32[256,8]{0,1:T(8,128)}, ...), condition=%wide.region_24.25_spmd, body=%wide.region_23.24_spmd.sunk | while | flops 1064965 | bytes 2728087 | solution.py:21
  307.4 1.9 fusion.173
  311.0 1.9 fusion.173
  314.5 1.9 fusion.173
  318.0 1.9 fusion.173
  321.6 1.9 fusion.173
  325.1 1.9 fusion.173
  328.6 1.9 fusion.173
  334.6 5.7 %convolution_convert_fusion.4 = bf16[32,4096]{1,0:T(8,128)(2,1)} fusion(bf16[32,1024]{1,0:T(8,128)(2,1)S(1)} %reshape.440, bf16[1024,4096]{1,0:T(8,128)(2,1)} %param.31), kind=kOutput, calls=%fused_computation.88 | convolution fusion | flops 268566528 | bytes 8716288 | tf_op jit(solution)/shard_map/dot_general | solution.py:183
  342.0 4.2 %scatter_fusion.3 = bf16[4,1024,256]{2,1,0:T(8,128)(2,1)} fusion(bf16[4,1024,256]{2,1,0:T(8,128)(2,1)} %scatter_fusion.1, s32[32]{0:T(128)S(1)} %reshape.505, bf16[32,256]{1,0:T(8,128)(2,1)S(1)} %get-tuple-element.381), kind=kCustom, calls=%fused_computation.7 | custom fusion | bytes 49408 | tf_op jit(solution)/shard_map/scatter | solution.py:195
  346.3 2.3 scatter_fusion.2
  348.6 9.2 %reduce-scatter.2.cloned.1.call-done = bf16[32,1024]{1,0:T(8,128)(2,1)} async-done(((bf16[32,4096]{1,0:T(8,128)(2,1)}), bf16[32,1024]{1,0:T(8,128)(2,1)}) %reduce-scatter.2.cloned.1.call-update) | async-done | bytes 65552 | tf_op jit(solution)/shard_map/reduce_scatter | solution.py:184
  (162 shorter events, 53.0 us)
Async XLA Ops:
  7.2 3.2 copy-start.6
  10.4 0.7 copy-start.23
  15.1 33.1 %all-to-all-start.1 = ((bf16[2,8,128,256]{3,2,0,1:T(8,128)(2,1)}), bf16[2,8,128,256]{3,2,0,1:T(8,128)(2,1)}, u32[]{:S(2)}, u32[]{:S(2)}) async-start(bf16[2,8,128,256]{3,2,0,1:T(8,128)(2,1)} %copy.105), calls=%async_computation.1 | async-start | bytes 2097152 | tf_op jit(solution)/shard_map/all_to_all | solution.py:80
  23.0 28.9 %copy-start.16 = (s32[4]{0:T(128)S(1)}, s32[4]{0:T(128)}, u32[]{:S(2)}) copy-start(s32[4]{0:T(128)} %param.27) | copy-start | bytes 52
  23.0 40.0 %copy-start.12 = (bf16[32,1024]{1,0:T(8,128)(2,1)S(1)}, bf16[32,1024]{1,0:T(8,128)(2,1)}, u32[]{:S(2)}) copy-start(bf16[32,1024]{1,0:T(8,128)(2,1)} %param.22) | copy-start | bytes 196612
  48.2 58.5 %all-to-all-start = ((bf16[2,8,128,256]{3,2,0,1:T(8,128)(2,1)}), bf16[2,8,128,256]{3,2,0,1:T(8,128)(2,1)S(1)}, u32[]{:S(2)}, u32[]{:S(2)}) async-start(bf16[2,8,128,256]{3,2,0,1:T(8,128)(2,1)} %copy.103), calls=%async_computation | async-start | bytes 2097152 | tf_op jit(solution)/shard_map/all_to_all | solution.py:73
  51.8 252.9 %all-gather.2.cloned.1.call-start = ((), (), s32[]{:S(2)}) async-start(), calls=%async_computation.3 | async-start | bytes 4718592 | tf_op jit(solution)/shard_map/all_gather | solution.py:13
  107.8 1.9 copy-start.5
  120.1 2.5 copy-start.1
  123.2 0.6 copy-start.19
  123.2 0.6 copy-start.21
  134.2 2.5 copy-start.2
  137.9 0.7 copy-start.9
  148.9 2.5 copy-start.3
  152.6 0.6 copy-start.11
  152.6 14.7 %copy-start.10 = (bf16[1,64,8,128]{3,2,1,0:T(8,128)(2,1)S(1)}, bf16[1,64,8,128]{3,2,1,0:T(8,128)(2,1)}, u32[]{:S(2)}) copy-start(bf16[1,64,8,128]{3,2,1,0:T(8,128)(2,1)} %copy-done.9) | copy-start | bytes 393220
  163.6 2.5 copy-start.4
  167.3 5.5 %copy-start.14 = (bf16[32,256]{1,0:T(8,128)(2,1)S(1)}, bf16[32,256]{1,0:T(8,128)(2,1)}, u32[]{:S(2)}) copy-start(bf16[32,256]{1,0:T(8,128)(2,1)} %param.23) | copy-start | bytes 49156
  167.3 36.6 %copy-start.15 = (bf16[32,256]{1,0:T(8,128)(2,1)S(1)}, bf16[32,256]{1,0:T(8,128)(2,1)}, u32[]{:S(2)}) copy-start(bf16[32,256]{1,0:T(8,128)(2,1)} %param.24) | copy-start | bytes 49156
  169.1 68.8 %copy-start.22 = (bf16[1,64,8]{1,2,0:T(8,128)(2,1)S(1)}, bf16[1,64,8]{1,2,0:T(8,128)(2,1)}, u32[]{:S(2)}) copy-start(bf16[1,64,8]{1,2,0:T(8,128)(2,1)} %copy-done.21) | copy-start | bytes 3076
  169.1 101.4 %copy-start.20 = (bf16[1,64,8]{1,2,0:T(8,128)(2,1)S(1)}, bf16[1,64,8]{1,2,0:T(8,128)(2,1)}, u32[]{:S(2)}) copy-start(bf16[1,64,8]{1,2,0:T(8,128)(2,1)} %copy-done.19) | copy-start | bytes 3076
  169.1 188.6 %reduce-scatter.2.cloned.1.call-start = ((), (), s32[]{:S(2)}) async-start(), calls=%async_computation.4 | async-start | bytes 327680 | tf_op jit(solution)/shard_map/reduce_scatter | solution.py:184
  235.6 69.1 %copy-start.7 = (bf16[256,256]{1,0:T(8,128)(2,1)}, bf16[256,256]{1,0:T(8,128)(2,1)S(1)}, u32[]{:S(2)}) copy-start(bf16[256,256]{1,0:T(8,128)(2,1)S(1)} %all_gather.26) | copy-start | bytes 393220
  236.4 68.3 %copy-start.13 = (pred[32,256]{1,0:T(8,128)(4,1)}, pred[32,256]{1,0:T(8,128)(4,1)S(1)}, u32[]{:S(2)}) copy-start(pred[32,256]{1,0:T(8,128)(4,1)S(1)} %compare_and_fusion) | copy-start | bytes 24580
  334.6 5.7 %copy-start.17 = (s32[4]{0:T(128)S(1)}, s32[4]{0:T(128)}, u32[]{:S(2)}) copy-start(s32[4]{0:T(128)} %param.27) | copy-start | bytes 52
  334.6 5.7 %copy-start.18 = (s32[4,8]{1,0:T(4,128)S(1)}, s32[4,8]{1,0:T(4,128)}, u32[]{:S(2)}) copy-start(s32[4,8]{1,0:T(4,128)} %param.30) | copy-start | bytes 388
  334.6 6.6 %copy-start.8 = (bf16[256,256]{1,0:T(8,128)(2,1)S(1)}, bf16[256,256]{1,0:T(8,128)(2,1)}, u32[]{:S(2)}) copy-start(bf16[256,256]{1,0:T(8,128)(2,1)} %copy-done.7) | copy-start | bytes 393220
  348.5 9.2 %copy-start = (bf16[4,1024,256]{2,1,0:T(8,128)(2,1)}, bf16[4,1024,256]{2,1,0:T(8,128)(2,1)S(1)}, u32[]{:S(2)}) copy-start(bf16[4,1024,256]{2,1,0:T(8,128)(2,1)S(1)} %scatter_fusion.2) | copy-start | bytes 6291460
Sparse Core Ops, SparseCore 0:
  169.3 73.3 all-gather.1
  340.4 17.2 reduce-scatter.1
where the time goes:
time: 367 us; the launch traced here: 365 us
  blocking collectives  165 us (45%)
  local copies, waits for them, and re-layouts  67.1 us (18%)
  other arithmetic  43.6 us (12%)
  waiting for transfers between devices  33.4 us (9%)
  matrix products  27.2 us (7%)
  between operations  17 us (5%)
  starting transfers between devices  10.9 us (3%)
    all_gather x2, blocking collectives, joined(): lax.all_gather(part.astype(kind), axis)  64 us
    all_gather x1, blocking collectives, per_device(): lax.all_gather(draft_q, 'seq', axis=0, tiled=True)  38.2 us
    all_gather x1, blocking collectives, per_device(): lax.all_gather(draft_v, 'seq', axis=0, tiled=True)  31.6 us
    all_gather x1, blocking collectives, per_device(): lax.all_gather(draft_k, 'seq', axis=0, tiled=True)  31 us
    another operation x8, local copies, waits for them, and re-layouts  25.4 us
    all_to_all x1, waiting for transfers between devices, per_device(): lax.all_to_all(cache_v[order].reshape(half, seq_count, block, kv_width),...  24.2 us
    add x7, other arithmetic, combine(): sum_one * factor_one[..., None] + sum_two * factor_two[..., None]  13.5 us
    dot_general x4, matrix products, partial_attend(): jnp.einsum('kgqp,pkd->qkgd', weights.astype(jnp.bfloat16), value_rows.res...  9.41 us
  transfers between devices with their start and end apart: 4, of which 2 were waited for; matrix products, arithmetic and copies ran while one was open for 9% of the time, Pallas kernels for 0%

commit v1 on v0

v1 whole, which is shorter than its diff:
```python
import functools
import math

import jax
import jax.numpy as jnp
from jax import lax
from jax.experimental import pallas as pl
from jax.experimental.pallas import tpu as pltpu
from jax.sharding import PartitionSpec as P

HD = 128
NEG = -1e30
FLOOR = -1e20
STATS = 128
bf16 = jnp.bfloat16
f32 = jnp.float32
i32 = jnp.int32


def nt(a, b):
    return lax.dot_general(a, b, (((1,), (1,)), ((), ())), preferred_element_type=f32)


def tn(a, b):
    return lax.dot_general(a, b, (((0,), (0,)), ((), ())), preferred_element_type=f32)


def split3(x):
    hi = x.astype(bf16).astype(f32)
    rest = x - hi
    mid = rest.astype(bf16).astype(f32)
    return hi, mid, rest - mid


def migrating_pair(mig_ref, requests):
    first = i32(requests)
    last = i32(0)
    for r in reversed(range(requests)):
        first = jnp.where(mig_ref[r] == 1, r, first)
    for r in range(requests):
        last = jnp.where(mig_ref[r] == 1, r, last)
    return first, last


def prep_kernel(me_ref, mig_ref, parents_ref, accepted_ref, dk_ref, dv_ref, ck_ref, cv_ref, *rest, count, block):
    sends = rest[: count - 1]
    bias_ref, acc_ref, rows_ref, sems, acc_sem = rest[count - 1 :]
    requests, drafts = parents_ref.shape
    rows = dk_ref.shape[0]
    accept = accepted_ref.shape[1]
    me = me_ref[0]
    pair = migrating_pair(mig_ref, requests)
    copies = []
    for d in range(1, count):
        target = lax.rem(me + d, count)
        for c, cache in enumerate((ck_ref, cv_ref)):
            for m in range(2):
                copies.append(
                    pltpu.make_async_copy(
                        cache.at[pair[m], pl.ds(pl.multiple_of(target * block, block), block)],
                        sends[d - 1].at[pl.ds((2 * c + m) * block, block)],
                        sems.at[len(copies)],
                    )
                )
                copies[-1].start()
    request = (me * rows) // drafts
    offset = me * rows - request * drafts
    mine = lax.broadcasted_iota(i32, (requests, drafts), 0) == request
    parent = jnp.sum(jnp.where(mine, parents_ref[...], 0), axis=0, keepdims=True)
    down = lax.broadcasted_iota(i32, (drafts, drafts), 0)
    along = lax.broadcasted_iota(i32, (drafts, drafts), 1)
    reach = jnp.where((down == along) | (parent == down), 1.0, 0.0).astype(bf16)
    for _ in range(max(1, (drafts - 1).bit_length())):
        both = jnp.dot(reach, reach, preferred_element_type=f32)
        reach = jnp.where(both > 0.5, 1.0, 0.0).astype(bf16)
    pick = jnp.where(
        lax.broadcasted_iota(i32, (drafts, rows), 0) == lax.broadcasted_iota(i32, (drafts, rows), 1) + offset, 1.0, 0.0
    ).astype(bf16)
    bias_ref[...] = jnp.where(tn(reach, pick) > 0.5, 0.0, NEG)
    mine = lax.broadcasted_iota(i32, (requests, accept), 0) == request
    node = jnp.sum(jnp.where(mine, accepted_ref[...], 0), axis=0, keepdims=True)
    pick = jnp.where(lax.broadcasted_iota(i32, (rows, accept), 0) + offset == node, 1.0, 0.0).astype(bf16)
    chosen = jnp.concatenate([tn(pick, dk_ref[...]), tn(pick, dv_ref[...])], axis=0).astype(bf16)
    acc_ref[...] = chosen
    rows_ref[...] = chosen
    extra = []
    for d in range(1, count):
        extra.append(
            pltpu.make_async_copy(rows_ref, sends[d - 1].at[pl.ds(4 * block, 2 * accept)], acc_sem.at[d - 1])
        )
        extra[-1].start()
    for copy in copies + extra:
        copy.wait()


def attend_kernel(
    base_ref, me_ref, len_ref, mig_ref, *rest, half, count, block, group, drafted
):
    q_refs = rest[:half]
    k_ref, v_ref = rest[half : half + 2]
    rest = rest[half + 2 :]
    if drafted:
        dk_ref, dv_ref, bias_ref = rest[:3]
        rest = rest[3:]
    outs = rest[:half]
    q_all, part = rest[half:]
    step = pl.program_id(0)
    me = me_ref[0]
    spot = lax.rem(me, half)
    rows, q_width = q_refs[0].shape
    cache_dev = k_ref.shape[1]
    kv_local = k_ref.shape[2] // HD
    steps = pl.num_programs(0)
    per_request = q_all.shape[0] // 2
    drafts = per_request * rows
    heads = kv_local * group

    @pl.when(step == 0)
    def _():
        for e in range(half):
            q_all[lax.rem(spot + half - e, half)] = q_refs[e][...].astype(q_all.dtype)

    request = base_ref[0] + step
    row = lax.broadcasted_iota(i32, (1, cache_dev), 1)
    shift = block.bit_length() - 1
    moved = row + (row >> shift) * ((count - 1) * block) + me * block
    position = jnp.where(mig_ref[request] == 1, moved, row + me * cache_dev)
    dead = jnp.where(position < len_ref[request], 0.0, NEG)
    scale = math.log2(math.e) / math.sqrt(HD)
    rows_q = q_all[pl.ds(step * per_request, per_request)].reshape(drafts, q_width)
    tops, totals, sums = [], [], []
    for g in range(kv_local):
        q = jnp.concatenate(
            [rows_q[:, (g * group + j) * HD : (g * group + j + 1) * HD] for j in range(group)], axis=0
        ).astype(bf16)
        s = nt(q, k_ref[0, :, g * HD : (g + 1) * HD]) * scale + dead
        top = jnp.max(s, axis=1, keepdims=True)
        if drafted:
            own = jnp.where(request == (me * rows) // drafts, bias_ref[...], NEG)
            sd = nt(q, dk_ref[:, g * HD : (g + 1) * HD]) * scale + jnp.concatenate([own] * group, axis=0)
            top = jnp.maximum(top, jnp.max(sd, axis=1, keepdims=True))
        top = jnp.maximum(top, FLOOR)
        w = jnp.exp2(s - top)
        total = jnp.sum(w, axis=1, keepdims=True)
        o = jnp.dot(w.astype(bf16), v_ref[0, :, g * HD : (g + 1) * HD], preferred_element_type=f32)
        if drafted:
            wd = jnp.exp2(sd - top)
            total = total + jnp.sum(wd, axis=1, keepdims=True)
            o = o + jnp.dot(wd.astype(bf16), dv_ref[:, g * HD : (g + 1) * HD], preferred_element_type=f32)
        tops.append(top)
        totals.append(total)
        sums.append(o)
    lane = lax.broadcasted_iota(i32, (drafts, STATS), 1)
    stats = jnp.zeros((drafts, STATS), f32)
    for h in range(heads):
        g, j = divmod(h, group)
        at = slice(j * drafts, (j + 1) * drafts)
        values = split3(tops[g][at]) + split3(totals[g][at])[:2]
        for k, value in enumerate(values):
            stats = jnp.where(lane == k * heads + h, value, stats)
    for p in range(per_request):
        at = step * per_request + p
        for h in range(heads):
            g, j = divmod(h, group)
            part[at, :, h * HD : (h + 1) * HD] = sums[g][j * drafts + p * rows : j * drafts + (p + 1) * rows].astype(
                part.dtype
            )
        part[at, :, q_width:] = stats[p * rows : (p + 1) * rows].astype(part.dtype)

    @pl.when(step == steps - 1)
    def _():
        for e in range(half):
            outs[e][...] = part[lax.rem(spot + e, half)].astype(bf16)


def merge(parts, heads):
    width = heads * HD
    stats = [p[:, width:].astype(f32) for p in parts]
    tops = [
        s[:, :heads] + s[:, heads : 2 * heads] + s[:, 2 * heads : 3 * heads] for s in stats
    ]
    totals = [s[:, 3 * heads : 4 * heads] + s[:, 4 * heads : 5 * heads] for s in stats]
    top = functools.reduce(jnp.maximum, tops)
    factors = [jnp.exp2(t - top) for t in tops]
    total = sum(f * t for f, t in zip(factors, totals))
    sums = []
    for h in range(heads):
        sums.append(
            sum(
                f[:, h : h + 1] * p[:, h * HD : (h + 1) * HD].astype(f32) for f, p in zip(factors, parts)
            )
        )
    return top, total, sums


def reduce_kernel(*refs, heads):
    out = refs[-1]
    top, total, sums = merge([r[...] for r in refs[:-1]], heads)
    rows = out.shape[0]
    lane = lax.broadcasted_iota(i32, (rows, STATS), 1)
    stats = jnp.zeros((rows, STATS), f32)
    values = split3(top) + split3(total)[:2]
    for k, value in enumerate(values):
        for h in range(heads):
            stats = jnp.where(lane == k * heads + h, value[:, h : h + 1], stats)
    for h in range(heads):
        out[:, h * HD : (h + 1) * HD] = sums[h].astype(bf16)
    out[:, heads * HD :] = stats.astype(bf16)


def project_kernel(tp_ref, *refs, heads, ways):
    w_ref = refs[-ways - 1]
    parts = refs[: -ways - 1]
    outs = refs[-ways:-1]
    attention_ref = refs[-1]
    top, total, sums = merge([r[...] for r in parts], heads)
    width = w_ref.shape[1] // ways
    for h in range(heads):
        attention_ref[:, h * HD : (h + 1) * HD] = (sums[h] / total[:, h : h + 1]).astype(bf16)
    attention = attention_ref[...]
    for d in range(1, ways):
        target = lax.rem(tp_ref[0] + d, ways)
        w = w_ref[:, pl.ds(pl.multiple_of(target * width, width), width)]
        outs[d - 1][...] = jnp.dot(attention, w, preferred_element_type=f32).astype(bf16)


def finish_kernel(tp_ref, a_ref, w_ref, out_ref, *, ways):
    width = w_ref.shape[1] // ways
    w = w_ref[:, pl.ds(pl.multiple_of(tp_ref[0] * width, width), width)]
    out_ref[...] = jnp.dot(a_ref[...], w, preferred_element_type=f32)


def place_kernel(me_ref, mig_ref, len_ref, accepted_ref, acc_ref, ck_ref, cv_ref, *rest, count, block):
    gots = rest[: count - 1]
    nk_ref, nv_ref, rows_ref, wins_ref, sems, acc_sem, win_sem = rest[count - 1 :]
    requests, accept = accepted_ref.shape
    cache_dev = ck_ref.shape[1]
    me = me_ref[0]
    pair = migrating_pair(mig_ref, requests)
    stay = migrating_pair_other(mig_ref, requests)
    copies = []

    def go(src, dst):
        copies.append(pltpu.make_async_copy(src, dst, sems.at[len(copies)]))
        copies[-1].start()

    extra = [pltpu.make_async_copy(acc_ref, rows_ref.at[me], acc_sem.at[0])]
    extra[-1].start()
    for d in range(1, count):
        source = lax.rem(me + count - d, count)
        extra.append(
            pltpu.make_async_copy(gots[d - 1].at[pl.ds(4 * block, 2 * accept)], rows_ref.at[source], acc_sem.at[d])
        )
        extra[-1].start()
    at_me = pl.ds(pl.multiple_of(me * block, block), block)
    for c, (cache, new) in enumerate(((ck_ref, nk_ref), (cv_ref, nv_ref))):
        for m in range(2):
            go(cache.at[stay[m]], new.at[stay[m]])
            go(cache.at[pair[m], at_me], new.at[pair[m], at_me])
        for d in range(1, count):
            source = lax.rem(me + count - d, count)
            at = pl.ds(pl.multiple_of(source * block, block), block)
            for m in range(2):
                go(gots[d - 1].at[pl.ds((2 * c + m) * block, block)], new.at[pair[m], at])
    for copy in extra + copies:
        copy.wait()
    span = wins_ref.shape[2]
    first = [len_ref[r] - me * cache_dev for r in range(requests)]
    low = [
        pl.multiple_of(jnp.clip((x >> 4) << 4, 0, cache_dev - span), 16) for x in first
    ]
    loads, stores = [], []
    for c, new in enumerate((nk_ref, nv_ref)):
        for r in range(requests):
            a, b = new.at[r, pl.ds(low[r], span)], wins_ref.at[c, r]
            loads.append(pltpu.make_async_copy(a, b, win_sem.at[0, c, r]))
            stores.append(pltpu.make_async_copy(b, a, win_sem.at[1, c, r]))
    for copy in loads:
        copy.start()
    per_request = count // requests
    for copy in loads:
        copy.wait()
    for r in range(requests):
        held = rows_ref[r * per_request].astype(f32)
        for p in range(1, per_request):
            held = held + rows_ref[r * per_request + p].astype(f32)
        row = lax.broadcasted_iota(i32, (span, 1), 0) + low[r]
        for c in range(2):
            window = wins_ref[c, r].astype(f32)
            for i in range(accept):
                hit = (row == first[r] + i) & (accepted_ref[r, i] >= 0)
                window = jnp.where(hit, held[c * accept + i : c * accept + i + 1], window)
            wins_ref[c, r] = window.astype(bf16)
    for copy in stores:
        copy.start()
    for copy in stores:
        copy.wait()


def migrating_pair_other(mig_ref, requests):
    first = i32(requests)
    last = i32(0)
    for r in reversed(range(requests)):
        first = jnp.where(mig_ref[r] == 1, first, r)
    for r in range(requests):
        last = jnp.where(mig_ref[r] == 1, last, r)
    return first, last


SMEM = pl.BlockSpec(memory_space=pltpu.SMEM)
VMEM = pl.BlockSpec(memory_space=pltpu.VMEM)
ANY = pl.BlockSpec(memory_space=pl.ANY)
LIMIT = pltpu.CompilerParams(vmem_limit_bytes=48 << 20)


def per_device(
    draft_q, draft_k, draft_v, cache_k, cache_v, lengths, migrating, parents, accepted, out_weight
):
    count = lax.axis_size("seq")
    ways = lax.axis_size("tp")
    half = count // 2
    me = lax.axis_index("seq").astype(i32)
    tp = lax.axis_index("tp").astype(i32)
    rows, q_width = draft_q.shape
    requests, drafts = parents.shape
    accept = accepted.shape[1]
    cache_dev, kv_width = cache_k.shape[1:]
    group = q_width // kv_width
    heads = q_width // HD
    block = cache_dev // count
    me1 = me.reshape(1)
    tp1 = tp.reshape(1)
    across = [(i, (i + half) % count) for i in range(count)]
    beside = [
        [(i, i // half * half + (i + e) % half) for i in range(count)] for e in range(half)
    ]
    shifts = [[(i, (i + d) % count) for i in range(count)] for d in range(count)]
    turns = [[(i, (i + d) % ways) for i in range(ways)] for d in range(ways)]

    def to_mates(parts):
        return [lax.ppermute(parts[e], "seq", beside[e]) for e in range(1, half)]

    q_mirror = lax.ppermute(draft_q, "seq", across)
    q_mine = [draft_q] + to_mates([draft_q] * half)

    payload = 4 * block + 2 * accept
    prepared = pl.pallas_call(
        functools.partial(prep_kernel, count=count, block=block),
        out_shape=[jax.ShapeDtypeStruct((payload, kv_width), bf16)] * (count - 1)
        + [
            jax.ShapeDtypeStruct((drafts, rows), f32),
            jax.ShapeDtypeStruct((2 * accept, kv_width), bf16),
        ],
        in_specs=[SMEM, SMEM, VMEM, VMEM, VMEM, VMEM, ANY, ANY],
        out_specs=[ANY] * (count - 1) + [VMEM, VMEM],
        scratch_shapes=[
            pltpu.VMEM((2 * accept, kv_width), bf16),
            pltpu.SemaphoreType.DMA((4 * (count - 1),)),
            pltpu.SemaphoreType.DMA((count - 1,)),
        ],
        name="prep",
    )(me1, migrating, parents, accepted, draft_k, draft_v, cache_k, cache_v)
    sends, (bias, acc_rows) = prepared[: count - 1], prepared[count - 1 :]
    gots = [lax.ppermute(sends[d - 1], "seq", shifts[d]) for d in range(1, count)]

    q_theirs = [q_mirror] + to_mates([q_mirror] * half)

    def attend(queries, base, drafted):
        whole = lambda shape: pl.BlockSpec(shape, lambda r, *_: (0,) * len(shape))
        cache_spec = pl.BlockSpec((1, cache_dev, kv_width), lambda r, b, *_: (b[0] + r, 0, 0))
        operands = list(queries) + [cache_k, cache_v]
        specs = [whole((rows, q_width))] * half + [cache_spec] * 2
        if drafted:
            operands += [draft_k, draft_v, bias]
            specs += [whole((rows, kv_width))] * 2 + [whole((drafts, rows))]
        kind = bf16 if rows % 16 == 0 else f32
        return pl.pallas_call(
            functools.partial(
                attend_kernel, half=half, count=count, block=block, group=group, drafted=drafted
            ),
            out_shape=[jax.ShapeDtypeStruct((rows, q_width + STATS), bf16)] * half,
            grid_spec=pltpu.PrefetchScalarGridSpec(
                num_scalar_prefetch=4,
                grid=(requests // 2,),
                in_specs=specs,
                out_specs=[whole((rows, q_width + STATS))] * half,
                scratch_shapes=[
                    pltpu.VMEM((half, rows, q_width), kind),
                    pltpu.VMEM((half, rows, q_width + STATS), kind),
                ],
            ),
            compiler_params=LIMIT,
            name="attend_own" if drafted else "attend_other",
        )(base.reshape(1), me1, lengths, migrating, *operands)

    side = me // half
    mine = attend(q_mine, side * (requests // 2), True)
    theirs = attend(q_theirs, (1 - side) * (requests // 2), False)
    mine_got = to_mates(mine)
    theirs_got = to_mates(theirs)
    theirs_sum = pl.pallas_call(
        functools.partial(reduce_kernel, heads=heads),
        out_shape=jax.ShapeDtypeStruct((rows, q_width + STATS), bf16),
        in_specs=[VMEM] * half,
        out_specs=VMEM,
        name="reduce_other",
    )(theirs[0], *theirs_got)
    crossed = lax.ppermute(theirs_sum, "seq", across)
    width = out_weight.shape[1] // ways
    projected = pl.pallas_call(
        functools.partial(project_kernel, heads=heads, ways=ways),
        out_shape=[jax.ShapeDtypeStruct((rows, width), bf16)] * (ways - 1)
        + [jax.ShapeDtypeStruct((rows, q_width), bf16)],
        in_specs=[SMEM] + [VMEM] * (half + 2),
        out_specs=[VMEM] * ways,
        compiler_params=LIMIT,
        name="project",
    )(tp1, mine[0], *mine_got, crossed, out_weight)
    outs, attention = projected[:-1], projected[-1]
    out_got = [lax.ppermute(outs[d - 1], "tp", turns[d]) for d in range(1, ways)]
    own = pl.pallas_call(
        functools.partial(finish_kernel, ways=ways),
        out_shape=jax.ShapeDtypeStruct((rows, width), f32),
        in_specs=[SMEM, VMEM, VMEM],
        out_specs=VMEM,
        compiler_params=LIMIT,
        name="finish",
    )(tp1, attention, out_weight)
    attn_out = (own + sum(x.astype(f32) for x in out_got)).astype(bf16)

    span = 32
    new_k, new_v = pl.pallas_call(
        functools.partial(place_kernel, count=count, block=block),
        out_shape=[jax.ShapeDtypeStruct(cache_k.shape, bf16)] * 2,
        in_specs=[SMEM] * 4 + [ANY] * (count + 2),
        out_specs=[ANY, ANY],
        scratch_shapes=[
            pltpu.VMEM((count, 2 * accept, kv_width), bf16),
            pltpu.VMEM((2, requests, span, kv_width), bf16),
            pltpu.SemaphoreType.DMA((4 * (count + 1),)),
            pltpu.SemaphoreType.DMA((count,)),
            pltpu.SemaphoreType.DMA((2, 2, requests)),
        ],
        name="place",
    )(me1, migrating, lengths, accepted, acc_rows, cache_k, cache_v, *gots)
    return (attn_out, new_k, new_v)


def solution(mesh):
    in_specs = (
        P("seq", "tp"),
        P("seq", "tp"),
        P("seq", "tp"),
        P(None, "seq", "tp"),
        P(None, "seq", "tp"),
        P(),
        P(),
        P(),
        P(),
        P("tp", None),
    )
    out_specs = (P("seq", "tp"), P(None, "seq", "tp"), P(None, "seq", "tp"))
    return jax.shard_map(
        per_device, mesh=mesh, in_specs=in_specs, out_specs=out_specs, check_vma=False
    )
```

time: 367 us -> 279 us (0.76)
  Pallas kernels: 0 us -> 207 us
  blocking collectives: 165 us -> 0 us
  local copies, waits for them, and re-layouts: 67.1 us -> 4.62 us
  other arithmetic: 43.6 us -> 0.66 us
  starting transfers between devices: 10.9 us -> 44.3 us
  matrix products: 27.2 us -> 0 us
  waiting for transfers between devices: 33.4 us -> 16.9 us
  between operations: 17 us -> 0.85 us
    pallas_call x0 -> x7, Pallas kernels: none -> 207 us  [the longest x1 131 us: per_device(): pl.pallas_call(functools.partial(place_kernel, count=count, block=block),...]
    all_gather x5 -> x0, blocking collectives: 165 us -> none  [the longest x2 64 us: joined(): lax.all_gather(part.astype(kind), axis)]
    ppermute x0 -> x24, starting transfers between devices: none -> 44.3 us  [the longest x7 19.5 us: per_device(): lax.ppermute(sends[d - 1], 'seq', shifts[d])]
    dot_general x17 -> x0, matrix products: 27.2 us -> none  [the longest x4 9.41 us: partial_attend(): jnp.einsum('kgqp,pkd->qkgd', weights.astype(jnp.bfloat16), value_rows.res...]
    another operation x9 -> x0, local copies, waits for them, and re-layouts: 25.4 us -> none
    all_to_all x2 -> x0, waiting for transfers between devices: 24.2 us -> none  [the longest x1 24.2 us: per_device(): lax.all_to_all(cache_v[order].reshape(half, seq_count, block, kv_width),...]
    add x15 -> x0, other arithmetic: 22.7 us -> none  [the longest x7 13.5 us: combine(): sum_one * factor_one[..., None] + sum_two * factor_two[..., None]]
    ppermute x0 -> x24, waiting for transfers between devices: none -> 16.9 us  [the longest x1 12.2 us: per_device(): crossed = lax.ppermute(theirs_sum, 'seq', across)]
  transfers between devices with their start and end apart: 4 -> 24, of which waited for: 2 -> 4; matrix products, arithmetic and copies ran while one was open for 9% -> 0% of each run, Pallas kernels for 0% -> 75%
where the time goes in v1:
time: 279 us; the launch traced here: 274 us
  Pallas kernels  207 us (74%)
  starting transfers between devices  44.3 us (16%)
  waiting for transfers between devices  16.9 us (6%)
  local copies, waits for them, and re-layouts  4.62 us (2%)
    pallas_call x1, Pallas kernels, per_device(): pl.pallas_call(functools.partial(place_kernel, count=count, block=block),...  131 us
    pallas_call x1, Pallas kernels, per_device(): pl.pallas_call(functools.partial(prep_kernel, count=count, block=block),...  58.6 us
    ppermute x7, starting transfers between devices, per_device(): lax.ppermute(sends[d - 1], 'seq', shifts[d])  19.5 us
    ppermute x12, starting transfers between devices, to_mates(): return [lax.ppermute(parts[e], 'seq', beside[e]) for e in range(1, half)]  17.3 us
    ppermute x1, waiting for transfers between devices, per_device(): crossed = lax.ppermute(theirs_sum, 'seq', across)  12.2 us
    pallas_call x2, Pallas kernels, attend(): pl.pallas_call(functools.partial(attend_kernel, half=half, count=count, b...  6.37 us
  transfers between devices with their start and end apart: 24, of which 4 were waited for; matrix products, arithmetic and copies ran while one was open for 0% of the time, Pallas kernels for 75%

profile of v1, /device:TPU:0, one launch (start us, length us, event | category | flops | bytes accessed | tf_op | source)
XLA Modules:
  0.0 274.1 jit_solution(5470024453450419369)
XLA Ops:
  0.6 4.1 %collective-permute-start.6 = (bf16[32,1024]{1,0:T(8,128)(2,1)}, bf16[32,1024]{1,0:T(8,128)(2,1)S(1)}, u32[]{:S(2)}, u32[]{:S(2)}) collective-permute-start(bf16[32,1024]{1,0:T(8,128)(2,1)} %rest_0_.1), channel_id=1, source_target_pairs={{0,16},{4,20},{8,24},{12,28},{16,0},{20,4},{24,8},{28,12},{1,17},{... | collective-permute-start | bytes 196616 | tf_op jit(solution)/shard_map/ppermute | solution.py:343
  4.7 3.9 %collective-permute-done.6.rest_0_ = bf16[32,1024]{1,0:T(8,128)(2,1)S(1)} collective-permute-done((bf16[32,1024]{1,0:T(8,128)(2,1)}, bf16[32,1024]{1,0:T(8,128)(2,1)S(1)}, u32[]{:S(2)}, u32[]{:S(2)}) %collective-permute-start.6) | collective-permute-done | bytes 65568 | tf_op jit(solution)/shard_map/ppermute | solution.py:343
  8.6 1.7 collective-permute-start.7
  10.3 0.5 collective-permute-start.8
  10.8 1.4 collective-permute-start.9
  12.2 58.6 %prep.1 = (bf16[528,256]{1,0:T(8,128)(2,1)}, bf16[528,256]{1,0:T(8,128)(2,1)}, bf16[528,256]{1,0:T(8,128)(2,1)}, bf16[528,256]{1,0:T(8,128)(2,1)}, bf16[528,256]...) custom-call(s32[1]{0:T(128)} %bitcast.2.me_ref, ...), custom_call_target="tpu_custom_call" | custom-call | tf_op jit(solution)/shard_map/prep/pallas_call | solution.py:347
  70.8 0.6 collective-permute-start.17
  71.4 2.2 collective-permute-start
  73.7 0.0 collective-permute-done.7.rest_1_
  73.7 2.5 collective-permute-start.1
  76.2 1.5 collective-permute-start.18
  77.7 1.6 copy-done.1
  79.3 3.0 %attend_other.1 = (bf16[32,1152]{1,0:T(8,128)(2,1)S(1)}, bf16[32,1152]{1,0:T(8,128)(2,1)S(1)}, bf16[32,1152]{1,0:T(8,128)(2,1)S(1)}, bf16[32,1152]{1,0:T(8,128)(2,1)S(1)}) custom-call(s32[1]{0:T(128)} %bitcast.3.base_ref, s32[1]{0:T(128)} %bitcast.2.me_ref, s32[4]{0:T(128)S(1)} %copy-done.9, s32[4]{0:T(128)S(1)} %copy-done.8, ...), custom_call_target="tpu_custom_call" | custom-call | tf_op jit(solution)/shard_map/attend_other/pallas_call | solution.py:377
  82.3 0.6 copy-done.3
  82.9 0.5 collective-permute-done.rest_1_
  83.4 0.0 collective-permute-start.10
  83.5 0.0 collective-permute-done.1.rest_2_
  83.5 1.1 collective-permute-start.11
  84.5 4.8 %collective-permute-start.12 = (bf16[32,1152]{1,0:T(8,128)(2,1)S(1)}, bf16[32,1152]{1,0:T(8,128)(2,1)}, u32[]{:S(2)}, u32[]{:S(2)}) collective-permute-start(bf16[32,1152]{1,0:T(8,128)(2,1)S(1)} %get-tuple-element.34), channel_id=1, source_target_pairs={{0,12},{4,0},{8,4},{12,8},{16,28},{20,16},{24,20},{28,24},{1,13},{... | collective-permute-start | bytes 221192 | tf_op jit(solution)/shard_map/ppermute | solution.py:341
  89.4 1.6 copy-done.2
  91.0 3.4 %attend_own.1 = (bf16[32,1152]{1,0:T(8,128)(2,1)S(1)}, bf16[32,1152]{1,0:T(8,128)(2,1)S(1)}, bf16[32,1152]{1,0:T(8,128)(2,1)S(1)}, bf16[32,1152]{1,0:T(8,128)(2,1)S(1)}) custom-call(s32[1]{0:T(128)} %bitcast.1.base_ref, s32[1]{0:T(128)} %bitcast.2.me_ref, s32[4]{0:T(128)S(1)} %copy-done.9, s32[4]{0:T(128)S(1)} %copy-done.8, bf16[32,1024]{1,0:T(8,128)(2,1)S(1)} %copy-done.4, ...), custom_call_target="tpu_custom_call" | custom-call | tf_op jit(solution)/shard_map/attend_own/pallas_call | solution.py:377
  94.4 0.0 collective-permute-done.10.refs_1_
  94.4 0.1 collective-permute-start.3
  94.5 0.0 collective-permute-done.11.refs_2_
  94.5 0.6 collective-permute-start.4
  95.0 2.4 collective-permute-start.5
  97.4 2.1 reduce_other.1
  99.5 0.2 collective-permute-done.3.refs_1_
  99.7 0.5 collective-permute-start.13
  100.2 0.0 collective-permute-done.4.refs_2_
  100.2 1.6 collective-permute-start.19
  101.7 1.3 collective-permute-start.20
  103.0 0.0 collective-permute-done.17.rest_0_
  103.0 3.5 %collective-permute-start.21 = (bf16[528,256]{1,0:T(8,128)(2,1)}, bf16[528,256]{1,0:T(8,128)(2,1)S(1)}, u32[]{:S(2)}, u32[]{:S(2)}) collective-permute-start(bf16[528,256]{1,0:T(8,128)(2,1)} %get-tuple-element.44), channel_id=1, source_target_pairs={{0,20},{4,24},{8,28},{12,0},{16,4},{20,8},{24,12},{28,16},{1,21},{... | collective-permute-start | bytes 811016 | tf_op jit(solution)/shard_map/ppermute | solution.py:364
  106.5 1.3 collective-permute-start.22
  107.7 12.2 %collective-permute-done.13.refs_4_ = bf16[32,1152]{1,0:T(8,128)(2,1)S(1)} collective-permute-done((bf16[32,1152]{1,0:T(8,128)(2,1)}, bf16[32,1152]{1,0:T(8,128)(2,1)S(1)}, u32[]{:S(2)}, u32[]{:S(2)}) %collective-permute-start.13) | collective-permute-done | bytes 73760 | tf_op jit(solution)/shard_map/ppermute | solution.py:408
  120.0 9.7 %collective-permute-start.23 = (bf16[528,256]{1,0:T(8,128)(2,1)}, bf16[528,256]{1,0:T(8,128)(2,1)S(1)}, u32[]{:S(2)}, u32[]{:S(2)}) collective-permute-start(bf16[528,256]{1,0:T(8,128)(2,1)} %get-tuple-element.46), channel_id=1, source_target_pairs={{0,28},{4,0},{8,4},{12,8},{16,12},{20,16},{24,20},{28,24},{1,29},{... | collective-permute-start | bytes 811016 | tf_op jit(solution)/shard_map/ppermute | solution.py:364
  129.7 4.8 %project.1 = (bf16[32,1024]{1,0:T(8,128)(2,1)S(1)}, bf16[32,1024]{1,0:T(8,128)(2,1)S(1)}, bf16[32,1024]{1,0:T(8,128)(2,1)S(1)}, bf16[32,1024]{1,0:T(8,128)(2,1)S(1)}) custom-call(s32[1]{0:T(128)} %bitcast.tp_ref, bf16[32,1152]{1,0:T(8,128)(2,1)S(1)} %get-tuple-element.27.refs_0_, bf16[32,1152]{1,0:T(8,128)(2,1)S(1)} %collective-permute-done.3.refs_1_, ...), custom_call_target="tpu_custom_call" | custom-call | tf_op jit(solution)/shard_map/project/pallas_call | solution.py:410
  134.5 0.0 copy-done.10
  134.6 0.1 collective-permute-start.14
  134.7 1.6 collective-permute-start.15
  136.3 1.4 collective-permute-start.16
  137.7 0.7 copy-done.14
  138.4 0.1 copy-done.15
  138.5 131.1 %place.1 = (bf16[4,1024,256]{2,1,0:T(8,128)(2,1)}, bf16[4,1024,256]{2,1,0:T(8,128)(2,1)}) custom-call(s32[1]{0:T(128)} %bitcast.2.me_ref, s32[4]{0:T(128)} %mig_ref.7, s32[4]{0:T(128)} %len_ref.5, s32[4,8]{1,0:T(4,128)} %accepted_ref.3, bf16[16,256]{1,0:T(8,128)(2,1)} %get-tuple-element.39.acc_ref, bf16[4,1024,256]{2,1,0:T(8,128)(2,1)} %ck_ref.3, ...), custom_call_target="tpu_custom_call" | custom-call | tf_op jit(solution)/shard_map/place/pallas_call | solution.py:432
  269.6 3.8 %finish.1 = f32[32,1024]{1,0:T(8,128)S(1)} custom-call(s32[1]{0:T(128)} %bitcast.tp_ref, bf16[32,1024]{1,0:T(8,128)(2,1)S(1)} %get-tuple-element.35.a_ref, bf16[1024,4096]{1,0:T(8,128)(2,1)} %w_ref.1), custom_call_target="tpu_custom_call" | custom-call | tf_op jit(solution)/shard_map/finish/pallas_call | solution.py:421
  273.4 0.0 collective-permute-done.15
  273.4 0.7 add_convert_fusion
  (42 shorter events, 0.1 us)
Async XLA Ops:
  0.6 8.0 %collective-permute-start.6 = (bf16[32,1024]{1,0:T(8,128)(2,1)}, bf16[32,1024]{1,0:T(8,128)(2,1)S(1)}, u32[]{:S(2)}, u32[]{:S(2)}) collective-permute-start(bf16[32,1024]{1,0:T(8,128)(2,1)} %rest_0_.1), channel_id=1, source_target_pairs={{0,16},{4,20},{8,24},{12,28},{16,0},{20,4},{24,8},{28,12},{1,17},{... | collective-permute-start | bytes 196616 | tf_op jit(solution)/shard_map/ppermute | solution.py:343
  8.6 65.1 %collective-permute-start.7 = (bf16[32,1024]{1,0:T(8,128)(2,1)S(1)}, bf16[32,1024]{1,0:T(8,128)(2,1)S(1)}, u32[]{:S(2)}, u32[]{:S(2)}) collective-permute-start(bf16[32,1024]{1,0:T(8,128)(2,1)S(1)} %collective-permute-done.6.rest_0_), channel_id=1, source_target_pairs={{0,4},{4,8},{8,12},{12,0},{16,20},{20,24},{24,28},{28,16},{1,5},{5... | collective-permute-start | bytes 196616 | tf_op jit(solution)/shard_map/ppermute | solution.py:341
  10.3 65.9 %collective-permute-start.8 = (bf16[32,1024]{1,0:T(8,128)(2,1)S(1)}, bf16[32,1024]{1,0:T(8,128)(2,1)S(1)}, u32[]{:S(2)}, u32[]{:S(2)}) collective-permute-start(bf16[32,1024]{1,0:T(8,128)(2,1)S(1)} %collective-permute-done.6.rest_0_), channel_id=1, source_target_pairs={{0,8},{4,12},{8,0},{12,4},{16,24},{20,28},{24,16},{28,20},{1,9},{5... | collective-permute-start | bytes 196616 | tf_op jit(solution)/shard_map/ppermute | solution.py:341
  10.8 65.4 %collective-permute-start.9 = (bf16[32,1024]{1,0:T(8,128)(2,1)S(1)}, bf16[32,1024]{1,0:T(8,128)(2,1)S(1)}, u32[]{:S(2)}, u32[]{:S(2)}) collective-permute-start(bf16[32,1024]{1,0:T(8,128)(2,1)S(1)} %collective-permute-done.6.rest_0_), channel_id=1, source_target_pairs={{0,12},{4,0},{8,4},{12,8},{16,28},{20,16},{24,20},{28,24},{1,13},{... | collective-permute-start | bytes 196616 | tf_op jit(solution)/shard_map/ppermute | solution.py:341
  12.2 59.2 %copy-start.4 = (bf16[32,1024]{1,0:T(8,128)(2,1)S(1)}, bf16[32,1024]{1,0:T(8,128)(2,1)}, u32[]{:S(2)}) copy-start(bf16[32,1024]{1,0:T(8,128)(2,1)} %rest_0_.1) | copy-start | bytes 196612
  12.2 65.5 %copy-start = (bf16[4,1024,256]{2,1,0:T(8,128)(2,1)S(1)}, bf16[4,1024,256]{2,1,0:T(8,128)(2,1)}, u32[]{:S(2)}) copy-start(bf16[4,1024,256]{2,1,0:T(8,128)(2,1)} %ck_ref.3) | copy-start | bytes 6291460
  12.2 65.5 %copy-start.8 = (s32[4]{0:T(128)S(1)}, s32[4]{0:T(128)}, u32[]{:S(2)}) copy-start(s32[4]{0:T(128)} %mig_ref.7) | copy-start | bytes 52
  12.2 65.5 %copy-start.9 = (s32[4]{0:T(128)S(1)}, s32[4]{0:T(128)}, u32[]{:S(2)}) copy-start(s32[4]{0:T(128)} %len_ref.5) | copy-start | bytes 52
  70.8 32.2 %collective-permute-start.17 = (bf16[528,256]{1,0:T(8,128)(2,1)}, bf16[528,256]{1,0:T(8,128)(2,1)S(1)}, u32[]{:S(2)}, u32[]{:S(2)}) collective-permute-start(bf16[528,256]{1,0:T(8,128)(2,1)} %get-tuple-element.40), channel_id=1, source_target_pairs={{0,4},{4,8},{8,12},{12,16},{16,20},{20,24},{24,28},{28,0},{1,5},{5... | collective-permute-start | bytes 811016 | tf_op jit(solution)/shard_map/ppermute | solution.py:364
  71.4 12.0 %collective-permute-start = (bf16[32,1024]{1,0:T(8,128)(2,1)S(1)}, bf16[32,1024]{1,0:T(8,128)(2,1)S(1)}, u32[]{:S(2)}, u32[]{:S(2)}) collective-permute-start(bf16[32,1024]{1,0:T(8,128)(2,1)S(1)} %copy-done.4), channel_id=1, source_target_pairs={{0,4},{4,8},{8,12},{12,0},{16,20},{20,24},{24,28},{28,16},{1,5},{5... | collective-permute-start | bytes 196616 | tf_op jit(solution)/shard_map/ppermute | solution.py:341
  73.7 9.8 %collective-permute-start.1 = (bf16[32,1024]{1,0:T(8,128)(2,1)S(1)}, bf16[32,1024]{1,0:T(8,128)(2,1)S(1)}, u32[]{:S(2)}, u32[]{:S(2)}) collective-permute-start(bf16[32,1024]{1,0:T(8,128)(2,1)S(1)} %copy-done.4), channel_id=1, source_target_pairs={{0,8},{4,12},{8,0},{12,4},{16,24},{20,28},{24,16},{28,20},{1,9},{5... | collective-permute-start | bytes 196616 | tf_op jit(solution)/shard_map/ppermute | solution.py:341
  76.1 8.4 %collective-permute-start.2 = (bf16[32,1024]{1,0:T(8,128)(2,1)S(1)}, bf16[32,1024]{1,0:T(8,128)(2,1)S(1)}, u32[]{:S(2)}, u32[]{:S(2)}) collective-permute-start(bf16[32,1024]{1,0:T(8,128)(2,1)S(1)} %copy-done.4), channel_id=1, source_target_pairs={{0,12},{4,0},{8,4},{12,8},{16,28},{20,16},{24,20},{28,24},{1,13},{... | collective-permute-start | bytes 196616 | tf_op jit(solution)/shard_map/ppermute | solution.py:341
  76.2 30.3 %collective-permute-start.18 = (bf16[528,256]{1,0:T(8,128)(2,1)}, bf16[528,256]{1,0:T(8,128)(2,1)}, u32[]{:S(2)}, u32[]{:S(2)}) collective-permute-start(bf16[528,256]{1,0:T(8,128)(2,1)} %get-tuple-element.41), channel_id=1, source_target_pairs={{0,8},{4,12},{8,16},{12,20},{16,24},{20,28},{24,0},{28,4},{1,9},{5... | collective-permute-start | bytes 811016 | tf_op jit(solution)/shard_map/ppermute | solution.py:364
  77.7 1.6 copy-start.1
  79.3 10.1 %copy-start.5 = (bf16[32,256]{1,0:T(8,128)(2,1)S(1)}, bf16[32,256]{1,0:T(8,128)(2,1)}, u32[]{:S(2)}) copy-start(bf16[32,256]{1,0:T(8,128)(2,1)} %rest_6_.1) | copy-start | bytes 49156
  79.3 10.1 %copy-start.6 = (bf16[32,256]{1,0:T(8,128)(2,1)S(1)}, bf16[32,256]{1,0:T(8,128)(2,1)}, u32[]{:S(2)}) copy-start(bf16[32,256]{1,0:T(8,128)(2,1)} %rest_7_.1) | copy-start | bytes 49156
  79.3 10.1 %copy-start.7 = (f32[64,32]{1,0:T(8,128)S(1)}, f32[64,32]{1,0:T(8,128)}, u32[]{:S(2)}) copy-start(f32[64,32]{1,0:T(8,128)} %get-tuple-element.26.rest_8_) | copy-start | bytes 24580
  82.3 0.6 copy-start.3
  83.4 10.9 %collective-permute-start.10 = (bf16[32,1152]{1,0:T(8,128)(2,1)S(1)}, bf16[32,1152]{1,0:T(8,128)(2,1)S(1)}, u32[]{:S(2)}, u32[]{:S(2)}) collective-permute-start(bf16[32,1152]{1,0:T(8,128)(2,1)S(1)} %get-tuple-element.32), channel_id=1, source_target_pairs={{0,4},{4,8},{8,12},{12,0},{16,20},{20,24},{24,28},{28,16},{1,5},{5... | collective-permute-start | bytes 221192 | tf_op jit(solution)/shard_map/ppermute | solution.py:341
  83.5 11.0 %collective-permute-start.11 = (bf16[32,1152]{1,0:T(8,128)(2,1)S(1)}, bf16[32,1152]{1,0:T(8,128)(2,1)}, u32[]{:S(2)}, u32[]{:S(2)}) collective-permute-start(bf16[32,1152]{1,0:T(8,128)(2,1)S(1)} %get-tuple-element.33), channel_id=1, source_target_pairs={{0,8},{4,12},{8,0},{12,4},{16,24},{20,28},{24,16},{28,20},{1,9},{5... | collective-permute-start | bytes 221192 | tf_op jit(solution)/shard_map/ppermute | solution.py:341
  84.5 10.5 %collective-permute-start.12 = (bf16[32,1152]{1,0:T(8,128)(2,1)S(1)}, bf16[32,1152]{1,0:T(8,128)(2,1)}, u32[]{:S(2)}, u32[]{:S(2)}) collective-permute-start(bf16[32,1152]{1,0:T(8,128)(2,1)S(1)} %get-tuple-element.34), channel_id=1, source_target_pairs={{0,12},{4,0},{8,4},{12,8},{16,28},{20,16},{24,20},{28,24},{1,13},{... | collective-permute-start | bytes 221192 | tf_op jit(solution)/shard_map/ppermute | solution.py:341
  89.4 1.6 copy-start.2
  94.4 3.1 %copy-start.16 = (bf16[32,1152]{1,0:T(8,128)(2,1)}, bf16[32,1152]{1,0:T(8,128)(2,1)S(1)}, u32[]{:S(2)}) copy-start(bf16[32,1152]{1,0:T(8,128)(2,1)S(1)} %collective-permute-done.10.refs_1_) | copy-start | bytes 221188
  94.4 5.3 %collective-permute-start.3 = (bf16[32,1152]{1,0:T(8,128)(2,1)S(1)}, bf16[32,1152]{1,0:T(8,128)(2,1)S(1)}, u32[]{:S(2)}, u32[]{:S(2)}) collective-permute-start(bf16[32,1152]{1,0:T(8,128)(2,1)S(1)} %get-tuple-element.28), channel_id=1, source_target_pairs={{0,4},{4,8},{8,12},{12,0},{16,20},{20,24},{24,28},{28,16},{1,5},{5... | collective-permute-start | bytes 221192 | tf_op jit(solution)/shard_map/ppermute | solution.py:341
  94.5 5.7 %collective-permute-start.4 = (bf16[32,1152]{1,0:T(8,128)(2,1)S(1)}, bf16[32,1152]{1,0:T(8,128)(2,1)S(1)}, u32[]{:S(2)}, u32[]{:S(2)}) collective-permute-start(bf16[32,1152]{1,0:T(8,128)(2,1)S(1)} %get-tuple-element.29), channel_id=1, source_target_pairs={{0,8},{4,12},{8,0},{12,4},{16,24},{20,28},{24,16},{28,20},{1,9},{5... | collective-permute-start | bytes 221192 | tf_op jit(solution)/shard_map/ppermute | solution.py:341
  95.0 6.7 %collective-permute-start.5 = (bf16[32,1152]{1,0:T(8,128)(2,1)S(1)}, bf16[32,1152]{1,0:T(8,128)(2,1)S(1)}, u32[]{:S(2)}, u32[]{:S(2)}) collective-permute-start(bf16[32,1152]{1,0:T(8,128)(2,1)S(1)} %get-tuple-element.30), channel_id=1, source_target_pairs={{0,12},{4,0},{8,4},{12,8},{16,28},{20,16},{24,20},{28,24},{1,13},{... | collective-permute-start | bytes 221192 | tf_op jit(solution)/shard_map/ppermute | solution.py:341
  99.7 20.2 %collective-permute-start.13 = (bf16[32,1152]{1,0:T(8,128)(2,1)}, bf16[32,1152]{1,0:T(8,128)(2,1)S(1)}, u32[]{:S(2)}, u32[]{:S(2)}) collective-permute-start(bf16[32,1152]{1,0:T(8,128)(2,1)} %reduce_other.1), channel_id=1, source_target_pairs={{0,16},{4,20},{8,24},{12,28},{16,0},{20,4},{24,8},{28,12},{1,17},{... | collective-permute-start | bytes 221192 | tf_op jit(solution)/shard_map/ppermute | solution.py:408
  100.2 34.4 %collective-permute-start.19 = (bf16[528,256]{1,0:T(8,128)(2,1)}, bf16[528,256]{1,0:T(8,128)(2,1)S(1)}, u32[]{:S(2)}, u32[]{:S(2)}) collective-permute-start(bf16[528,256]{1,0:T(8,128)(2,1)} %get-tuple-element.42), channel_id=1, source_target_pairs={{0,12},{4,16},{8,20},{12,24},{16,28},{20,0},{24,4},{28,8},{1,13},{... | collective-permute-start | bytes 811016 | tf_op jit(solution)/shard_map/ppermute | solution.py:364
  101.7 32.9 %collective-permute-start.20 = (bf16[528,256]{1,0:T(8,128)(2,1)}, bf16[528,256]{1,0:T(8,128)(2,1)S(1)}, u32[]{:S(2)}, u32[]{:S(2)}) collective-permute-start(bf16[528,256]{1,0:T(8,128)(2,1)} %get-tuple-element.43), channel_id=1, source_target_pairs={{0,16},{4,20},{8,24},{12,28},{16,0},{20,4},{24,8},{28,12},{1,17},{... | collective-permute-start | bytes 811016 | tf_op jit(solution)/shard_map/ppermute | solution.py:364
  103.0 31.5 %copy-start.10 = (bf16[528,256]{1,0:T(8,128)(2,1)}, bf16[528,256]{1,0:T(8,128)(2,1)S(1)}, u32[]{:S(2)}) copy-start(bf16[528,256]{1,0:T(8,128)(2,1)S(1)} %collective-permute-done.17.rest_0_) | copy-start | bytes 811012
  103.0 33.2 %collective-permute-start.21 = (bf16[528,256]{1,0:T(8,128)(2,1)}, bf16[528,256]{1,0:T(8,128)(2,1)S(1)}, u32[]{:S(2)}, u32[]{:S(2)}) collective-permute-start(bf16[528,256]{1,0:T(8,128)(2,1)} %get-tuple-element.44), channel_id=1, source_target_pairs={{0,20},{4,24},{8,28},{12,0},{16,4},{20,8},{24,12},{28,16},{1,21},{... | collective-permute-start | bytes 811016 | tf_op jit(solution)/shard_map/ppermute | solution.py:364
  106.5 31.1 %collective-permute-start.22 = (bf16[528,256]{1,0:T(8,128)(2,1)}, bf16[528,256]{1,0:T(8,128)(2,1)S(1)}, u32[]{:S(2)}, u32[]{:S(2)}) collective-permute-start(bf16[528,256]{1,0:T(8,128)(2,1)} %get-tuple-element.45), channel_id=1, source_target_pairs={{0,24},{4,28},{8,0},{12,4},{16,8},{20,12},{24,16},{28,20},{1,25},{... | collective-permute-start | bytes 811016 | tf_op jit(solution)/shard_map/ppermute | solution.py:364
  120.0 17.7 %collective-permute-start.23 = (bf16[528,256]{1,0:T(8,128)(2,1)}, bf16[528,256]{1,0:T(8,128)(2,1)S(1)}, u32[]{:S(2)}, u32[]{:S(2)}) collective-permute-start(bf16[528,256]{1,0:T(8,128)(2,1)} %get-tuple-element.46), channel_id=1, source_target_pairs={{0,28},{4,0},{8,4},{12,8},{16,12},{20,16},{24,20},{28,24},{1,29},{... | collective-permute-start | bytes 811016 | tf_op jit(solution)/shard_map/ppermute | solution.py:364
  134.6 3.1 %copy-start.11 = (bf16[528,256]{1,0:T(8,128)(2,1)}, bf16[528,256]{1,0:T(8,128)(2,1)S(1)}, u32[]{:S(2)}) copy-start(bf16[528,256]{1,0:T(8,128)(2,1)S(1)} %collective-permute-done.19.rest_2_) | copy-start | bytes 811012
  134.6 138.8 %collective-permute-start.14 = (bf16[32,1024]{1,0:T(8,128)(2,1)S(1)}, bf16[32,1024]{1,0:T(8,128)(2,1)S(1)}, u32[]{:S(2)}, u32[]{:S(2)}) collective-permute-start(bf16[32,1024]{1,0:T(8,128)(2,1)S(1)} %get-tuple-element.36), channel_id=1, source_target_pairs={{0,1},{1,2},{2,3},{3,0},{4,5},{5,6},{6,7},{7,4},{8,9},{9,10},{10,1... | collective-permute-start | bytes 196616 | tf_op jit(solution)/shard_map/ppermute | solution.py:420
  134.7 3.0 %copy-start.12 = (bf16[528,256]{1,0:T(8,128)(2,1)}, bf16[528,256]{1,0:T(8,128)(2,1)S(1)}, u32[]{:S(2)}) copy-start(bf16[528,256]{1,0:T(8,128)(2,1)S(1)} %collective-permute-done.20.rest_3_) | copy-start | bytes 811012
  134.7 138.8 %collective-permute-start.15 = (bf16[32,1024]{1,0:T(8,128)(2,1)S(1)}, bf16[32,1024]{1,0:T(8,128)(2,1)S(1)}, u32[]{:S(2)}, u32[]{:S(2)}) collective-permute-start(bf16[32,1024]{1,0:T(8,128)(2,1)S(1)} %get-tuple-element.37), channel_id=1, source_target_pairs={{0,2},{1,3},{2,0},{3,1},{4,6},{5,7},{6,4},{7,5},{8,10},{9,11},{10,... | collective-permute-start | bytes 196616 | tf_op jit(solution)/shard_map/ppermute | solution.py:420
  136.3 1.4 copy-start.13
  136.3 137.2 %collective-permute-start.16 = (bf16[32,1024]{1,0:T(8,128)(2,1)S(1)}, bf16[32,1024]{1,0:T(8,128)(2,1)S(1)}, u32[]{:S(2)}, u32[]{:S(2)}) collective-permute-start(bf16[32,1024]{1,0:T(8,128)(2,1)S(1)} %get-tuple-element.38), channel_id=1, source_target_pairs={{0,3},{1,0},{2,1},{3,2},{4,7},{5,4},{6,5},{7,6},{8,11},{9,8},{10,9... | collective-permute-start | bytes 196616 | tf_op jit(solution)/shard_map/ppermute | solution.py:420
  137.6 0.7 copy-start.14
  137.6 0.8 copy-start.15

commit v2 on v1

v2 whole, which is shorter than its diff:
```python
import functools
import math

import jax
import jax.numpy as jnp
from jax import lax
from jax.experimental import pallas as pl
from jax.experimental.pallas import tpu as pltpu
from jax.sharding import PartitionSpec as P

HD = 128
NEG = -1e30
FLOOR = -1e20
STATS = 128
bf16 = jnp.bfloat16
f32 = jnp.float32
i32 = jnp.int32


def nt(a, b):
    return lax.dot_general(a, b, (((1,), (1,)), ((), ())), preferred_element_type=f32)


def tn(a, b):
    return lax.dot_general(a, b, (((0,), (0,)), ((), ())), preferred_element_type=f32)


def split3(x):
    hi = x.astype(bf16).astype(f32)
    rest = x - hi
    mid = rest.astype(bf16).astype(f32)
    return hi, mid, rest - mid


def migrating_pair(mig_ref, requests, flag=1):
    first = i32(0)
    last = i32(0)
    for r in reversed(range(requests)):
        first = jnp.where(mig_ref[r] == flag, r, first)
    for r in range(requests):
        last = jnp.where(mig_ref[r] == flag, r, last)
    return first, last


def block_copies(me, pair, caches, targets, slots, block, sems, back=False):
    copies = []
    for target, slot in zip(targets, slots):
        at = pl.ds(pl.multiple_of(target * block, block), block)
        for c, cache in enumerate(caches):
            for m in range(2):
                ends = cache.at[pair[m], at], slot.at[pl.ds((2 * c + m) * block, block)]
                copies.append(pltpu.make_async_copy(*(ends[::-1] if back else ends), sems.at[len(copies)]))
    return copies


def prep_kernel(me_ref, mig_ref, parents_ref, accepted_ref, dk_ref, dv_ref, ck_ref, cv_ref, near_ref, *rest, block):
    *outs, bias_ref, hold_ref, load_sems, store_sems, sems = rest
    half = near_ref.shape[0]
    requests, drafts = parents_ref.shape
    rows = dk_ref.shape[0]
    accept = accepted_ref.shape[1]
    me = me_ref[0]
    pair = migrating_pair(mig_ref, requests)
    caches = (ck_ref, cv_ref)
    mine = [me // half * half + t for t in range(half)]
    loads = block_copies(me, pair, caches, mine, [hold_ref.at[t] for t in range(half)], block, load_sems)
    copies = block_copies(me, pair, caches, [me ^ (half + n) for n in range(half)], outs, block, sems)
    for copy in loads + copies:
        copy.start()
    request = (me * rows) // drafts
    offset = me * rows - request * drafts
    mine = lax.broadcasted_iota(i32, (requests, drafts), 0) == request
    parent = jnp.sum(jnp.where(mine, parents_ref[...], 0), axis=0, keepdims=True)
    down = lax.broadcasted_iota(i32, (drafts, drafts), 0)
    along = lax.broadcasted_iota(i32, (drafts, drafts), 1)
    reach = jnp.where((down == along) | (parent == down), 1.0, 0.0).astype(bf16)
    for _ in range(max(1, (drafts - 1).bit_length())):
        both = jnp.dot(reach, reach, preferred_element_type=f32)
        reach = jnp.where(both > 0.5, 1.0, 0.0).astype(bf16)
    pick = jnp.where(
        lax.broadcasted_iota(i32, (drafts, rows), 0) == lax.broadcasted_iota(i32, (drafts, rows), 1) + offset, 1.0, 0.0
    ).astype(bf16)
    bias_ref[...] = jnp.where(tn(reach, pick) > 0.5, 0.0, NEG)
    mine = lax.broadcasted_iota(i32, (requests, accept), 0) == request
    node = jnp.sum(jnp.where(mine, accepted_ref[...], 0), axis=0, keepdims=True)
    pick = jnp.where(lax.broadcasted_iota(i32, (rows, accept), 0) + offset == node, 1.0, 0.0).astype(bf16)
    chosen = jnp.concatenate([tn(pick, dk_ref[...]), tn(pick, dv_ref[...])], axis=0).astype(bf16)
    for out in outs:
        out[4 * block :] = chosen
    stores = []
    for t in range(half):
        hold_ref[t, 4 * block :] = chosen
        for copy in loads[4 * t : 4 * t + 4]:
            copy.wait()
        stores.append(pltpu.make_async_copy(hold_ref.at[t], near_ref.at[t], store_sems.at[t]))
        stores[-1].start()
    for copy in stores + copies:
        copy.wait()


def attend_kernel(me_ref, len_ref, mig_ref, *rest, half, count, block, group, steps):
    q_refs = rest[:half]
    ck_ref, cv_ref, dk_ref, dv_ref, bias_ref = rest[half : half + 5]
    outs = rest[-half - 5 : -5]
    k_ref, v_ref, q_all, part, sems = rest[-5:]
    me = me_ref[0]
    spot = lax.rem(me, half)
    side = me // half
    rows, q_width = q_all.shape[2:]
    cache_dev = k_ref.shape[1]
    kv_local = k_ref.shape[2] // HD
    per_request = half // steps
    drafts = per_request * rows
    heads = kv_local * group
    requests = [side * steps + r for r in range(steps)] + [(1 - side) * steps + r for r in range(steps)]
    loads = []
    for i, request in enumerate(requests):
        for c, (cache, here) in enumerate(((ck_ref, k_ref), (cv_ref, v_ref))):
            loads.append(pltpu.make_async_copy(cache.at[request], here.at[i], sems.at[i, c]))
            loads[-1].start()
    for e in range(half):
        both = q_refs[e][...].astype(q_all.dtype)
        for k in range(2):
            q_all[k, spot ^ e] = both[k * rows : (k + 1) * rows]
    row = lax.broadcasted_iota(i32, (1, cache_dev), 1)
    shift = block.bit_length() - 1
    moved = row + (row >> shift) * ((count - 1) * block) + me * block
    scale = math.log2(math.e) / math.sqrt(HD)
    lane = lax.broadcasted_iota(i32, (drafts, STATS), 1)
    for i, request in enumerate(requests):
        drafted = i < steps
        k, step = divmod(i, steps)
        position = jnp.where(mig_ref[request] == 1, moved, row + me * cache_dev)
        dead = jnp.where(position < len_ref[request], 0.0, NEG)
        rows_q = q_all[k, step * per_request : (step + 1) * per_request].reshape(drafts, q_width)
        loads[2 * i].wait()
        loads[2 * i + 1].wait()
        stats = jnp.zeros((drafts, STATS), f32)
        for g in range(kv_local):
            at_g = slice(g * HD, (g + 1) * HD)
            q = jnp.concatenate(
                [rows_q[:, (g * group + j) * HD : (g * group + j + 1) * HD] for j in range(group)], axis=0
            ).astype(bf16)
            s = nt(q, k_ref[i, :, at_g]) * scale + dead
            top = jnp.max(s, axis=1, keepdims=True)
            if drafted:
                own = jnp.where(request == (me * rows) // drafts, bias_ref[...], NEG)
                sd = nt(q, dk_ref[:, at_g]) * scale + jnp.concatenate([own] * group, axis=0)
                top = jnp.maximum(top, jnp.max(sd, axis=1, keepdims=True))
            top = jnp.maximum(top, FLOOR)
            w = jnp.exp2(s - top)
            total = jnp.sum(w, axis=1, keepdims=True)
            o = jnp.dot(w.astype(bf16), v_ref[i, :, at_g], preferred_element_type=f32)
            if drafted:
                wd = jnp.exp2(sd - top)
                total = total + jnp.sum(wd, axis=1, keepdims=True)
                o = o + jnp.dot(wd.astype(bf16), dv_ref[:, at_g], preferred_element_type=f32)
            for j in range(group):
                h = g * group + j
                at = slice(j * drafts, (j + 1) * drafts)
                values = split3(top[at]) + split3(total[at])[:2]
                for n, value in enumerate(values):
                    stats = jnp.where(lane == n * heads + h, value, stats)
                for p in range(per_request):
                    part[k, step * per_request + p, :, h * HD : (h + 1) * HD] = o[
                        j * drafts + p * rows : j * drafts + (p + 1) * rows
                    ].astype(part.dtype)
        for p in range(per_request):
            part[k, step * per_request + p, :, q_width:] = stats[p * rows : (p + 1) * rows].astype(part.dtype)
    for e in range(half):
        outs[e][...] = jnp.concatenate([part[k, spot ^ e] for k in range(2)], axis=0).astype(bf16)


def view(ref, k, rows):
    def get(at):
        if rows % 16 == 0 or ref.shape[0] == rows:
            return ref[k * rows : (k + 1) * rows, at].astype(f32)
        return ref[:, at].astype(f32)[k * rows : (k + 1) * rows]

    return get


def merge(parts, heads):
    width = heads * HD
    stats = [get(slice(width, width + STATS)) for get in parts]
    tops = [s[:, :heads] + s[:, heads : 2 * heads] + s[:, 2 * heads : 3 * heads] for s in stats]
    totals = [s[:, 3 * heads : 4 * heads] + s[:, 4 * heads : 5 * heads] for s in stats]
    top = functools.reduce(jnp.maximum, tops)
    factors = [jnp.exp2(t - top) for t in tops]
    total = sum(f * t for f, t in zip(factors, totals))
    sums = []
    for h in range(heads):
        sums.append(sum(f[:, h : h + 1] * get(slice(h * HD, (h + 1) * HD)) for f, get in zip(factors, parts)))
    return top, total, sums


def reduce_kernel(*refs, heads):
    all_ref, out, sems = refs[-3:]
    rows = out.shape[0]
    top, total, sums = merge([view(r, 1, rows) for r in refs[:-3]], heads)
    lane = lax.broadcasted_iota(i32, (rows, STATS), 1)
    stats = jnp.zeros((rows, STATS), f32)
    values = split3(top) + split3(total)[:2]
    for k, value in enumerate(values):
        for h in range(heads):
            stats = jnp.where(lane == k * heads + h, value[:, h : h + 1], stats)
    for h in range(heads):
        out[:, h * HD : (h + 1) * HD] = sums[h].astype(bf16)
    out[:, heads * HD :] = stats.astype(bf16)
    copies = [pltpu.make_async_copy(out, all_ref.at[t], sems.at[t]) for t in range(2)]
    for copy in copies:
        copy.start()
    for copy in copies:
        copy.wait()


def weight_blocks(tp_ref, w_ref, here_ref, sems, targets):
    width = here_ref.shape[2]
    loads = []
    for n, target in enumerate(targets):
        at = pl.ds(pl.multiple_of((tp_ref[0] ^ target) * width, width), width)
        loads.append(pltpu.make_async_copy(w_ref.at[:, at], here_ref.at[n], sems.at[n]))
        loads[-1].start()
    return loads


def project_kernel(tp_ref, me_ref, done_ref, *refs, heads, targets):
    *parts, crossed_ref, w_ref, out_ref, attention_ref, here_ref, sems = refs
    width = here_ref.shape[2]
    loads = weight_blocks(tp_ref, w_ref, here_ref, sems, targets)
    rows = attention_ref.shape[0]
    other = 1 - me_ref[0] // len(parts)
    crossed = lambda at: crossed_ref[other, :, at].astype(f32)
    top, total, sums = merge([view(r, 0, rows) for r in parts] + [crossed], heads)
    for h in range(heads):
        attention_ref[:, h * HD : (h + 1) * HD] = (sums[h] / total[:, h : h + 1]).astype(bf16)
    attention = attention_ref[...]
    for n, load in enumerate(loads):
        load.wait()
        out_ref[:, n * width : (n + 1) * width] = jnp.dot(
            attention, here_ref[n], preferred_element_type=f32
        ).astype(bf16)


def finish_kernel(tp_ref, done_ref, a_ref, w_ref, *rest, targets):
    *outs, here_ref, sems = rest
    loads = weight_blocks(tp_ref, w_ref, here_ref, sems, targets)
    attention = a_ref[...]
    for n, load in enumerate(loads):
        load.wait()
        outs[n][...] = jnp.dot(attention, here_ref[n], preferred_element_type=f32)


def side_kernel(me_ref, mig_ref, ck_ref, cv_ref, after_ref, near_ref, *rest, which, block):
    gots = rest[: len(which)]
    nk_ref, nv_ref, done_ref, hold_ref, sems, near_sems, put_sems = rest[len(which) :]
    me = me_ref[0]
    half = near_ref.shape[0]
    stay = migrating_pair(mig_ref, ck_ref.shape[0], 0)
    pair = migrating_pair(mig_ref, ck_ref.shape[0])
    news = (nk_ref, nv_ref)
    loads, stores = [], []
    for c, cache in enumerate((ck_ref, cv_ref)):
        for m in range(2):
            loads.append(pltpu.make_async_copy(cache.at[stay[m]], hold_ref.at[c, m], sems.at[0, c, m]))
            stores.append(pltpu.make_async_copy(hold_ref.at[c, m], news[c].at[stay[m]], sems.at[1, c, m]))
    mine = [me // half * half + t for t in range(half)]
    copies = block_copies(me, pair, news, mine, [near_ref.at[t] for t in range(half)], block, near_sems, back=True)
    copies += block_copies(me, pair, news, [me ^ d for d in which], gots, block, put_sems, back=True)
    for copy in loads + copies:
        copy.start()
    done_ref[...] = jnp.zeros_like(done_ref)
    for load, store in zip(loads, stores):
        load.wait()
        store.start()
    for copy in stores + copies:
        copy.wait()


def put_kernel(me_ref, mig_ref, *rest, which, block):
    gots = rest[: len(which)]
    fk_ref, fv_ref, nk_ref, nv_ref, done_ref, sems = rest[len(which) :]
    pair = migrating_pair(mig_ref, mig_ref.shape[0])
    done_ref[...] = jnp.zeros_like(done_ref)
    me = me_ref[0]
    copies = block_copies(me, pair, (nk_ref, nv_ref), [me ^ d for d in which], gots, block, sems, back=True)
    for copy in copies:
        copy.start()
    for copy in copies:
        copy.wait()


def place_kernel(me_ref, mig_ref, len_ref, accepted_ref, near_ref, *rest, block):
    *gots, fk_ref, fv_ref, nk_ref, nv_ref, wins_ref, win_sem = rest
    requests, accept = accepted_ref.shape
    half = len(gots)
    count = 2 * half
    cache_dev = nk_ref.shape[1]
    me = me_ref[0]
    span = wins_ref.shape[2]
    first = [len_ref[r] - me * cache_dev for r in range(requests)]
    low = [pl.multiple_of(jnp.clip((x >> 4) << 4, 0, cache_dev - span), 16) for x in first]
    loads, stores = [], []
    for c, new in enumerate((nk_ref, nv_ref)):
        for r in range(requests):
            a, b = new.at[r, pl.ds(low[r], span)], wins_ref.at[c, r]
            loads.append(pltpu.make_async_copy(a, b, win_sem.at[0, c, r]))
            stores.append(pltpu.make_async_copy(b, a, win_sem.at[1, c, r]))
    for copy in loads:
        copy.start()
    per_request = count // requests
    for copy in loads:
        copy.wait()
    for r in range(requests):
        held = jnp.zeros((2 * accept, nk_ref.shape[2]), f32)
        for t in range(half):
            owner = me // half * half + t
            held = held + jnp.where(owner // per_request == r, near_ref[t, 4 * block :].astype(f32), 0.0)
        for n in range(half):
            owner = me ^ (half + n)
            held = held + jnp.where(owner // per_request == r, gots[n][4 * block :].astype(f32), 0.0)
        row = lax.broadcasted_iota(i32, (span, 1), 0) + low[r]
        for c in range(2):
            window = wins_ref[c, r].astype(f32)
            for i in range(accept):
                hit = (row == first[r] + i) & (accepted_ref[r, i] >= 0)
                window = jnp.where(hit, held[c * accept + i : c * accept + i + 1], window)
            wins_ref[c, r] = window.astype(bf16)
    for copy in stores:
        copy.start()
    for copy in stores:
        copy.wait()


SMEM = pl.BlockSpec(memory_space=pltpu.SMEM)
VMEM = pl.BlockSpec(memory_space=pltpu.VMEM)
HBM = pl.BlockSpec(memory_space=pltpu.HBM)

CHEAP = pl.CostEstimate(flops=1, transcendentals=0, bytes_accessed=1)


def limit(mib):
    return pltpu.CompilerParams(vmem_limit_bytes=mib << 20)


def per_device(
    draft_q, draft_k, draft_v, cache_k, cache_v, lengths, migrating, parents, accepted, out_weight
):
    count = lax.axis_size("seq")
    ways = lax.axis_size("tp")
    half = count // 2
    me = lax.axis_index("seq").astype(i32)
    tp = lax.axis_index("tp").astype(i32)
    rows, q_width = draft_q.shape
    requests, drafts = parents.shape
    accept = accepted.shape[1]
    cache_dev, kv_width = cache_k.shape[1:]
    group = q_width // kv_width
    heads = q_width // HD
    block = cache_dev // count
    draft_k, draft_v, cache_k, cache_v, lengths, migrating, parents, accepted, out_weight = [
        pltpu.with_memory_space_constraint(x, pltpu.HBM)
        for x in (draft_k, draft_v, cache_k, cache_v, lengths, migrating, parents, accepted, out_weight)
    ]
    me1 = me.reshape(1)
    tp1 = tp.reshape(1)
    across = [(i, (i + half) % count) for i in range(count)]
    beside = [[(i, i ^ e) for i in range(count)] for e in range(half)]

    def to_mates(parts):
        return [lax.ppermute(parts[e], "seq", beside[e]) for e in range(1, half)]

    q_mirror = lax.ppermute(draft_q, "seq", across)

    payload = 4 * block + 2 * accept
    near_send, *sends, bias = pl.pallas_call(
        functools.partial(prep_kernel, block=block),
        out_shape=[pltpu.HBM((half, payload, kv_width), bf16)]
        + [pltpu.VMEM((payload, kv_width), bf16)] * half
        + [pltpu.VMEM((drafts, rows), f32)],
        in_specs=[SMEM, SMEM, VMEM, VMEM, VMEM, VMEM, HBM, HBM],
        out_specs=[HBM] + [VMEM] * (half + 1),
        scratch_shapes=[
            pltpu.VMEM((half, payload, kv_width), bf16),
            pltpu.SemaphoreType.DMA((4 * half,)),
            pltpu.SemaphoreType.DMA((half,)),
            pltpu.SemaphoreType.DMA((4 * half,)),
        ],
        compiler_params=limit(4),
        cost_estimate=CHEAP,
        name="prep",
    )(me1, migrating, parents, accepted, draft_k, draft_v, cache_k, cache_v)
    sides = [list(range(k * half, (k + 1) * half)) for k in range(2)]
    q_mirror, sends = lax.optimization_barrier((q_mirror, sends))
    q_both = jnp.concatenate([draft_q, q_mirror], axis=0)
    q_got = to_mates([q_both] * half)
    near_send, _ = lax.optimization_barrier((near_send, q_got))
    near = lax.all_to_all(near_send, "seq", 0, 0, axis_index_groups=sides, tiled=True)
    gots = [None] * count

    def migrate(which, after):
        for d in which:
            send, _ = lax.optimization_barrier((sends[d - half], after))
            gots[d] = lax.ppermute(send, "seq", [(i, i ^ d) for i in range(count)])

    def part(which, k, n):
        which = list(which)
        return which[k * len(which) // n : (k + 1) * len(which) // n]

    groups = [part(range(half, count), k, 4) for k in range(4)]
    migrate(groups[0] + groups[1], q_got)
    steps = requests // 2
    kind = bf16 if rows % 16 == 0 else f32
    parts = pl.pallas_call(
        functools.partial(attend_kernel, half=half, count=count, block=block, group=group, steps=steps),
        out_shape=[pltpu.VMEM((2 * rows, q_width + STATS), bf16)] * half,
        in_specs=[SMEM] * 3 + [VMEM] * half + [HBM] * 2 + [VMEM] * 3,
        out_specs=[VMEM] * half,
        scratch_shapes=[
            pltpu.VMEM((2 * steps, cache_dev, kv_width), bf16),
            pltpu.VMEM((2 * steps, cache_dev, kv_width), bf16),
            pltpu.VMEM((2, half, rows, q_width), kind),
            pltpu.VMEM((2, half, rows, q_width + STATS), kind),
            pltpu.SemaphoreType.DMA((2 * steps, 2)),
        ],
        compiler_params=limit(20),
        cost_estimate=CHEAP,
        name="attend",
    )(me1, lengths, migrating, q_both, *q_got, cache_k, cache_v, draft_k, draft_v, bias)
    parts_got = to_mates(parts)
    shapes = [pltpu.HBM(cache_k.shape, bf16)] * 2
    token = pltpu.VMEM((8, 128), f32)

    def put(which, new_k, new_v):
        return pl.pallas_call(
            functools.partial(put_kernel, which=which, block=block),
            out_shape=shapes + [token],
            in_specs=[SMEM] * 2 + [VMEM] * len(which) + [HBM] * 2,
            out_specs=[HBM, HBM, VMEM],
            input_output_aliases={2 + len(which): 0, 3 + len(which): 1},
            scratch_shapes=[pltpu.SemaphoreType.DMA((4 * len(which),))],
            compiler_params=limit(2),
            cost_estimate=CHEAP,
            name="put",
        )(me1, migrating, *[gots[d] for d in which], new_k, new_v)

    migrate(groups[2], [gots[d] for d in groups[0]])
    early = groups[0] + groups[1]
    new_k, new_v, done = pl.pallas_call(
        functools.partial(side_kernel, which=early, block=block),
        out_shape=shapes + [token],
        in_specs=[SMEM, SMEM, HBM, HBM] + [VMEM] * (2 + len(early)),
        out_specs=[HBM, HBM, VMEM],
        scratch_shapes=[
            pltpu.VMEM((2, 2, cache_dev, kv_width), bf16),
            pltpu.SemaphoreType.DMA((2, 2, 2)),
            pltpu.SemaphoreType.DMA((4 * half,)),
            pltpu.SemaphoreType.DMA((4 * len(early),)),
        ],
        compiler_params=limit(4),
        cost_estimate=CHEAP,
        name="side",
    )(me1, migrating, cache_k, cache_v, parts[0], near, *[gots[d] for d in early])
    theirs_sum = pl.pallas_call(
        functools.partial(reduce_kernel, heads=heads),
        out_shape=pltpu.HBM((2, rows, q_width + STATS), bf16),
        in_specs=[VMEM] * half,
        out_specs=HBM,
        scratch_shapes=[pltpu.VMEM((rows, q_width + STATS), bf16), pltpu.SemaphoreType.DMA((2,))],
        compiler_params=limit(2),
        cost_estimate=CHEAP,
        name="reduce_other",
    )(*parts[:1], *parts_got)
    crossed = lax.all_to_all(
        theirs_sum, "seq", 0, 0, axis_index_groups=[[i, i + half] for i in range(half)], tiled=True
    )
    migrate(groups[3], theirs_sum)
    new_k, new_v, done = put(groups[2], new_k, new_v)
    width = out_weight.shape[1] // ways
    away, home = [t for t in range(ways) if t & 1], [t for t in range(ways) if not t & 1]
    blocks = lambda n: [pltpu.VMEM((n, q_width, width), bf16), pltpu.SemaphoreType.DMA((n,))]
    sent, attention = pl.pallas_call(
        functools.partial(project_kernel, heads=heads, targets=away),
        out_shape=[pltpu.VMEM((rows, len(away) * width), bf16), pltpu.VMEM((rows, q_width), bf16)],
        in_specs=[SMEM] * 2 + [VMEM] * (half + 2) + [HBM],
        out_specs=[VMEM] * 2,
        scratch_shapes=blocks(len(away)),
        compiler_params=limit(10),
        cost_estimate=CHEAP,
        name="project",
    )(tp1, me1, done, *parts[:1], *parts_got, crossed, out_weight)
    turn = lambda x, t: lax.ppermute(x, "tp", [(i, i ^ t) for i in range(ways)])
    came = turn(sent, 1).astype(f32)
    new_k, new_v, done = put(groups[3], new_k, new_v)
    own = pl.pallas_call(
        functools.partial(finish_kernel, targets=home),
        out_shape=[pltpu.VMEM((rows, width), f32)] * len(home),
        in_specs=[SMEM, VMEM, VMEM, HBM],
        out_specs=[VMEM] * len(home),
        scratch_shapes=blocks(len(home)),
        compiler_params=limit(10),
        cost_estimate=CHEAP,
        name="finish",
    )(tp1, done, attention, out_weight)
    held = {t: x + came[:, n * width : (n + 1) * width] for n, (t, x) in enumerate(zip(home, own))}
    step = 2
    while step < ways:
        leave = [t for t in held if t & step]
        came = turn(jnp.concatenate([held[t].astype(bf16) for t in leave], axis=1), step).astype(f32)
        held = {t ^ step: held[t ^ step] + came[:, n * width : (n + 1) * width] for n, t in enumerate(leave)}
        step *= 2
    attn_out = held[0].astype(bf16)

    span = 32
    new_k, new_v = pl.pallas_call(
        functools.partial(place_kernel, block=block),
        out_shape=shapes,
        in_specs=[SMEM] * 4 + [VMEM] * (1 + half) + [HBM, HBM],
        out_specs=[HBM, HBM],
        input_output_aliases={5 + half: 0, 6 + half: 1},
        scratch_shapes=[
            pltpu.VMEM((2, requests, span, kv_width), bf16),
            pltpu.SemaphoreType.DMA((2, 2, requests)),
        ],
        compiler_params=limit(4),
        cost_estimate=CHEAP,
        name="place",
    )(me1, migrating, lengths, accepted, near, *gots[half:], new_k, new_v)
    return (attn_out, new_k, new_v)


def solution(mesh):
    in_specs = (
        P("seq", "tp"),
        P("seq", "tp"),
        P("seq", "tp"),
        P(None, "seq", "tp"),
        P(None, "seq", "tp"),
        P(),
        P(),
        P(),
        P(),
        P("tp", None),
    )
    out_specs = (P("seq", "tp"), P(None, "seq", "tp"), P(None, "seq", "tp"))
    return jax.shard_map(
        per_device, mesh=mesh, in_specs=in_specs, out_specs=out_specs, check_vma=False
    )
```

time: 279 us -> 87.7 us (0.31); the launches traced: 274 us -> 87.1 us
  Pallas kernels: 207 us -> 28.1 us
  starting transfers between devices: 44.3 us -> 30.2 us
  waiting for transfers between devices: 16.9 us -> 27.2 us
  local copies, waits for them, and re-layouts: 4.62 us -> 0.02 us
    pallas_call x7 -> x9, Pallas kernels: 207 us -> 28.1 us  [the longest x1 7.13 us: per_device(): pl.pallas_call(functools.partial(attend_kernel, half=half, count=count, b...]
    ppermute x12 -> x6, waiting for transfers between devices: 0.77 us -> 16 us  [to_mates(): return [lax.ppermute(parts[e], 'seq', beside[e]) for e in range(1, half)]]
    ppermute x11 -> x6, starting transfers between devices: 22.9 us -> 11.8 us  [the longest x4 10.1 us: migrate(): gots[d] = lax.ppermute(send, 'seq', [(i, i ^ d) for i in range(count)])]
    ppermute x12 -> x6, starting transfers between devices: 17.3 us -> 7.18 us  [to_mates(): return [lax.ppermute(parts[e], 'seq', beside[e]) for e in range(1, half)]]
    ppermute x11 -> x6, waiting for transfers between devices: 12.3 us -> 4.1 us  [the longest x4 3.75 us: migrate(): gots[d] = lax.ppermute(send, 'seq', [(i, i ^ d) for i in range(count)])]
    all_to_all x0 -> x2, waiting for transfers between devices: none -> 7.16 us  [the longest x1 7.16 us: per_device(): lax.all_to_all(theirs_sum, 'seq', 0, 0, axis_index_groups=[[i, i + half]...]
    all_to_all x0 -> x2, starting transfers between devices: none -> 7.13 us  [the longest x1 3.7 us: per_device(): lax.all_to_all(near_send, 'seq', 0, 0, axis_index_groups=sides, tiled=True)]
    unnamed x34 -> x3, local copies, waits for them, and re-layouts: 4.62 us -> 0.01 us
  transfers between devices with their start and end apart: 24 -> 15, of which waited for: 4 -> 7; matrix products, arithmetic and copies ran while one was open for 0% -> 0% of each run, Pallas kernels for 75% -> 32%
where the time goes in v2:
time: 87.7 us; the launch traced here: 87.1 us
  starting transfers between devices  30.2 us (34%)
  Pallas kernels  28.1 us (32%)
  waiting for transfers between devices  27.2 us (31%)
    ppermute x6, waiting for transfers between devices, to_mates(): return [lax.ppermute(parts[e], 'seq', beside[e]) for e in range(1, half)]  16 us
    ppermute x4, starting transfers between devices, migrate(): gots[d] = lax.ppermute(send, 'seq', [(i, i ^ d) for i in range(count)])  10.1 us
    ppermute x6, starting transfers between devices, to_mates(): return [lax.ppermute(parts[e], 'seq', beside[e]) for e in range(1, half)]  7.18 us
    all_to_all x1, waiting for transfers between devices, per_device(): lax.all_to_all(theirs_sum, 'seq', 0, 0, axis_index_groups=[[i, i + half]...  7.16 us
    pallas_call x1, Pallas kernels, per_device(): pl.pallas_call(functools.partial(attend_kernel, half=half, count=count, b...  7.13 us
    pallas_call x1, Pallas kernels, per_device(): pl.pallas_call(functools.partial(side_kernel, which=early, block=block),...  4.5 us
    pallas_call x1, Pallas kernels, per_device(): pl.pallas_call(functools.partial(prep_kernel, block=block), out_shape=[pl...  4.49 us
    ppermute x1, starting transfers between devices, per_device(): q_mirror = lax.ppermute(draft_q, 'seq', across)  4.1 us
  transfers between devices with their start and end apart: 15, of which 7 were waited for; matrix products, arithmetic and copies ran while one was open for 0% of the time, Pallas kernels for 32%

profile of v2, /device:TPU:0, one launch (start us, length us, event | category | flops | bytes accessed | tf_op | source)
XLA Modules:
  0.0 87.1 jit_solution(8085953125532160683)
XLA Ops:
  0.6 4.1 %collective-permute-start = (bf16[32,1024]{1,0:T(8,128)(2,1)}, bf16[32,1024]{1,0:T(8,128)(2,1)S(1)}, u32[]{:S(2)}, u32[]{:S(2)}) collective-permute-start(bf16[32,1024]{1,0:T(8,128)(2,1)} %param.10), channel_id=1, source_target_pairs={{0,16},{4,20},{8,24},{12,28},{16,0},{20,4},{24,8},{28,12},{1,17},{... | collective-permute-start | bytes 196616 | tf_op jit(solution)/shard_map/ppermute | solution.py:373
  4.7 0.0 copy-start
  4.7 4.5 %prep.1 = (bf16[4,528,256]{2,1,0:T(8,128)(2,1)}, bf16[528,256]{1,0:T(8,128)(2,1)S(1)}, bf16[528,256]{1,0:T(8,128)(2,1)}, bf16[528,256]{1,0:T(8,128)(2,1)S(1)}, b...) custom-call(s32[1]{0:T(128)} %bitcast.1.me_ref, s32[4]{0:T(128)} %mig_ref.11, s32[4,64]{1,0:T(4,128)} %parents_ref.1, ...), custom_call_target="tpu_custom_call" | custom-call | flops 1 | bytes 1 | tf_op jit(solution)/shard_map/prep/pallas_call | solution.py:376
  9.2 0.0 copy-done
  9.3 0.0 collective-permute-done
  9.3 2.6 %collective-permute-start.3 = (bf16[64,1024]{1,0:T(8,128)(2,1)S(1)}, bf16[64,1024]{1,0:T(8,128)(2,1)S(1)}, u32[]{:S(2)}, u32[]{:S(2)}) collective-permute-start(bf16[64,1024]{1,0:T(8,128)(2,1)S(1)} %constant_dynamic-update-slice_fusion.rest_0_), channel_id=1, source_target_pairs={{0,12},{4,8},{8,4},{12,0},{16,28},{20,24},{24,20},{28,16},{1,13},{... | collective-permute-start | bytes 393224 | tf_op jit(solution)/shard_map/ppermute | solution.py:371
  11.8 0.4 collective-permute-start.2
  12.3 0.5 collective-permute-start.1
  12.8 3.9 %collective-permute-done.3.rest_3_ = bf16[64,1024]{1,0:T(8,128)(2,1)S(1)} collective-permute-done((bf16[64,1024]{1,0:T(8,128)(2,1)S(1)}, bf16[64,1024]{1,0:T(8,128)(2,1)S(1)}, u32[]{:S(2)}, u32[]{:S(2)}) %collective-permute-start.3) | collective-permute-done | bytes 131104 | tf_op jit(solution)/shard_map/ppermute | solution.py:371
  16.7 1.3 %collective-permute-done.2.rest_2_ = bf16[64,1024]{1,0:T(8,128)(2,1)S(1)} collective-permute-done((bf16[64,1024]{1,0:T(8,128)(2,1)S(1)}, bf16[64,1024]{1,0:T(8,128)(2,1)S(1)}, u32[]{:S(2)}, u32[]{:S(2)}) %collective-permute-start.2) | collective-permute-done | bytes 131104 | tf_op jit(solution)/shard_map/ppermute | solution.py:371
  18.0 0.0 collective-permute-done.1.rest_1_
  18.1 3.7 %all-to-all-start = ((bf16[4,528,256]{2,1,0:T(8,128)(2,1)}), bf16[4,528,256]{2,1,0:T(8,128)(2,1)S(1)}, u32[]{:S(2)}, u32[]{:S(2)}) async-start(bf16[4,528,256]{2,1,0:T(8,128)(2,1)} %get-tuple-element.54), calls=%async_computation | async-start | bytes 2162688 | tf_op jit(solution)/shard_map/all_to_all | solution.py:398
  21.8 1.7 %collective-permute-start.8 = (bf16[528,256]{1,0:T(8,128)(2,1)S(1)}, bf16[528,256]{1,0:T(8,128)(2,1)S(1)}, u32[]{:S(2)}, u32[]{:S(2)}) collective-permute-start(bf16[528,256]{1,0:T(8,128)(2,1)S(1)} %get-tuple-element.51), channel_id=1, source_target_pairs={{0,16},{4,20},{8,24},{12,28},{16,0},{20,4},{24,8},{28,12},{1,17},{... | collective-permute-start | bytes 811016 | tf_op jit(solution)/shard_map/ppermute | solution.py:404
  23.5 7.1 %attend.1 = (bf16[64,1152]{1,0:T(8,128)(2,1)S(1)}, bf16[64,1152]{1,0:T(8,128)(2,1)S(1)}, bf16[64,1152]{1,0:T(8,128)(2,1)S(1)}, bf16[64,1152]{1,0:T(8,128)(2,1)S(1)}) custom-call(s32[1]{0:T(128)} %bitcast.1.me_ref, s32[4]{0:T(128)} %len_ref.3, s32[4]{0:T(128)} %mig_ref.11, bf16[64,1024]{1,0:T(8,128)(2,1)S(1)} %constant_dynamic-update-slice_fusion.rest_0_, ...), custom_call_target="tpu_custom_call" | custom-call | flops 1 | bytes 1 | tf_op jit(solution)/shard_map/attend/pallas_call | solution.py:414
  30.7 2.1 %collective-permute-start.4 = (bf16[64,1152]{1,0:T(8,128)(2,1)S(1)}, bf16[64,1152]{1,0:T(8,128)(2,1)S(1)}, u32[]{:S(2)}, u32[]{:S(2)}) collective-permute-start(bf16[64,1152]{1,0:T(8,128)(2,1)S(1)} %get-tuple-element.45), channel_id=1, source_target_pairs={{0,4},{4,0},{8,12},{12,8},{16,20},{20,16},{24,28},{28,24},{1,5},{5... | collective-permute-start | bytes 442376 | tf_op jit(solution)/shard_map/ppermute | solution.py:371
  32.7 1.5 %collective-permute-start.5 = (bf16[64,1152]{1,0:T(8,128)(2,1)S(1)}, bf16[64,1152]{1,0:T(8,128)(2,1)S(1)}, u32[]{:S(2)}, u32[]{:S(2)}) collective-permute-start(bf16[64,1152]{1,0:T(8,128)(2,1)S(1)} %get-tuple-element.46), channel_id=1, source_target_pairs={{0,8},{4,12},{8,0},{12,4},{16,24},{20,28},{24,16},{28,20},{1,9},{5... | collective-permute-start | bytes 442376 | tf_op jit(solution)/shard_map/ppermute | solution.py:371
  34.2 0.1 collective-permute-start.6
  34.3 2.6 %collective-permute-start.10 = (bf16[528,256]{1,0:T(8,128)(2,1)}, bf16[528,256]{1,0:T(8,128)(2,1)S(1)}, u32[]{:S(2)}, u32[]{:S(2)}) collective-permute-start(bf16[528,256]{1,0:T(8,128)(2,1)} %get-tuple-element.56), channel_id=1, source_target_pairs={{0,20},{4,16},{8,28},{12,24},{16,4},{20,0},{24,12},{28,8},{1,21},{... | collective-permute-start | bytes 811016 | tf_op jit(solution)/shard_map/ppermute | solution.py:404
  36.9 3.7 %collective-permute-done.8.rest_0_ = bf16[528,256]{1,0:T(8,128)(2,1)S(1)} collective-permute-done((bf16[528,256]{1,0:T(8,128)(2,1)S(1)}, bf16[528,256]{1,0:T(8,128)(2,1)S(1)}, u32[]{:S(2)}, u32[]{:S(2)}) %collective-permute-start.8) | collective-permute-done | bytes 270368 | tf_op jit(solution)/shard_map/ppermute | solution.py:404
  40.6 3.2 %collective-permute-start.9 = (bf16[528,256]{1,0:T(8,128)(2,1)S(1)}, bf16[528,256]{1,0:T(8,128)(2,1)S(1)}, u32[]{:S(2)}, u32[]{:S(2)}) collective-permute-start(bf16[528,256]{1,0:T(8,128)(2,1)S(1)} %get-tuple-element.52), channel_id=1, source_target_pairs={{0,24},{4,28},{8,16},{12,20},{16,8},{20,12},{24,0},{28,4},{1,25},{... | collective-permute-start | bytes 811016 | tf_op jit(solution)/shard_map/ppermute | solution.py:404
  43.8 0.0 collective-permute-done.4.refs_1_
  43.8 7.2 %collective-permute-done.5.refs_2_ = bf16[64,1152]{1,0:T(8,128)(2,1)S(1)} collective-permute-done((bf16[64,1152]{1,0:T(8,128)(2,1)S(1)}, bf16[64,1152]{1,0:T(8,128)(2,1)S(1)}, u32[]{:S(2)}, u32[]{:S(2)}) %collective-permute-start.5) | collective-permute-done | bytes 147488 | tf_op jit(solution)/shard_map/ppermute | solution.py:371
  51.0 3.5 %collective-permute-done.6.refs_3_ = bf16[64,1152]{1,0:T(8,128)(2,1)S(1)} collective-permute-done((bf16[64,1152]{1,0:T(8,128)(2,1)S(1)}, bf16[64,1152]{1,0:T(8,128)(2,1)S(1)}, u32[]{:S(2)}, u32[]{:S(2)}) %collective-permute-start.6) | collective-permute-done | bytes 147488 | tf_op jit(solution)/shard_map/ppermute | solution.py:371
  54.5 1.1 %reduce_other.1 = bf16[2,32,1152]{2,1,0:T(8,128)(2,1)} custom-call(bf16[64,1152]{1,0:T(8,128)(2,1)S(1)} %get-tuple-element.44.refs_0_.after_ref, bf16[64,1152]{1,0:T(8,128)(2,1)S(1)} %collective-permute-done.4.refs_1_, bf16[64,1152]{1,0:T(8,128)(2,1)S(1)} %collective-permute-done.5.refs_2_, bf16[64,1152]{1,0:T(8,128)(2,1)S(1)} %collective-permute-done.6.refs_3_), custom_call_target="tpu_custom_call" | custom-call | flops 1 | bytes 1 | tf_op jit(solution)/shard_map/reduce_other/pallas_call | solution.py:464
  55.6 0.0 all-to-all-done.near_ref
  55.6 3.4 %all-to-all-start.1 = ((bf16[2,32,1152]{2,1,0:T(8,128)(2,1)}), bf16[2,32,1152]{2,1,0:T(8,128)(2,1)S(1)}, u32[]{:S(2)}, u32[]{:S(2)}) async-start(bf16[2,32,1152]{2,1,0:T(8,128)(2,1)} %reduce_other.1), calls=%async_computation.1 | async-start | bytes 294912 | tf_op jit(solution)/shard_map/all_to_all | solution.py:474
  59.1 2.7 %collective-permute-start.7 = (bf16[528,256]{1,0:T(8,128)(2,1)S(1)}, bf16[528,256]{1,0:T(8,128)(2,1)S(1)}, u32[]{:S(2)}, u32[]{:S(2)}) collective-permute-start(bf16[528,256]{1,0:T(8,128)(2,1)S(1)} %get-tuple-element.48), channel_id=1, source_target_pairs={{0,28},{4,24},{8,20},{12,16},{16,12},{20,8},{24,4},{28,0},{1,29},{... | collective-permute-start | bytes 811016 | tf_op jit(solution)/shard_map/ppermute | solution.py:404
  61.7 0.0 collective-permute-done.10.rest_1_
  61.7 4.5 %side.1 = (bf16[4,1024,256]{2,1,0:T(8,128)(2,1)}, bf16[4,1024,256]{2,1,0:T(8,128)(2,1)}, f32[8,128]{1,0:T(8,128)}) custom-call(s32[1]{0:T(128)} %bitcast.1.me_ref, s32[4]{0:T(128)} %mig_ref.11, bf16[4,1024,256]{2,1,0:T(8,128)(2,1)} %ck_ref.3, bf16[4,1024,256]{2,1,0:T(8,128)(2,1)} %cv_ref.3, bf16[64,1152]{1,0:T(8,128)(2,1)S(1)} %get-tuple-element.44.refs_0_.after_ref, ...), custom_call_target="tpu_custom_call" | custom-call | flops 1 | bytes 1 | tf_op jit(solution)/shard_map/side/pallas_call | solution.py:449
  66.2 0.0 collective-permute-done.9.rest_0_.rest_2_
  66.2 1.4 %put.2 = (bf16[4,1024,256]{2,1,0:T(8,128)(2,1)}, bf16[4,1024,256]{2,1,0:T(8,128)(2,1)}, f32[8,128]{1,0:T(8,128)S(1)}) custom-call(s32[1]{0:T(128)} %bitcast.1.me_ref, s32[4]{0:T(128)} %mig_ref.11, bf16[528,256]{1,0:T(8,128)(2,1)S(1)} %collective-permute-done.9.rest_0_.rest_2_, ...), custom_call_target="tpu_custom_call", output_to_operand_aliasing={{0}: (3, {}), {1}: (4, {})} | custom-call | flops 1 | bytes 1 | tf_op jit(solution)/shard_map/put/pallas_call | solution.py:435
  67.7 7.2 %all-to-all-done.1.refs_4_ = bf16[2,32,1152]{2,1,0:T(8,128)(2,1)S(1)} async-done(((bf16[2,32,1152]{2,1,0:T(8,128)(2,1)}), bf16[2,32,1152]{2,1,0:T(8,128)(2,1)S(1)}, u32[]{:S(2)}, u32[]{:S(2)}) %all-to-all-start.1) | async-done | bytes 147488 | tf_op jit(solution)/shard_map/all_to_all | solution.py:474
  74.8 2.7 %project.1 = (bf16[32,2048]{1,0:T(8,128)(2,1)S(1)}, bf16[32,1024]{1,0:T(8,128)(2,1)S(1)}) custom-call(s32[1]{0:T(128)} %bitcast.tp_ref, s32[1]{0:T(128)} %bitcast.1.me_ref, f32[8,128]{1,0:T(8,128)S(1)} %get-tuple-element.62.done_ref, bf16[64,1152]{1,0:T(8,128)(2,1)S(1)} %get-tuple-element.44.refs_0_.after_ref, ...), custom_call_target="tpu_custom_call" | custom-call | flops 1 | bytes 1 | tf_op jit(solution)/shard_map/project/pallas_call | solution.py:482
  77.6 0.1 collective-permute-start.11
  77.6 0.0 collective-permute-done.7.rest_0_.rest_3_
  77.7 1.4 %put.3 = (bf16[4,1024,256]{2,1,0:T(8,128)(2,1)}, bf16[4,1024,256]{2,1,0:T(8,128)(2,1)}, f32[8,128]{1,0:T(8,128)S(1)}) custom-call(s32[1]{0:T(128)} %bitcast.1.me_ref, s32[4]{0:T(128)} %mig_ref.11, bf16[528,256]{1,0:T(8,128)(2,1)S(1)} %collective-permute-done.7.rest_0_.rest_3_, ...), custom_call_target="tpu_custom_call", output_to_operand_aliasing={{0}: (3, {}), {1}: (4, {})} | custom-call | flops 1 | bytes 1 | tf_op jit(solution)/shard_map/put/pallas_call | solution.py:435
  79.1 2.7 %finish.1 = (f32[32,1024]{1,0:T(8,128)S(1)}, f32[32,1024]{1,0:T(8,128)S(1)}) custom-call(s32[1]{0:T(128)} %bitcast.tp_ref, f32[8,128]{1,0:T(8,128)S(1)} %get-tuple-element.61.done_ref, bf16[32,1024]{1,0:T(8,128)(2,1)S(1)} %get-tuple-element.63.a_ref, bf16[1024,4096]{1,0:T(8,128)(2,1)} %w_ref.1), custom_call_target="tpu_custom_call" | custom-call | flops 1 | bytes 1 | tf_op jit(solution)/shard_map/finish/pallas_call | solution.py:495
  81.8 0.0 collective-permute-done.11
  81.9 1.6 %collective-permute-start.12 = (bf16[32,1024]{1,0:T(8,128)(2,1)S(1)}, bf16[32,1024]{1,0:T(8,128)(2,1)S(1)}, u32[]{:S(2)}, u32[]{:S(2)}) collective-permute-start(bf16[32,1024]{1,0:T(8,128)(2,1)S(1)} %fusion), channel_id=1, source_target_pairs={{0,2},{1,3},{2,0},{3,1},{4,6},{5,7},{6,4},{7,5},{8,10},{9,11},{10,... | collective-permute-start | bytes 196616 | tf_op jit(solution)/shard_map/ppermute | solution.py:492
  83.4 2.6 %place.1 = (bf16[4,1024,256]{2,1,0:T(8,128)(2,1)}, bf16[4,1024,256]{2,1,0:T(8,128)(2,1)}) custom-call(s32[1]{0:T(128)} %bitcast.1.me_ref, s32[4]{0:T(128)} %mig_ref.11, s32[4]{0:T(128)} %len_ref.3, s32[4,8]{1,0:T(4,128)} %accepted_ref.3, bf16[4,528,256]{2,1,0:T(8,128)(2,1)S(1)} %all-to-all-done.near_ref, ...), custom_call_target="tpu_custom_call", output_to_operand_aliasing={{0}: (9, {}), {1}: (10, {})} | custom-call | flops 1 | bytes 1 | tf_op jit(solution)/shard_map/place/pallas_call | solution.py:515
  86.1 0.4 collective-permute-done.12
  86.4 0.7 fusion.2
  (4 shorter events, 0.1 us)
Async XLA Ops:
  0.6 8.6 %collective-permute-start = (bf16[32,1024]{1,0:T(8,128)(2,1)}, bf16[32,1024]{1,0:T(8,128)(2,1)S(1)}, u32[]{:S(2)}, u32[]{:S(2)}) collective-permute-start(bf16[32,1024]{1,0:T(8,128)(2,1)} %param.10), channel_id=1, source_target_pairs={{0,16},{4,20},{8,24},{12,28},{16,0},{20,4},{24,8},{28,12},{1,17},{... | collective-permute-start | bytes 196616 | tf_op jit(solution)/shard_map/ppermute | solution.py:373
  4.7 4.5 %copy-start = (bf16[32,1024]{1,0:T(8,128)(2,1)S(1)}, bf16[32,1024]{1,0:T(8,128)(2,1)}, u32[]{:S(2)}) copy-start(bf16[32,1024]{1,0:T(8,128)(2,1)} %param.10) | copy-start | bytes 196612
  9.3 7.4 %collective-permute-start.3 = (bf16[64,1024]{1,0:T(8,128)(2,1)S(1)}, bf16[64,1024]{1,0:T(8,128)(2,1)S(1)}, u32[]{:S(2)}, u32[]{:S(2)}) collective-permute-start(bf16[64,1024]{1,0:T(8,128)(2,1)S(1)} %constant_dynamic-update-slice_fusion.rest_0_), channel_id=1, source_target_pairs={{0,12},{4,8},{8,4},{12,0},{16,28},{20,24},{24,20},{28,16},{1,13},{... | collective-permute-start | bytes 393224 | tf_op jit(solution)/shard_map/ppermute | solution.py:371
  11.8 6.2 %collective-permute-start.2 = (bf16[64,1024]{1,0:T(8,128)(2,1)S(1)}, bf16[64,1024]{1,0:T(8,128)(2,1)S(1)}, u32[]{:S(2)}, u32[]{:S(2)}) collective-permute-start(bf16[64,1024]{1,0:T(8,128)(2,1)S(1)} %constant_dynamic-update-slice_fusion.rest_0_), channel_id=1, source_target_pairs={{0,8},{4,12},{8,0},{12,4},{16,24},{20,28},{24,16},{28,20},{1,9},{5... | collective-permute-start | bytes 393224 | tf_op jit(solution)/shard_map/ppermute | solution.py:371
  12.3 5.8 %collective-permute-start.1 = (bf16[64,1024]{1,0:T(8,128)(2,1)S(1)}, bf16[64,1024]{1,0:T(8,128)(2,1)S(1)}, u32[]{:S(2)}, u32[]{:S(2)}) collective-permute-start(bf16[64,1024]{1,0:T(8,128)(2,1)S(1)} %constant_dynamic-update-slice_fusion.rest_0_), channel_id=1, source_target_pairs={{0,4},{4,0},{8,12},{12,8},{16,20},{20,16},{24,28},{28,24},{1,5},{5... | collective-permute-start | bytes 393224 | tf_op jit(solution)/shard_map/ppermute | solution.py:371
  18.1 37.5 %all-to-all-start = ((bf16[4,528,256]{2,1,0:T(8,128)(2,1)}), bf16[4,528,256]{2,1,0:T(8,128)(2,1)S(1)}, u32[]{:S(2)}, u32[]{:S(2)}) async-start(bf16[4,528,256]{2,1,0:T(8,128)(2,1)} %get-tuple-element.54), calls=%async_computation | async-start | bytes 2162688 | tf_op jit(solution)/shard_map/all_to_all | solution.py:398
  21.8 18.8 %collective-permute-start.8 = (bf16[528,256]{1,0:T(8,128)(2,1)S(1)}, bf16[528,256]{1,0:T(8,128)(2,1)S(1)}, u32[]{:S(2)}, u32[]{:S(2)}) collective-permute-start(bf16[528,256]{1,0:T(8,128)(2,1)S(1)} %get-tuple-element.51), channel_id=1, source_target_pairs={{0,16},{4,20},{8,24},{12,28},{16,0},{20,4},{24,8},{28,12},{1,17},{... | collective-permute-start | bytes 811016 | tf_op jit(solution)/shard_map/ppermute | solution.py:404
  30.7 13.1 %collective-permute-start.4 = (bf16[64,1152]{1,0:T(8,128)(2,1)S(1)}, bf16[64,1152]{1,0:T(8,128)(2,1)S(1)}, u32[]{:S(2)}, u32[]{:S(2)}) collective-permute-start(bf16[64,1152]{1,0:T(8,128)(2,1)S(1)} %get-tuple-element.45), channel_id=1, source_target_pairs={{0,4},{4,0},{8,12},{12,8},{16,20},{20,16},{24,28},{28,24},{1,5},{5... | collective-permute-start | bytes 442376 | tf_op jit(solution)/shard_map/ppermute | solution.py:371
  32.7 18.3 %collective-permute-start.5 = (bf16[64,1152]{1,0:T(8,128)(2,1)S(1)}, bf16[64,1152]{1,0:T(8,128)(2,1)S(1)}, u32[]{:S(2)}, u32[]{:S(2)}) collective-permute-start(bf16[64,1152]{1,0:T(8,128)(2,1)S(1)} %get-tuple-element.46), channel_id=1, source_target_pairs={{0,8},{4,12},{8,0},{12,4},{16,24},{20,28},{24,16},{28,20},{1,9},{5... | collective-permute-start | bytes 442376 | tf_op jit(solution)/shard_map/ppermute | solution.py:371
  34.2 20.3 %collective-permute-start.6 = (bf16[64,1152]{1,0:T(8,128)(2,1)S(1)}, bf16[64,1152]{1,0:T(8,128)(2,1)S(1)}, u32[]{:S(2)}, u32[]{:S(2)}) collective-permute-start(bf16[64,1152]{1,0:T(8,128)(2,1)S(1)} %get-tuple-element.47), channel_id=1, source_target_pairs={{0,12},{4,8},{8,4},{12,0},{16,28},{20,24},{24,20},{28,16},{1,13},{... | collective-permute-start | bytes 442376 | tf_op jit(solution)/shard_map/ppermute | solution.py:371
  34.3 27.4 %collective-permute-start.10 = (bf16[528,256]{1,0:T(8,128)(2,1)}, bf16[528,256]{1,0:T(8,128)(2,1)S(1)}, u32[]{:S(2)}, u32[]{:S(2)}) collective-permute-start(bf16[528,256]{1,0:T(8,128)(2,1)} %get-tuple-element.56), channel_id=1, source_target_pairs={{0,20},{4,16},{8,28},{12,24},{16,4},{20,0},{24,12},{28,8},{1,21},{... | collective-permute-start | bytes 811016 | tf_op jit(solution)/shard_map/ppermute | solution.py:404
  40.6 25.6 %collective-permute-start.9 = (bf16[528,256]{1,0:T(8,128)(2,1)S(1)}, bf16[528,256]{1,0:T(8,128)(2,1)S(1)}, u32[]{:S(2)}, u32[]{:S(2)}) collective-permute-start(bf16[528,256]{1,0:T(8,128)(2,1)S(1)} %get-tuple-element.52), channel_id=1, source_target_pairs={{0,24},{4,28},{8,16},{12,20},{16,8},{20,12},{24,0},{28,4},{1,25},{... | collective-permute-start | bytes 811016 | tf_op jit(solution)/shard_map/ppermute | solution.py:404
  55.6 19.2 %all-to-all-start.1 = ((bf16[2,32,1152]{2,1,0:T(8,128)(2,1)}), bf16[2,32,1152]{2,1,0:T(8,128)(2,1)S(1)}, u32[]{:S(2)}, u32[]{:S(2)}) async-start(bf16[2,32,1152]{2,1,0:T(8,128)(2,1)} %reduce_other.1), calls=%async_computation.1 | async-start | bytes 294912 | tf_op jit(solution)/shard_map/all_to_all | solution.py:474
  59.1 18.6 %collective-permute-start.7 = (bf16[528,256]{1,0:T(8,128)(2,1)S(1)}, bf16[528,256]{1,0:T(8,128)(2,1)S(1)}, u32[]{:S(2)}, u32[]{:S(2)}) collective-permute-start(bf16[528,256]{1,0:T(8,128)(2,1)S(1)} %get-tuple-element.48), channel_id=1, source_target_pairs={{0,28},{4,24},{8,20},{12,16},{16,12},{20,8},{24,4},{28,0},{1,29},{... | collective-permute-start | bytes 811016 | tf_op jit(solution)/shard_map/ppermute | solution.py:404
  77.6 4.2 %collective-permute-start.11 = (bf16[32,2048]{1,0:T(8,128)(2,1)S(1)}, bf16[32,2048]{1,0:T(8,128)(2,1)S(1)}, u32[]{:S(2)}, u32[]{:S(2)}) collective-permute-start(bf16[32,2048]{1,0:T(8,128)(2,1)S(1)} %get-tuple-element.65), channel_id=1, source_target_pairs={{0,1},{1,0},{2,3},{3,2},{4,5},{5,4},{6,7},{7,6},{8,9},{9,8},{10,11... | collective-permute-start | bytes 393224 | tf_op jit(solution)/shard_map/ppermute | solution.py:492
  81.9 4.5 %collective-permute-start.12 = (bf16[32,1024]{1,0:T(8,128)(2,1)S(1)}, bf16[32,1024]{1,0:T(8,128)(2,1)S(1)}, u32[]{:S(2)}, u32[]{:S(2)}) collective-permute-start(bf16[32,1024]{1,0:T(8,128)(2,1)S(1)} %fusion), channel_id=1, source_target_pairs={{0,2},{1,3},{2,0},{3,1},{4,6},{5,7},{6,4},{7,5},{8,10},{9,11},{10,... | collective-permute-start | bytes 196616 | tf_op jit(solution)/shard_map/ppermute | solution.py:492

commit v3 on v2

v3 whole, which is shorter than its diff:
```python
import functools
import math

import jax
import jax.numpy as jnp
from jax import lax
from jax.experimental import pallas as pl
from jax.experimental.pallas import tpu as pltpu
from jax.sharding import PartitionSpec as P

HD = 128
NEG = -1e30
FLOOR = -1e20
STATS = 128
bf16 = jnp.bfloat16
f32 = jnp.float32
i32 = jnp.int32


def nt(a, b):
    return lax.dot_general(a, b, (((1,), (1,)), ((), ())), preferred_element_type=f32)


def tn(a, b):
    return lax.dot_general(a, b, (((0,), (0,)), ((), ())), preferred_element_type=f32)


def split3(x):
    hi = x.astype(bf16).astype(f32)
    rest = x - hi
    mid = rest.astype(bf16).astype(f32)
    return hi, mid, rest - mid


def migrating_pair(mig_ref, requests, flag=1):
    first = i32(0)
    last = i32(0)
    for r in reversed(range(requests)):
        first = jnp.where(mig_ref[r] == flag, r, first)
    for r in range(requests):
        last = jnp.where(mig_ref[r] == flag, r, last)
    return first, last


def block_copies(me, pair, caches, targets, slots, block, sems, back=False):
    copies = []
    for target, slot in zip(targets, slots):
        at = pl.ds(pl.multiple_of(target * block, block), block)
        for c, cache in enumerate(caches):
            for m in range(2):
                ends = cache.at[pair[m], at], slot.at[pl.ds((2 * c + m) * block, block)]
                copies.append(pltpu.make_async_copy(*(ends[::-1] if back else ends), sems.at[len(copies)]))
    return copies


def deltas(me, kind, k, quarter):
    z = me // quarter
    inner = (z == 1) | (z == 2)
    pick = jnp.where if not isinstance(me, int) else lambda c, a, b: a if c else b
    near, far = quarter + k, 2 * quarter + k
    if kind == "inner":
        return pick(inner, far, near), pick(inner, near, far)
    if kind == "outer":
        return pick(inner, near, far), pick(inner, far, near)
    both = k if kind == "same" else 3 * quarter + k
    return both, both


def prep_kernel(me_ref, mig_ref, parents_ref, accepted_ref, dk_ref, dv_ref, ck_ref, cv_ref, *rest, ops, block, quarter):
    *outs, bias_ref, acc_ref, sems = rest
    requests, drafts = parents_ref.shape
    rows = dk_ref.shape[0]
    accept = accepted_ref.shape[1]
    me = me_ref[0]
    pair = migrating_pair(mig_ref, requests)
    goals = [me ^ deltas(me, kind, k, quarter)[0] for kind, k in ops]
    copies = block_copies(me, pair, (ck_ref, cv_ref), goals, outs, block, sems)
    for copy in copies:
        copy.start()
    request = (me * rows) // drafts
    offset = me * rows - request * drafts
    mine = lax.broadcasted_iota(i32, (requests, drafts), 0) == request
    parent = jnp.sum(jnp.where(mine, parents_ref[...], 0), axis=0, keepdims=True)
    down = lax.broadcasted_iota(i32, (drafts, drafts), 0)
    along = lax.broadcasted_iota(i32, (drafts, drafts), 1)
    reach = jnp.where((down == along) | (parent == down), 1.0, 0.0).astype(bf16)
    for _ in range(max(1, (drafts - 1).bit_length())):
        both = jnp.dot(reach, reach, preferred_element_type=f32)
        reach = jnp.where(both > 0.5, 1.0, 0.0).astype(bf16)
    pick = jnp.where(
        lax.broadcasted_iota(i32, (drafts, rows), 0) == lax.broadcasted_iota(i32, (drafts, rows), 1) + offset, 1.0, 0.0
    ).astype(bf16)
    bias_ref[...] = jnp.where(tn(reach, pick) > 0.5, 0.0, NEG)
    mine = lax.broadcasted_iota(i32, (requests, accept), 0) == request
    node = jnp.sum(jnp.where(mine, accepted_ref[...], 0), axis=0, keepdims=True)
    pick = jnp.where(lax.broadcasted_iota(i32, (rows, accept), 0) + offset == node, 1.0, 0.0).astype(bf16)
    chosen = jnp.concatenate([tn(pick, dk_ref[...]), tn(pick, dv_ref[...])], axis=0).astype(bf16)
    acc_ref[...] = chosen
    for out in outs:
        out[4 * block :] = chosen
    for copy in copies:
        copy.wait()


def attend_kernel(me_ref, len_ref, mig_ref, *rest, half, count, block, group, steps):
    q_refs = rest[:half]
    ck_ref, cv_ref, dk_ref, dv_ref, bias_ref = rest[half : half + 5]
    outs = rest[-half - 5 : -5]
    k_ref, v_ref, q_all, part, sems = rest[-5:]
    me = me_ref[0]
    spot = lax.rem(me, half)
    side = me // half
    rows, q_width = q_all.shape[2:]
    cache_dev = k_ref.shape[1]
    kv_local = k_ref.shape[2] // HD
    per_request = half // steps
    drafts = per_request * rows
    heads = kv_local * group
    requests = [side * steps + r for r in range(steps)] + [(1 - side) * steps + r for r in range(steps)]
    loads = []
    for i, request in enumerate(requests):
        for c, (cache, here) in enumerate(((ck_ref, k_ref), (cv_ref, v_ref))):
            loads.append(pltpu.make_async_copy(cache.at[request], here.at[i], sems.at[i, c]))
            loads[-1].start()
    for e in range(half):
        both = q_refs[e][...].astype(q_all.dtype)
        for k in range(2):
            q_all[k, spot ^ e] = both[k * rows : (k + 1) * rows]
    row = lax.broadcasted_iota(i32, (1, cache_dev), 1)
    shift = block.bit_length() - 1
    moved = row + (row >> shift) * ((count - 1) * block) + me * block
    scale = math.log2(math.e) / math.sqrt(HD)
    lane = lax.broadcasted_iota(i32, (drafts, STATS), 1)
    for i, request in enumerate(requests):
        drafted = i < steps
        k, step = divmod(i, steps)
        position = jnp.where(mig_ref[request] == 1, moved, row + me * cache_dev)
        dead = jnp.where(position < len_ref[request], 0.0, NEG)
        rows_q = q_all[k, step * per_request : (step + 1) * per_request].reshape(drafts, q_width)
        loads[2 * i].wait()
        loads[2 * i + 1].wait()
        stats = jnp.zeros((drafts, STATS), f32)
        for g in range(kv_local):
            at_g = slice(g * HD, (g + 1) * HD)
            q = jnp.concatenate(
                [rows_q[:, (g * group + j) * HD : (g * group + j + 1) * HD] for j in range(group)], axis=0
            ).astype(bf16)
            s = nt(q, k_ref[i, :, at_g]) * scale + dead
            top = jnp.max(s, axis=1, keepdims=True)
            if drafted:
                own = jnp.where(request == (me * rows) // drafts, bias_ref[...], NEG)
                sd = nt(q, dk_ref[:, at_g]) * scale + jnp.concatenate([own] * group, axis=0)
                top = jnp.maximum(top, jnp.max(sd, axis=1, keepdims=True))
            top = jnp.maximum(top, FLOOR)
            w = jnp.exp2(s - top)
            total = jnp.sum(w, axis=1, keepdims=True)
            o = jnp.dot(w.astype(bf16), v_ref[i, :, at_g], preferred_element_type=f32)
            if drafted:
                wd = jnp.exp2(sd - top)
                total = total + jnp.sum(wd, axis=1, keepdims=True)
                o = o + jnp.dot(wd.astype(bf16), dv_ref[:, at_g], preferred_element_type=f32)
            for j in range(group):
                h = g * group + j
                at = slice(j * drafts, (j + 1) * drafts)
                values = split3(top[at]) + split3(total[at])[:2]
                for n, value in enumerate(values):
                    stats = jnp.where(lane == n * heads + h, value, stats)
                for p in range(per_request):
                    part[k, step * per_request + p, :, h * HD : (h + 1) * HD] = o[
                        j * drafts + p * rows : j * drafts + (p + 1) * rows
                    ].astype(part.dtype)
        for p in range(per_request):
            part[k, step * per_request + p, :, q_width:] = stats[p * rows : (p + 1) * rows].astype(part.dtype)
    for e in range(half):
        outs[e][...] = jnp.concatenate([part[k, spot ^ e] for k in range(2)], axis=0).astype(bf16)


def view(ref, k, rows):
    def get(at):
        if rows % 16 == 0 or ref.shape[0] == rows:
            return ref[k * rows : (k + 1) * rows, at].astype(f32)
        return ref[:, at].astype(f32)[k * rows : (k + 1) * rows]

    return get


def merge(parts, heads):
    width = heads * HD
    stats = [get(slice(width, width + STATS)) for get in parts]
    tops = [s[:, :heads] + s[:, heads : 2 * heads] + s[:, 2 * heads : 3 * heads] for s in stats]
    totals = [s[:, 3 * heads : 4 * heads] + s[:, 4 * heads : 5 * heads] for s in stats]
    top = functools.reduce(jnp.maximum, tops)
    factors = [jnp.exp2(t - top) for t in tops]
    total = sum(f * t for f, t in zip(factors, totals))
    sums = []
    for h in range(heads):
        sums.append(sum(f[:, h : h + 1] * get(slice(h * HD, (h + 1) * HD)) for f, get in zip(factors, parts)))
    return top, total, sums


def reduce_kernel(*refs, heads):
    *parts, out = refs
    rows = out.shape[0]
    top, total, sums = merge([view(r, 1, rows) for r in parts], heads)
    lane = lax.broadcasted_iota(i32, (rows, STATS), 1)
    stats = jnp.zeros((rows, STATS), f32)
    values = split3(top) + split3(total)[:2]
    for k, value in enumerate(values):
        for h in range(heads):
            stats = jnp.where(lane == k * heads + h, value[:, h : h + 1], stats)
    for h in range(heads):
        out[:, h * HD : (h + 1) * HD] = sums[h].astype(bf16)
    out[:, heads * HD :] = stats.astype(bf16)


def project_kernel(tp_ref, done_ref, *refs, heads, ways):
    parts, w_ref, outs = refs[: -ways - 3], refs[-ways - 3], refs[-ways - 2 : -3]
    own_ref, here_ref, sems = refs[-3:]
    rows, width = own_ref.shape
    loads = []
    for d in range(ways):
        at = pl.ds(pl.multiple_of((tp_ref[0] ^ ((d + 1) % ways)) * width, width), width)
        loads.append(pltpu.make_async_copy(w_ref.at[:, at], here_ref.at[d], sems.at[d]))
        loads[-1].start()
    top, total, sums = merge([view(r, 0, rows) for r in parts], heads)
    attention = jnp.concatenate(
        [(sums[h] / total[:, h : h + 1]).astype(bf16) for h in range(heads)], axis=1
    )
    for d in range(ways):
        loads[d].wait()
        block = jnp.dot(attention, here_ref[d], preferred_element_type=f32)
        if d < ways - 1:
            outs[d][...] = block.astype(bf16)
        else:
            own_ref[...] = block


def final_kernel(done_ref, own_ref, *rest):
    out_ref = rest[-1]
    total = own_ref[...]
    for ref in rest[:-1]:
        total = total + ref[...].astype(f32)
    out_ref[...] = total.astype(bf16)


def put_kernel(me_ref, mig_ref, after_ref, *rest, ops, block, quarter, first, fill):
    gots = rest[: len(ops)]
    rest = rest[len(ops) :]
    if fill:
        ck_ref, cv_ref = rest[:2]
        rest = rest[2:]
    if not first:
        rest = rest[2:]
    nk_ref, nv_ref, done_ref, sems, *rest = rest
    me = me_ref[0]
    pair = migrating_pair(mig_ref, mig_ref.shape[0])
    news = (nk_ref, nv_ref)
    sources = [me ^ deltas(me, kind, k, quarter)[1] for kind, k in ops]
    copies = block_copies(me, pair, news, sources, gots, block, sems, back=True)
    for copy in copies:
        copy.start()
    done_ref[...] = jnp.zeros_like(done_ref)
    if fill:
        hold_ref, own_ref, hold_sems, own_sems = rest
        stay = migrating_pair(mig_ref, mig_ref.shape[0], 0)
        at = pl.ds(pl.multiple_of(me * block, block), block)
        loads, stores = [], []
        for c, (cache, new) in enumerate(zip((ck_ref, cv_ref), news)):
            for m in range(2):
                for here, held, there, sem in (
                    (cache.at[stay[m]], hold_ref.at[c, m], new.at[stay[m]], hold_sems),
                    (cache.at[pair[m], at], own_ref.at[c, m], new.at[pair[m], at], own_sems),
                ):
                    loads.append(pltpu.make_async_copy(here, held, sem.at[0, c, m]))
                    stores.append(pltpu.make_async_copy(held, there, sem.at[1, c, m]))
                    loads[-1].start()
        for load, store in zip(loads, stores):
            load.wait()
            store.start()
        copies = copies + stores
    for copy in copies:
        copy.wait()


def place_kernel(me_ref, mig_ref, len_ref, accepted_ref, acc_ref, *rest, ops, last, quarter, block):
    *gots, fk_ref, fv_ref, nk_ref, nv_ref, done_ref, wins_ref, sems, win_sem = rest
    requests, accept = accepted_ref.shape
    count = 4 * quarter
    cache_dev = nk_ref.shape[1]
    me = me_ref[0]
    pair = migrating_pair(mig_ref, requests)
    sources = [me ^ deltas(me, kind, k, quarter)[1] for kind, k in ops]
    done_ref[...] = jnp.zeros_like(done_ref)
    ends = [(source, got) for op, source, got in zip(ops, sources, gots) if op in last]
    copies = block_copies(me, pair, (nk_ref, nv_ref), *zip(*ends), block, sems, back=True)
    for copy in copies:
        copy.start()
    for copy in copies:
        copy.wait()
    span = wins_ref.shape[2]
    first = [len_ref[r] - me * cache_dev for r in range(requests)]
    low = [pl.multiple_of(jnp.clip((x >> 4) << 4, 0, cache_dev - span), 16) for x in first]
    loads, stores = [], []
    for c, new in enumerate((nk_ref, nv_ref)):
        for r in range(requests):
            a, b = new.at[r, pl.ds(low[r], span)], wins_ref.at[c, r]
            loads.append(pltpu.make_async_copy(a, b, win_sem.at[0, c, r]))
            stores.append(pltpu.make_async_copy(b, a, win_sem.at[1, c, r]))
    for copy in loads:
        copy.start()
    per_request = count // requests
    for copy in loads:
        copy.wait()
    for r in range(requests):
        held = jnp.where(me // per_request == r, acc_ref[...].astype(f32), 0.0)
        for owner, got in zip(sources, gots):
            held = held + jnp.where(owner // per_request == r, got[4 * block :].astype(f32), 0.0)
        row = lax.broadcasted_iota(i32, (span, 1), 0) + low[r]
        for c in range(2):
            window = wins_ref[c, r].astype(f32)
            for i in range(accept):
                hit = (row == first[r] + i) & (accepted_ref[r, i] >= 0)
                window = jnp.where(hit, held[c * accept + i : c * accept + i + 1], window)
            wins_ref[c, r] = window.astype(bf16)
    for copy in stores:
        copy.start()
    for copy in stores:
        copy.wait()


ANY = pl.BlockSpec(memory_space=pl.ANY)
SMEM = pl.BlockSpec(memory_space=pltpu.SMEM)
VMEM = pl.BlockSpec(memory_space=pltpu.VMEM)
HBM = pl.BlockSpec(memory_space=pltpu.HBM)

CHEAP = pl.CostEstimate(flops=1, transcendentals=0, bytes_accessed=1)


def limit(mib):
    return pltpu.CompilerParams(vmem_limit_bytes=mib << 20)


def per_device(
    draft_q, draft_k, draft_v, cache_k, cache_v, lengths, migrating, parents, accepted, out_weight
):
    count = lax.axis_size("seq")
    ways = lax.axis_size("tp")
    half = count // 2
    me = lax.axis_index("seq").astype(i32)
    tp = lax.axis_index("tp").astype(i32)
    rows, q_width = draft_q.shape
    requests, drafts = parents.shape
    accept = accepted.shape[1]
    cache_dev, kv_width = cache_k.shape[1:]
    group = q_width // kv_width
    heads = q_width // HD
    block = cache_dev // count
    draft_k, draft_v, cache_k, cache_v, lengths, migrating, parents, accepted, out_weight = [
        pltpu.with_memory_space_constraint(x, pltpu.HBM)
        for x in (draft_k, draft_v, cache_k, cache_v, lengths, migrating, parents, accepted, out_weight)
    ]
    me1 = me.reshape(1)
    tp1 = tp.reshape(1)
    across = [(i, (i + half) % count) for i in range(count)]
    beside = [[(i, i ^ e) for i in range(count)] for e in range(half)]

    def to_mates(parts):
        got = {e: lax.ppermute(parts[e], "seq", beside[e]) for e in reversed(range(1, half))}
        return [got[e] for e in range(1, half)]

    q_mirror = lax.ppermute(draft_q, "seq", across)

    payload = 4 * block + 2 * accept
    quarter = count // 4
    every = lambda kind, first=0: [(kind, k) for k in range(first, quarter)]
    bulk = every("inner") + every("outer") + every("same", 1) + every("across")
    *sends, bias, acc_rows = pl.pallas_call(
        functools.partial(prep_kernel, ops=bulk, block=block, quarter=quarter),
        out_shape=[pltpu.VMEM((payload, kv_width), bf16)] * len(bulk)
        + [pltpu.VMEM((drafts, rows), f32), pltpu.VMEM((2 * accept, kv_width), bf16)],
        in_specs=[SMEM, SMEM, VMEM, VMEM, VMEM, VMEM, HBM, HBM],
        out_specs=[VMEM] * (len(bulk) + 2),
        scratch_shapes=[pltpu.SemaphoreType.DMA((4 * len(bulk),))],
        compiler_params=limit(4),
        cost_estimate=CHEAP,
        name="prep",
    )(me1, migrating, parents, accepted, draft_k, draft_v, cache_k, cache_v)
    sends = dict(zip(bulk, sends))
    gots = {}

    def migrate(which, after):
        ready, after = lax.optimization_barrier(([sends[op] for op in which], after))
        for op, send in zip(which, ready):
            gots[op] = lax.ppermute(send, "seq", [(i, i ^ deltas(i, *op, quarter)[0]) for i in range(count)])
        return after

    q_mirror, bias = lax.optimization_barrier((q_mirror, bias))
    q_both = jnp.concatenate([draft_q, q_mirror], axis=0)
    q_got = to_mates([q_both] * half)
    far = every("across")
    draft_k = migrate(every("inner"), draft_k)
    q_got[0] = migrate(every("outer"), q_got[0])
    shapes = [pltpu.HBM(cache_k.shape, bf16)] * 2
    token = pltpu.VMEM((8, 128), f32)

    def put(which, filled, after, fill=False):
        pipes = [pltpu.SemaphoreType.DMA((4 * max(len(which), 1),))]
        if fill:
            pipes += [
                pltpu.VMEM((2, 2, cache_dev, kv_width), bf16),
                pltpu.VMEM((2, 2, block, kv_width), bf16),
                pltpu.SemaphoreType.DMA((2, 2, 2)),
                pltpu.SemaphoreType.DMA((2, 2, 2)),
            ]
        caches = [cache_k, cache_v] if fill else []
        base = 3 + len(which) + len(caches)
        return pl.pallas_call(
            functools.partial(put_kernel, ops=which, block=block, quarter=quarter, first=not filled, fill=fill),
            out_shape=shapes + [token],
            in_specs=[SMEM] * 2 + [ANY] + [VMEM] * len(which) + [HBM] * (len(caches) + len(filled)),
            out_specs=[HBM, HBM, VMEM],
            input_output_aliases={base: 0, base + 1: 1} if filled else {},
            scratch_shapes=pipes,
            compiler_params=limit(6),
            cost_estimate=CHEAP,
            name="put",
        )(me1, migrating, after, *[gots[op] for op in which], *caches, *filled)

    steps = requests // 2
    kind = bf16 if rows % 16 == 0 else f32
    parts = pl.pallas_call(
        functools.partial(attend_kernel, half=half, count=count, block=block, group=group, steps=steps),
        out_shape=[pltpu.VMEM((2 * rows, q_width + STATS), bf16)] * half,
        in_specs=[SMEM] * 3 + [VMEM] * half + [HBM] * 2 + [VMEM] * 3,
        out_specs=[VMEM] * half,
        scratch_shapes=[
            pltpu.VMEM((2 * steps, cache_dev, kv_width), bf16),
            pltpu.VMEM((2 * steps, cache_dev, kv_width), bf16),
            pltpu.VMEM((2, half, rows, q_width), kind),
            pltpu.VMEM((2, half, rows, q_width + STATS), kind),
            pltpu.SemaphoreType.DMA((2 * steps, 2)),
        ],
        compiler_params=limit(20),
        cost_estimate=CHEAP,
        name="attend",
    )(me1, lengths, migrating, q_both, *q_got, cache_k, cache_v, draft_k, draft_v, bias)
    *filled, done = put(every("inner"), [], parts[0])
    done = migrate(far[: quarter // 2], done)
    parts, done = lax.optimization_barrier((parts, done))
    parts_got = to_mates(parts)
    *filled, done = put(every("outer"), filled, done)
    done = migrate(far[quarter // 2 :], done)
    *filled, done = put(far[: quarter // 2], filled, done)
    done = migrate(every("same", 1), done)
    parts_got, done = lax.optimization_barrier((parts_got, done))
    theirs_sum = pl.pallas_call(
        functools.partial(reduce_kernel, heads=heads),
        out_shape=pltpu.VMEM((rows, q_width + STATS), bf16),
        in_specs=[VMEM] * half,
        out_specs=VMEM,
        compiler_params=limit(2),
        cost_estimate=CHEAP,
        name="reduce_other",
    )(parts[0], *parts_got)
    crossed = lax.ppermute(theirs_sum, "seq", across)
    theirs_sum, done = lax.optimization_barrier((theirs_sum, done))
    *filled, done = put([], filled, done, fill=True)
    last = far[quarter // 2 :] + every("same", 1)
    width = out_weight.shape[1] // ways
    *outs, own = pl.pallas_call(
        functools.partial(project_kernel, heads=heads, ways=ways),
        out_shape=[pltpu.VMEM((rows, width), bf16)] * (ways - 1) + [pltpu.VMEM((rows, width), f32)],
        in_specs=[SMEM] + [VMEM] * (half + 2) + [HBM],
        out_specs=[VMEM] * ways,
        scratch_shapes=[pltpu.VMEM((ways, q_width, width), bf16), pltpu.SemaphoreType.DMA((ways,))],
        compiler_params=limit(12),
        cost_estimate=CHEAP,
        name="project",
    )(tp1, done, parts[0], *parts_got, crossed, out_weight)
    out_got = [
        lax.ppermute(x, "tp", [(i, i ^ (d + 1)) for i in range(ways)]) for d, x in enumerate(outs)
    ]
    span = 32
    base = 5 + len(bulk)
    own, filled = lax.optimization_barrier((own, filled))
    new_k, new_v, done = pl.pallas_call(
        functools.partial(place_kernel, ops=bulk, last=last, quarter=quarter, block=block),
        out_shape=shapes + [token],
        in_specs=[SMEM] * 4 + [VMEM] * (1 + len(bulk)) + [HBM, HBM],
        out_specs=[HBM, HBM, VMEM],
        input_output_aliases={base: 0, base + 1: 1},
        scratch_shapes=[
            pltpu.VMEM((2, requests, span, kv_width), bf16),
            pltpu.SemaphoreType.DMA((4 * len(last),)),
            pltpu.SemaphoreType.DMA((2, 2, requests)),
        ],
        compiler_params=limit(4),
        cost_estimate=CHEAP,
        name="place",
    )(me1, migrating, lengths, accepted, acc_rows, *[gots[op] for op in bulk], *filled)
    attn_out = pl.pallas_call(
        final_kernel,
        out_shape=jax.ShapeDtypeStruct((rows, width), bf16),
        in_specs=[VMEM] * (1 + ways),
        out_specs=VMEM,
        compiler_params=limit(2),
        cost_estimate=CHEAP,
        name="final",
    )(done, own, *out_got)

    return (attn_out, new_k, new_v)


def solution(mesh):
    in_specs = (
        P("seq", "tp"),
        P("seq", "tp"),
        P("seq", "tp"),
        P(None, "seq", "tp"),
        P(None, "seq", "tp"),
        P(),
        P(),
        P(),
        P(),
        P("tp", None),
    )
    out_specs = (P("seq", "tp"), P(None, "seq", "tp"), P(None, "seq", "tp"))
    return jax.shard_map(
        per_device, mesh=mesh, in_specs=in_specs, out_specs=out_specs, check_vma=False
    )
```

time: 87.7 us -> 76 us (0.87)
  waiting for transfers between devices: 27.2 us -> 11.8 us
  starting transfers between devices: 30.2 us -> 36.5 us
  Pallas kernels: 28.1 us -> 26.5 us
    ppermute x12 -> x17, starting transfers between devices: 19 us -> 32.3 us  [the longest x7 19.6 us: migrate(): lax.ppermute(send, 'seq', [(i, i ^ deltas(i, *op, quarter)[0]) for i in r...]
    ppermute x12 -> x17, waiting for transfers between devices: 20.1 us -> 11.8 us  [the longest x6 6.98 us: to_mates(): lax.ppermute(parts[e], 'seq', beside[e])]
    all_to_all x2 -> x0, waiting for transfers between devices: 7.16 us -> none  [the longest x1 7.16 us: per_device(): lax.all_to_all(theirs_sum, 'seq', 0, 0, axis_index_groups=[[i, i + half]...]
    all_to_all x2 -> x0, starting transfers between devices: 7.13 us -> none  [the longest x1 3.7 us: per_device(): lax.all_to_all(near_send, 'seq', 0, 0, axis_index_groups=sides, tiled=True)]
    pallas_call x7 -> x8, Pallas kernels: 19.9 us -> 18.9 us  [the longest x4 7.72 us: put(): pl.pallas_call(functools.partial(put_kernel, ops=which, block=block, quar...]
  transfers between devices with their start and end apart: 15 -> 18, of which waited for: 7 -> 7; matrix products, arithmetic and copies ran while one was open for 0% -> 0% of each run, Pallas kernels for 32% -> 34%
where the time goes in v3:
time: 76 us; the launch traced here: 75.5 us
  starting transfers between devices  36.5 us (48%)
  Pallas kernels  26.5 us (35%)
  waiting for transfers between devices  11.8 us (16%)
  between operations  0.77 us (1%)
    ppermute x7, starting transfers between devices, migrate(): lax.ppermute(send, 'seq', [(i, i ^ deltas(i, *op, quarter)[0]) for i in r...  19.6 us
    pallas_call x4, Pallas kernels, put(): pl.pallas_call(functools.partial(put_kernel, ops=which, block=block, quar...  7.72 us
    pallas_call x1, Pallas kernels, per_device(): pl.pallas_call(functools.partial(attend_kernel, half=half, count=count, b...  7.13 us
    ppermute x6, starting transfers between devices, to_mates(): lax.ppermute(parts[e], 'seq', beside[e])  7.04 us
    ppermute x6, waiting for transfers between devices, to_mates(): lax.ppermute(parts[e], 'seq', beside[e])  6.98 us
    ppermute x1, starting transfers between devices, per_device(): q_mirror = lax.ppermute(draft_q, 'seq', across)  4.1 us
    pallas_call x1, Pallas kernels, per_device(): pl.pallas_call(functools.partial(project_kernel, heads=heads, ways=ways),...  4.03 us
    ppermute x1, starting transfers between devices, per_device(): crossed = lax.ppermute(theirs_sum, 'seq', across)  3.8 us
  transfers between devices with their start and end apart: 18, of which 7 were waited for; matrix products, arithmetic and copies ran while one was open for 0% of the time, Pallas kernels for 34%

profile of v3, /device:TPU:0, one launch (start us, length us, event | category | flops | bytes accessed | tf_op | source)
XLA Modules:
  0.0 75.5 jit_solution(7182756504357444719)
XLA Ops:
  0.6 4.1 %collective-permute-start.2 = (bf16[32,1024]{1,0:T(8,128)(2,1)}, bf16[32,1024]{1,0:T(8,128)(2,1)S(1)}, u32[]{:S(2)}, u32[]{:S(2)}) collective-permute-start(bf16[32,1024]{1,0:T(8,128)(2,1)} %param.10), channel_id=1, source_target_pairs={{0,16},{4,20},{8,24},{12,28},{16,0},{20,4},{24,8},{28,12},{1,17},{... | collective-permute-start | bytes 196616 | tf_op jit(solution)/shard_map/ppermute | solution.py:371
  4.7 0.0 copy-start
  4.7 3.0 %prep.1 = (bf16[528,256]{1,0:T(8,128)(2,1)S(1)}, bf16[528,256]{1,0:T(8,128)(2,1)S(1)}, bf16[528,256]{1,0:T(8,128)(2,1)S(1)}, bf16[528,256]{1,0:T(8,128)(2,1)S(1)...) custom-call(s32[1]{0:T(128)} %bitcast.me_ref, ...), custom_call_target="tpu_custom_call" | custom-call | flops 1 | bytes 1 | tf_op jit(solution)/shard_map/prep/pallas_call | solution.py:377
  7.8 1.6 %collective-permute-start = (bf16[528,256]{1,0:T(8,128)(2,1)S(1)}, bf16[528,256]{1,0:T(8,128)(2,1)S(1)}, u32[]{:S(2)}, u32[]{:S(2)}) collective-permute-start(bf16[528,256]{1,0:T(8,128)(2,1)S(1)} %get-tuple-element.65), channel_id=1, source_target_pairs={{0,8},{4,12},{8,24},{12,28},{16,0},{20,4},{24,16},{28,20},{1,9},{5... | collective-permute-start | bytes 811016 | tf_op jit(solution)/shard_map/ppermute | solution.py:394
  9.4 1.3 %collective-permute-start.1 = (bf16[528,256]{1,0:T(8,128)(2,1)S(1)}, bf16[528,256]{1,0:T(8,128)(2,1)S(1)}, u32[]{:S(2)}, u32[]{:S(2)}) collective-permute-start(bf16[528,256]{1,0:T(8,128)(2,1)S(1)} %get-tuple-element.66), channel_id=1, source_target_pairs={{0,12},{4,8},{8,28},{12,24},{16,4},{20,0},{24,20},{28,16},{1,13},{... | collective-permute-start | bytes 811016 | tf_op jit(solution)/shard_map/ppermute | solution.py:394
  10.7 0.0 copy-done
  10.7 0.0 collective-permute-done.2
  10.7 0.6 collective-permute-start.3
  11.3 1.4 %collective-permute-start.7 = (bf16[64,1024]{1,0:T(8,128)(2,1)S(1)}, bf16[64,1024]{1,0:T(8,128)(2,1)S(1)}, u32[]{:S(2)}, u32[]{:S(2)}) collective-permute-start(bf16[64,1024]{1,0:T(8,128)(2,1)S(1)} %constant_dynamic-update-slice_fusion.rest_0_), channel_id=1, source_target_pairs={{0,12},{4,8},{8,4},{12,0},{16,28},{20,24},{24,20},{28,16},{1,13},{... | collective-permute-start | bytes 393224 | tf_op jit(solution)/shard_map/ppermute | solution.py:368
  12.7 1.6 %collective-permute-start.6 = (bf16[64,1024]{1,0:T(8,128)(2,1)S(1)}, bf16[64,1024]{1,0:T(8,128)(2,1)S(1)}, u32[]{:S(2)}, u32[]{:S(2)}) collective-permute-start(bf16[64,1024]{1,0:T(8,128)(2,1)S(1)} %constant_dynamic-update-slice_fusion.rest_0_), channel_id=1, source_target_pairs={{0,8},{4,12},{8,0},{12,4},{16,24},{20,28},{24,16},{28,20},{1,9},{5... | collective-permute-start | bytes 393224 | tf_op jit(solution)/shard_map/ppermute | solution.py:368
  14.2 1.5 %collective-permute-done.3.rest_1_ = bf16[64,1024]{1,0:T(8,128)(2,1)S(1)} collective-permute-done((bf16[64,1024]{1,0:T(8,128)(2,1)S(1)}, bf16[64,1024]{1,0:T(8,128)(2,1)S(1)}, u32[]{:S(2)}, u32[]{:S(2)}) %collective-permute-start.3) | collective-permute-done | bytes 131104 | tf_op jit(solution)/shard_map/ppermute | solution.py:368
  15.7 9.8 %collective-permute-start.4 = (bf16[528,256]{1,0:T(8,128)(2,1)S(1)}, bf16[528,256]{1,0:T(8,128)(2,1)S(1)}, u32[]{:S(2)}, u32[]{:S(2)}) collective-permute-start(bf16[528,256]{1,0:T(8,128)(2,1)S(1)} %get-tuple-element.71), channel_id=1, source_target_pairs={{0,16},{4,20},{8,0},{12,4},{16,24},{20,28},{24,8},{28,12},{1,17},{... | collective-permute-start | bytes 811016 | tf_op jit(solution)/shard_map/ppermute | solution.py:394
  25.6 0.7 collective-permute-done.7.rest_3_
  26.3 0.5 collective-permute-start.5
  26.8 1.4 %collective-permute-done.6.rest_2_ = bf16[64,1024]{1,0:T(8,128)(2,1)S(1)} collective-permute-done((bf16[64,1024]{1,0:T(8,128)(2,1)S(1)}, bf16[64,1024]{1,0:T(8,128)(2,1)S(1)}, u32[]{:S(2)}, u32[]{:S(2)}) %collective-permute-start.6) | collective-permute-done | bytes 131104 | tf_op jit(solution)/shard_map/ppermute | solution.py:368
  28.2 7.1 %attend.1 = (bf16[64,1152]{1,0:T(8,128)(2,1)S(1)}, bf16[64,1152]{1,0:T(8,128)(2,1)S(1)}, bf16[64,1152]{1,0:T(8,128)(2,1)S(1)}, bf16[64,1152]{1,0:T(8,128)(2,1)S(1)}) custom-call(s32[1]{0:T(128)} %bitcast.me_ref, s32[4]{0:T(128)} %len_ref.3, s32[4]{0:T(128)} %mig_ref.13, bf16[64,1024]{1,0:T(8,128)(2,1)S(1)} %constant_dynamic-update-slice_fusion.rest_0_, ...), custom_call_target="tpu_custom_call" | custom-call | flops 1 | bytes 1 | tf_op jit(solution)/shard_map/attend/pallas_call | solution.py:431
  35.3 0.0 collective-permute-done.rest_0_
  35.3 0.0 collective-permute-done.1.rest_1_
  35.3 1.5 %put.4 = (bf16[4,1024,256]{2,1,0:T(8,128)(2,1)}, bf16[4,1024,256]{2,1,0:T(8,128)(2,1)}, f32[8,128]{1,0:T(8,128)S(1)}) custom-call(s32[1]{0:T(128)} %bitcast.me_ref, s32[4]{0:T(128)} %mig_ref.13, bf16[64,1152]{1,0:T(8,128)(2,1)S(1)} %get-tuple-element.96.after_ref.refs_0_, bf16[528,256]{1,0:T(8,128)(2,1)S(1)} %collective-permute-done.rest_0_, ...), custom_call_target="tpu_custom_call" | custom-call | flops 1 | bytes 1 | tf_op jit(solution)/shard_map/put/pallas_call | solution.py:417
  36.9 2.6 %collective-permute-start.8 = (bf16[528,256]{1,0:T(8,128)(2,1)S(1)}, bf16[528,256]{1,0:T(8,128)(2,1)S(1)}, u32[]{:S(2)}, u32[]{:S(2)}) collective-permute-start(bf16[528,256]{1,0:T(8,128)(2,1)S(1)} %get-tuple-element.90), channel_id=1, source_target_pairs={{0,24},{4,28},{8,16},{12,20},{16,8},{20,12},{24,0},{28,4},{1,25},{... | collective-permute-start | bytes 811016 | tf_op jit(solution)/shard_map/ppermute | solution.py:394
  39.4 1.5 %collective-permute-start.11 = (bf16[64,1152]{1,0:T(8,128)(2,1)S(1)}, bf16[64,1152]{1,0:T(8,128)(2,1)S(1)}, u32[]{:S(2)}, u32[]{:S(2)}) collective-permute-start(bf16[64,1152]{1,0:T(8,128)(2,1)S(1)} %get-tuple-element.97), channel_id=1, source_target_pairs={{0,4},{4,0},{8,12},{12,8},{16,20},{20,16},{24,28},{28,24},{1,5},{5... | collective-permute-start | bytes 442376 | tf_op jit(solution)/shard_map/ppermute | solution.py:368
  40.9 0.0 collective-permute-start.12
  40.9 0.0 collective-permute-done.4.rest_0_.rest_2_
  40.9 2.0 %collective-permute-start.13 = (bf16[64,1152]{1,0:T(8,128)(2,1)S(1)}, bf16[64,1152]{1,0:T(8,128)(2,1)S(1)}, u32[]{:S(2)}, u32[]{:S(2)}) collective-permute-start(bf16[64,1152]{1,0:T(8,128)(2,1)S(1)} %get-tuple-element.99), channel_id=1, source_target_pairs={{0,12},{4,8},{8,4},{12,0},{16,28},{20,24},{24,20},{28,16},{1,13},{... | collective-permute-start | bytes 442376 | tf_op jit(solution)/shard_map/ppermute | solution.py:368
  42.9 0.0 collective-permute-done.5.rest_1_.rest_3_
  42.9 1.5 %put.5 = (bf16[4,1024,256]{2,1,0:T(8,128)(2,1)}, bf16[4,1024,256]{2,1,0:T(8,128)(2,1)}, f32[8,128]{1,0:T(8,128)S(1)}) custom-call(s32[1]{0:T(128)} %bitcast.me_ref, s32[4]{0:T(128)} %mig_ref.13, f32[8,128]{1,0:T(8,128)S(1)} %get-tuple-element.85.after_ref, ...), custom_call_target="tpu_custom_call", output_to_operand_aliasing={{0}: (5, {}), {1}: (6, {})} | custom-call | flops 1 | bytes 1 | tf_op jit(solution)/shard_map/put/pallas_call | solution.py:417
  44.5 2.3 %collective-permute-start.10 = (bf16[528,256]{1,0:T(8,128)(2,1)S(1)}, bf16[528,256]{1,0:T(8,128)(2,1)S(1)}, u32[]{:S(2)}, u32[]{:S(2)}) collective-permute-start(bf16[528,256]{1,0:T(8,128)(2,1)S(1)} %get-tuple-element.95), channel_id=1, source_target_pairs={{0,28},{4,24},{8,20},{12,16},{16,12},{20,8},{24,4},{28,0},{1,29},{... | collective-permute-start | bytes 811016 | tf_op jit(solution)/shard_map/ppermute | solution.py:394
  46.8 1.4 %collective-permute-done.8.rest_0_.rest_5_ = bf16[528,256]{1,0:T(8,128)(2,1)S(1)} collective-permute-done((bf16[528,256]{1,0:T(8,128)(2,1)S(1)}, bf16[528,256]{1,0:T(8,128)(2,1)S(1)}, u32[]{:S(2)}, u32[]{:S(2)}) %collective-permute-start.8) | collective-permute-done | bytes 270368 | tf_op jit(solution)/shard_map/ppermute | solution.py:394
  48.1 1.4 %put.6 = (bf16[4,1024,256]{2,1,0:T(8,128)(2,1)}, bf16[4,1024,256]{2,1,0:T(8,128)(2,1)}, f32[8,128]{1,0:T(8,128)S(1)}) custom-call(s32[1]{0:T(128)} %bitcast.me_ref, s32[4]{0:T(128)} %mig_ref.13, f32[8,128]{1,0:T(8,128)S(1)} %get-tuple-element.89.after_ref, ...), custom_call_target="tpu_custom_call", output_to_operand_aliasing={{0}: (4, {}), {1}: (5, {})} | custom-call | flops 1 | bytes 1 | tf_op jit(solution)/shard_map/put/pallas_call | solution.py:417
  49.5 1.5 %collective-permute-start.9 = (bf16[528,256]{1,0:T(8,128)(2,1)S(1)}, bf16[528,256]{1,0:T(8,128)(2,1)S(1)}, u32[]{:S(2)}, u32[]{:S(2)}) collective-permute-start(bf16[528,256]{1,0:T(8,128)(2,1)S(1)} %get-tuple-element.94), channel_id=1, source_target_pairs={{0,4},{4,0},{8,12},{12,8},{16,20},{20,16},{24,28},{28,24},{1,5},{5... | collective-permute-start | bytes 811016 | tf_op jit(solution)/shard_map/ppermute | solution.py:394
  51.0 0.0 collective-permute-done.11.refs_1_
  51.0 0.0 collective-permute-done.12.refs_2_
  51.1 3.4 %collective-permute-done.13.refs_3_ = bf16[64,1152]{1,0:T(8,128)(2,1)S(1)} collective-permute-done((bf16[64,1152]{1,0:T(8,128)(2,1)S(1)}, bf16[64,1152]{1,0:T(8,128)(2,1)S(1)}, u32[]{:S(2)}, u32[]{:S(2)}) %collective-permute-start.13) | collective-permute-done | bytes 147488 | tf_op jit(solution)/shard_map/ppermute | solution.py:368
  54.4 0.4 reduce_other.1
  54.8 3.8 %collective-permute-start.14 = (bf16[32,1152]{1,0:T(8,128)(2,1)S(1)}, bf16[32,1152]{1,0:T(8,128)(2,1)S(1)}, u32[]{:S(2)}, u32[]{:S(2)}) collective-permute-start(bf16[32,1152]{1,0:T(8,128)(2,1)S(1)} %reduce_other.1), channel_id=1, source_target_pairs={{0,16},{4,20},{8,24},{12,28},{16,0},{20,4},{24,8},{28,12},{1,17},{... | collective-permute-start | bytes 221192 | tf_op jit(solution)/shard_map/ppermute | solution.py:465
  58.7 3.3 %put.7 = (bf16[4,1024,256]{2,1,0:T(8,128)(2,1)}, bf16[4,1024,256]{2,1,0:T(8,128)(2,1)}, f32[8,128]{1,0:T(8,128)S(1)}) custom-call(s32[1]{0:T(128)} %bitcast.me_ref, s32[4]{0:T(128)} %mig_ref.13, f32[8,128]{1,0:T(8,128)S(1)} %get-tuple-element.105.after_ref, bf16[4,1024,256]{2,1,0:T(8,128)(2,1)} %rest_0_.1, ...), custom_call_target="tpu_custom_call", output_to_operand_aliasing={{0}: (5, {}), {1}: (6, {})} | custom-call | flops 1 | bytes 1 | tf_op jit(solution)/shard_map/put/pallas_call | solution.py:417
  61.9 3.1 %collective-permute-done.14.refs_4_ = bf16[32,1152]{1,0:T(8,128)(2,1)S(1)} collective-permute-done((bf16[32,1152]{1,0:T(8,128)(2,1)S(1)}, bf16[32,1152]{1,0:T(8,128)(2,1)S(1)}, u32[]{:S(2)}, u32[]{:S(2)}) %collective-permute-start.14) | collective-permute-done | bytes 73760 | tf_op jit(solution)/shard_map/ppermute | solution.py:465
  65.0 4.0 %project.1 = (bf16[32,1024]{1,0:T(8,128)(2,1)S(1)}, bf16[32,1024]{1,0:T(8,128)(2,1)S(1)}, bf16[32,1024]{1,0:T(8,128)(2,1)S(1)}, f32[32,1024]{1,0:T(8,128)S(1)}) custom-call(s32[1]{0:T(128)} %bitcast.1.tp_ref, f32[8,128]{1,0:T(8,128)S(1)} %get-tuple-element.108.done_ref, bf16[64,1152]{1,0:T(8,128)(2,1)S(1)} %get-tuple-element.96.after_ref.refs_0_, ...), custom_call_target="tpu_custom_call" | custom-call | flops 1 | bytes 1 | tf_op jit(solution)/shard_map/project/pallas_call | solution.py:470
  69.1 0.1 collective-permute-start.15
  69.2 1.6 %collective-permute-start.16 = (bf16[32,1024]{1,0:T(8,128)(2,1)S(1)}, bf16[32,1024]{1,0:T(8,128)(2,1)S(1)}, u32[]{:S(2)}, u32[]{:S(2)}) collective-permute-start(bf16[32,1024]{1,0:T(8,128)(2,1)S(1)} %get-tuple-element.117), channel_id=1, source_target_pairs={{0,2},{1,3},{2,0},{3,1},{4,6},{5,7},{6,4},{7,5},{8,10},{9,11},{10,... | collective-permute-start | bytes 196616 | tf_op jit(solution)/shard_map/ppermute | solution.py:481
  70.8 0.3 collective-permute-start.17
  71.0 0.0 collective-permute-done.10.rest_6_
  71.0 0.0 collective-permute-done.9.rest_4_
  71.0 3.4 %place.1 = (bf16[4,1024,256]{2,1,0:T(8,128)(2,1)}, bf16[4,1024,256]{2,1,0:T(8,128)(2,1)}, f32[8,128]{1,0:T(8,128)S(1)}) custom-call(s32[1]{0:T(128)} %bitcast.me_ref, s32[4]{0:T(128)} %mig_ref.13, s32[4]{0:T(128)} %len_ref.3, s32[4,8]{1,0:T(4,128)} %accepted_ref.3, ...), custom_call_target="tpu_custom_call", output_to_operand_aliasing={{0}: (12, {}), {1}: (13, {})} | custom-call | flops 1 | bytes 1 | tf_op jit(solution)/shard_map/place/pallas_call | solution.py:486
  74.5 0.0 collective-permute-done.15.rest_0_
  74.5 0.0 collective-permute-done.16.rest_1_
  74.5 0.3 collective-permute-done.17.rest_2_
  74.8 0.7 final.1
  (2 shorter events, 0.0 us)
Async XLA Ops:
  0.6 10.0 %collective-permute-start.2 = (bf16[32,1024]{1,0:T(8,128)(2,1)}, bf16[32,1024]{1,0:T(8,128)(2,1)S(1)}, u32[]{:S(2)}, u32[]{:S(2)}) collective-permute-start(bf16[32,1024]{1,0:T(8,128)(2,1)} %param.10), channel_id=1, source_target_pairs={{0,16},{4,20},{8,24},{12,28},{16,0},{20,4},{24,8},{28,12},{1,17},{... | collective-permute-start | bytes 196616 | tf_op jit(solution)/shard_map/ppermute | solution.py:371
  4.7 5.9 %copy-start = (bf16[32,1024]{1,0:T(8,128)(2,1)S(1)}, bf16[32,1024]{1,0:T(8,128)(2,1)}, u32[]{:S(2)}) copy-start(bf16[32,1024]{1,0:T(8,128)(2,1)} %param.10) | copy-start | bytes 196612
  7.8 27.5 %collective-permute-start = (bf16[528,256]{1,0:T(8,128)(2,1)S(1)}, bf16[528,256]{1,0:T(8,128)(2,1)S(1)}, u32[]{:S(2)}, u32[]{:S(2)}) collective-permute-start(bf16[528,256]{1,0:T(8,128)(2,1)S(1)} %get-tuple-element.65), channel_id=1, source_target_pairs={{0,8},{4,12},{8,24},{12,28},{16,0},{20,4},{24,16},{28,20},{1,9},{5... | collective-permute-start | bytes 811016 | tf_op jit(solution)/shard_map/ppermute | solution.py:394
  9.4 25.9 %collective-permute-start.1 = (bf16[528,256]{1,0:T(8,128)(2,1)S(1)}, bf16[528,256]{1,0:T(8,128)(2,1)S(1)}, u32[]{:S(2)}, u32[]{:S(2)}) collective-permute-start(bf16[528,256]{1,0:T(8,128)(2,1)S(1)} %get-tuple-element.66), channel_id=1, source_target_pairs={{0,12},{4,8},{8,28},{12,24},{16,4},{20,0},{24,20},{28,16},{1,13},{... | collective-permute-start | bytes 811016 | tf_op jit(solution)/shard_map/ppermute | solution.py:394
  10.7 5.1 %collective-permute-start.3 = (bf16[64,1024]{1,0:T(8,128)(2,1)S(1)}, bf16[64,1024]{1,0:T(8,128)(2,1)S(1)}, u32[]{:S(2)}, u32[]{:S(2)}) collective-permute-start(bf16[64,1024]{1,0:T(8,128)(2,1)S(1)} %constant_dynamic-update-slice_fusion.rest_0_), channel_id=1, source_target_pairs={{0,4},{4,0},{8,12},{12,8},{16,20},{20,16},{24,28},{28,24},{1,5},{5... | collective-permute-start | bytes 393224 | tf_op jit(solution)/shard_map/ppermute | solution.py:368
  11.3 15.0 %collective-permute-start.7 = (bf16[64,1024]{1,0:T(8,128)(2,1)S(1)}, bf16[64,1024]{1,0:T(8,128)(2,1)S(1)}, u32[]{:S(2)}, u32[]{:S(2)}) collective-permute-start(bf16[64,1024]{1,0:T(8,128)(2,1)S(1)} %constant_dynamic-update-slice_fusion.rest_0_), channel_id=1, source_target_pairs={{0,12},{4,8},{8,4},{12,0},{16,28},{20,24},{24,20},{28,16},{1,13},{... | collective-permute-start | bytes 393224 | tf_op jit(solution)/shard_map/ppermute | solution.py:368
  12.7 15.5 %collective-permute-start.6 = (bf16[64,1024]{1,0:T(8,128)(2,1)S(1)}, bf16[64,1024]{1,0:T(8,128)(2,1)S(1)}, u32[]{:S(2)}, u32[]{:S(2)}) collective-permute-start(bf16[64,1024]{1,0:T(8,128)(2,1)S(1)} %constant_dynamic-update-slice_fusion.rest_0_), channel_id=1, source_target_pairs={{0,8},{4,12},{8,0},{12,4},{16,24},{20,28},{24,16},{28,20},{1,9},{5... | collective-permute-start | bytes 393224 | tf_op jit(solution)/shard_map/ppermute | solution.py:368
  15.7 25.2 %collective-permute-start.4 = (bf16[528,256]{1,0:T(8,128)(2,1)S(1)}, bf16[528,256]{1,0:T(8,128)(2,1)S(1)}, u32[]{:S(2)}, u32[]{:S(2)}) collective-permute-start(bf16[528,256]{1,0:T(8,128)(2,1)S(1)} %get-tuple-element.71), channel_id=1, source_target_pairs={{0,16},{4,20},{8,0},{12,4},{16,24},{20,28},{24,8},{28,12},{1,17},{... | collective-permute-start | bytes 811016 | tf_op jit(solution)/shard_map/ppermute | solution.py:394
  26.3 16.6 %collective-permute-start.5 = (bf16[528,256]{1,0:T(8,128)(2,1)S(1)}, bf16[528,256]{1,0:T(8,128)(2,1)S(1)}, u32[]{:S(2)}, u32[]{:S(2)}) collective-permute-start(bf16[528,256]{1,0:T(8,128)(2,1)S(1)} %get-tuple-element.72), channel_id=1, source_target_pairs={{0,20},{4,16},{8,4},{12,0},{16,28},{20,24},{24,12},{28,8},{1,21},{... | collective-permute-start | bytes 811016 | tf_op jit(solution)/shard_map/ppermute | solution.py:394
  36.9 11.3 %collective-permute-start.8 = (bf16[528,256]{1,0:T(8,128)(2,1)S(1)}, bf16[528,256]{1,0:T(8,128)(2,1)S(1)}, u32[]{:S(2)}, u32[]{:S(2)}) collective-permute-start(bf16[528,256]{1,0:T(8,128)(2,1)S(1)} %get-tuple-element.90), channel_id=1, source_target_pairs={{0,24},{4,28},{8,16},{12,20},{16,8},{20,12},{24,0},{28,4},{1,25},{... | collective-permute-start | bytes 811016 | tf_op jit(solution)/shard_map/ppermute | solution.py:394
  39.4 11.6 %collective-permute-start.11 = (bf16[64,1152]{1,0:T(8,128)(2,1)S(1)}, bf16[64,1152]{1,0:T(8,128)(2,1)S(1)}, u32[]{:S(2)}, u32[]{:S(2)}) collective-permute-start(bf16[64,1152]{1,0:T(8,128)(2,1)S(1)} %get-tuple-element.97), channel_id=1, source_target_pairs={{0,4},{4,0},{8,12},{12,8},{16,20},{20,16},{24,28},{28,24},{1,5},{5... | collective-permute-start | bytes 442376 | tf_op jit(solution)/shard_map/ppermute | solution.py:368
  40.9 10.1 %collective-permute-start.12 = (bf16[64,1152]{1,0:T(8,128)(2,1)S(1)}, bf16[64,1152]{1,0:T(8,128)(2,1)S(1)}, u32[]{:S(2)}, u32[]{:S(2)}) collective-permute-start(bf16[64,1152]{1,0:T(8,128)(2,1)S(1)} %get-tuple-element.98), channel_id=1, source_target_pairs={{0,8},{4,12},{8,0},{12,4},{16,24},{20,28},{24,16},{28,20},{1,9},{5... | collective-permute-start | bytes 442376 | tf_op jit(solution)/shard_map/ppermute | solution.py:368
  40.9 13.5 %collective-permute-start.13 = (bf16[64,1152]{1,0:T(8,128)(2,1)S(1)}, bf16[64,1152]{1,0:T(8,128)(2,1)S(1)}, u32[]{:S(2)}, u32[]{:S(2)}) collective-permute-start(bf16[64,1152]{1,0:T(8,128)(2,1)S(1)} %get-tuple-element.99), channel_id=1, source_target_pairs={{0,12},{4,8},{8,4},{12,0},{16,28},{20,24},{24,20},{28,16},{1,13},{... | collective-permute-start | bytes 442376 | tf_op jit(solution)/shard_map/ppermute | solution.py:368
  44.5 26.6 %collective-permute-start.10 = (bf16[528,256]{1,0:T(8,128)(2,1)S(1)}, bf16[528,256]{1,0:T(8,128)(2,1)S(1)}, u32[]{:S(2)}, u32[]{:S(2)}) collective-permute-start(bf16[528,256]{1,0:T(8,128)(2,1)S(1)} %get-tuple-element.95), channel_id=1, source_target_pairs={{0,28},{4,24},{8,20},{12,16},{16,12},{20,8},{24,4},{28,0},{1,29},{... | collective-permute-start | bytes 811016 | tf_op jit(solution)/shard_map/ppermute | solution.py:394
  49.5 21.5 %collective-permute-start.9 = (bf16[528,256]{1,0:T(8,128)(2,1)S(1)}, bf16[528,256]{1,0:T(8,128)(2,1)S(1)}, u32[]{:S(2)}, u32[]{:S(2)}) collective-permute-start(bf16[528,256]{1,0:T(8,128)(2,1)S(1)} %get-tuple-element.94), channel_id=1, source_target_pairs={{0,4},{4,0},{8,12},{12,8},{16,20},{20,16},{24,28},{28,24},{1,5},{5... | collective-permute-start | bytes 811016 | tf_op jit(solution)/shard_map/ppermute | solution.py:394
  54.8 10.2 %collective-permute-start.14 = (bf16[32,1152]{1,0:T(8,128)(2,1)S(1)}, bf16[32,1152]{1,0:T(8,128)(2,1)S(1)}, u32[]{:S(2)}, u32[]{:S(2)}) collective-permute-start(bf16[32,1152]{1,0:T(8,128)(2,1)S(1)} %reduce_other.1), channel_id=1, source_target_pairs={{0,16},{4,20},{8,24},{12,28},{16,0},{20,4},{24,8},{28,12},{1,17},{... | collective-permute-start | bytes 221192 | tf_op jit(solution)/shard_map/ppermute | solution.py:465
  69.1 5.4 %collective-permute-start.15 = (bf16[32,1024]{1,0:T(8,128)(2,1)S(1)}, bf16[32,1024]{1,0:T(8,128)(2,1)S(1)}, u32[]{:S(2)}, u32[]{:S(2)}) collective-permute-start(bf16[32,1024]{1,0:T(8,128)(2,1)S(1)} %get-tuple-element.116), channel_id=1, source_target_pairs={{0,1},{1,0},{2,3},{3,2},{4,5},{5,4},{6,7},{7,6},{8,9},{9,8},{10,11... | collective-permute-start | bytes 196616 | tf_op jit(solution)/shard_map/ppermute | solution.py:481
  69.2 5.3 %collective-permute-start.16 = (bf16[32,1024]{1,0:T(8,128)(2,1)S(1)}, bf16[32,1024]{1,0:T(8,128)(2,1)S(1)}, u32[]{:S(2)}, u32[]{:S(2)}) collective-permute-start(bf16[32,1024]{1,0:T(8,128)(2,1)S(1)} %get-tuple-element.117), channel_id=1, source_target_pairs={{0,2},{1,3},{2,0},{3,1},{4,6},{5,7},{6,4},{7,5},{8,10},{9,11},{10,... | collective-permute-start | bytes 196616 | tf_op jit(solution)/shard_map/ppermute | solution.py:481
  70.8 4.0 %collective-permute-start.17 = (bf16[32,1024]{1,0:T(8,128)(2,1)S(1)}, bf16[32,1024]{1,0:T(8,128)(2,1)S(1)}, u32[]{:S(2)}, u32[]{:S(2)}) collective-permute-start(bf16[32,1024]{1,0:T(8,128)(2,1)S(1)} %get-tuple-element.118), channel_id=1, source_target_pairs={{0,3},{1,2},{2,1},{3,0},{4,7},{5,6},{6,5},{7,4},{8,11},{9,10},{10,... | collective-permute-start | bytes 196616 | tf_op jit(solution)/shard_map/ppermute | solution.py:481

commit v4 on v3

--- a/solution.py
+++ b/solution.py
@@ -66,11 +66,11 @@
     return both, both
 
 
-def prep_kernel(me_ref, mig_ref, parents_ref, accepted_ref, dk_ref, dv_ref, ck_ref, cv_ref, *rest, ops, block, quarter):
-    *outs, bias_ref, acc_ref, sems = rest
-    requests, drafts = parents_ref.shape
+def prep_kernel(me_ref, mig_ref, accepted_ref, dk_ref, dv_ref, ck_ref, cv_ref, *rest, ops, block, quarter):
+    *outs, acc_ref, sems = rest
+    requests, accept = accepted_ref.shape
     rows = dk_ref.shape[0]
-    accept = accepted_ref.shape[1]
+    drafts = rows * quarter
     me = me_ref[0]
     pair = migrating_pair(mig_ref, requests)
     goals = [me ^ deltas(me, kind, k, quarter)[0] for kind, k in ops]
@@ -79,6 +79,21 @@
         copy.start()
     request = (me * rows) // drafts
     offset = me * rows - request * drafts
+    mine = lax.broadcasted_iota(i32, (requests, accept), 0) == request
+    node = jnp.sum(jnp.where(mine, accepted_ref[...], 0), axis=0, keepdims=True)
+    pick = jnp.where(lax.broadcasted_iota(i32, (rows, accept), 0) + offset == node, 1.0, 0.0).astype(bf16)
+    chosen = jnp.concatenate([tn(pick, dk_ref[...]), tn(pick, dv_ref[...])], axis=0).astype(bf16)
+    acc_ref[...] = chosen
+    for out in outs:
+        out[4 * block :] = chosen
+    for copy in copies:
+        copy.wait()
+
+
+def tree_bias(me_ref, parents_ref, rows):
+    requests, drafts = parents_ref.shape
+    request = (me_ref[0] * rows) // drafts
+    offset = me_ref[0] * rows - request * drafts
     mine = lax.broadcasted_iota(i32, (requests, drafts), 0) == request
     parent = jnp.sum(jnp.where(mine, parents_ref[...], 0), axis=0, keepdims=True)
     down = lax.broadcasted_iota(i32, (drafts, drafts), 0)
@@ -90,53 +105,50 @@
     pick = jnp.where(
         lax.broadcasted_iota(i32, (drafts, rows), 0) == lax.broadcasted_iota(i32, (drafts, rows), 1) + offset, 1.0, 0.0
     ).astype(bf16)
-    bias_ref[...] = jnp.where(tn(reach, pick) > 0.5, 0.0, NEG)
-    mine = lax.broadcasted_iota(i32, (requests, accept), 0) == request
-    node = jnp.sum(jnp.where(mine, accepted_ref[...], 0), axis=0, keepdims=True)
-    pick = jnp.where(lax.broadcasted_iota(i32, (rows, accept), 0) + offset == node, 1.0, 0.0).astype(bf16)
-    chosen = jnp.concatenate([tn(pick, dk_ref[...]), tn(pick, dv_ref[...])], axis=0).astype(bf16)
-    acc_ref[...] = chosen
-    for out in outs:
-        out[4 * block :] = chosen
-    for copy in copies:
-        copy.wait()
-
-
-def attend_kernel(me_ref, len_ref, mig_ref, *rest, half, count, block, group, steps):
-    q_refs = rest[:half]
-    ck_ref, cv_ref, dk_ref, dv_ref, bias_ref = rest[half : half + 5]
-    outs = rest[-half - 5 : -5]
+    return jnp.where(tn(reach, pick) > 0.5, 0.0, NEG)
+
+
+def attend_kernel(me_ref, len_ref, mig_ref, *rest, count, block, group, own):
+    quarter = count // 4
+    q_refs = rest[:quarter]
+    rest = rest[quarter:]
+    if own:
+        dk_ref, dv_ref, parents_ref = rest[:3]
+        rest = rest[3:]
+    ck_ref, cv_ref = rest[:2]
+    outs = rest[2 : 2 + quarter]
     k_ref, v_ref, q_all, part, sems = rest[-5:]
     me = me_ref[0]
-    spot = lax.rem(me, half)
-    side = me // half
+    spot = lax.rem(me, quarter)
+    z = me // quarter
+    first = z if own else z ^ 1
     rows, q_width = q_all.shape[2:]
     cache_dev = k_ref.shape[1]
     kv_local = k_ref.shape[2] // HD
-    per_request = half // steps
-    drafts = per_request * rows
+    drafts = quarter * rows
     heads = kv_local * group
-    requests = [side * steps + r for r in range(steps)] + [(1 - side) * steps + r for r in range(steps)]
+    requests = [first, first ^ 2]
     loads = []
     for i, request in enumerate(requests):
         for c, (cache, here) in enumerate(((ck_ref, k_ref), (cv_ref, v_ref))):
             loads.append(pltpu.make_async_copy(cache.at[request], here.at[i], sems.at[i, c]))
             loads[-1].start()
-    for e in range(half):
+    for e in range(quarter):
         both = q_refs[e][...].astype(q_all.dtype)
         for k in range(2):
             q_all[k, spot ^ e] = both[k * rows : (k + 1) * rows]
+    if own:
+        bias = tree_bias(me_ref, parents_ref, rows)
     row = lax.broadcasted_iota(i32, (1, cache_dev), 1)
     shift = block.bit_length() - 1
     moved = row + (row >> shift) * ((count - 1) * block) + me * block
     scale = math.log2(math.e) / math.sqrt(HD)
     lane = lax.broadcasted_iota(i32, (drafts, STATS), 1)
     for i, request in enumerate(requests):
-        drafted = i < steps
-        k, step = divmod(i, steps)
+        drafted = own and i == 0
         position = jnp.where(mig_ref[request] == 1, moved, row + me * cache_dev)
         dead = jnp.where(position < len_ref[request], 0.0, NEG)
-        rows_q = q_all[k, step * per_request : (step + 1) * per_request].reshape(drafts, q_width)
+        rows_q = q_all[i].reshape(drafts, q_width)
         loads[2 * i].wait()
         loads[2 * i + 1].wait()
         stats = jnp.zeros((drafts, STATS), f32)
@@ -148,8 +160,7 @@
             s = nt(q, k_ref[i, :, at_g]) * scale + dead
             top = jnp.max(s, axis=1, keepdims=True)
             if drafted:
-                own = jnp.where(request == (me * rows) // drafts, bias_ref[...], NEG)
-                sd = nt(q, dk_ref[:, at_g]) * scale + jnp.concatenate([own] * group, axis=0)
+                sd = nt(q, dk_ref[:, at_g]) * scale + jnp.concatenate([bias] * group, axis=0)
                 top = jnp.maximum(top, jnp.max(sd, axis=1, keepdims=True))
             top = jnp.maximum(top, FLOOR)
             w = jnp.exp2(s - top)
@@ -165,13 +176,13 @@
                 values = split3(top[at]) + split3(total[at])[:2]
                 for n, value in enumerate(values):
                     stats = jnp.where(lane == n * heads + h, value, stats)
-                for p in range(per_request):
-                    part[k, step * per_request + p, :, h * HD : (h + 1) * HD] = o[
+                for p in range(quarter):
+                    part[i, p, :, h * HD : (h + 1) * HD] = o[
                         j * drafts + p * rows : j * drafts + (p + 1) * rows
                     ].astype(part.dtype)
-        for p in range(per_request):
-            part[k, step * per_request + p, :, q_width:] = stats[p * rows : (p + 1) * rows].astype(part.dtype)
-    for e in range(half):
+        for p in range(quarter):
+            part[i, p, :, q_width:] = stats[p * rows : (p + 1) * rows].astype(part.dtype)
+    for e in range(quarter):
         outs[e][...] = jnp.concatenate([part[k, spot ^ e] for k in range(2)], axis=0).astype(bf16)
 
 
@@ -213,21 +224,26 @@
     out[:, heads * HD :] = stats.astype(bf16)
 
 
-def project_kernel(tp_ref, done_ref, *refs, heads, ways):
-    parts, w_ref, outs = refs[: -ways - 3], refs[-ways - 3], refs[-ways - 2 : -3]
-    own_ref, here_ref, sems = refs[-3:]
-    rows, width = own_ref.shape
+def weight_kernel(tp_ref, after_ref, w_ref, here_ref, sems):
+    ways, _, width = here_ref.shape
     loads = []
     for d in range(ways):
         at = pl.ds(pl.multiple_of((tp_ref[0] ^ ((d + 1) % ways)) * width, width), width)
         loads.append(pltpu.make_async_copy(w_ref.at[:, at], here_ref.at[d], sems.at[d]))
         loads[-1].start()
+    for load in loads:
+        load.wait()
+
+
+def project_kernel(done_ref, *refs, heads, ways):
+    parts, here_ref, outs = refs[: -ways - 1], refs[-ways - 1], refs[-ways:-1]
+    own_ref = refs[-1]
+    rows, width = own_ref.shape
     top, total, sums = merge([view(r, 0, rows) for r in parts], heads)
     attention = jnp.concatenate(
         [(sums[h] / total[:, h : h + 1]).astype(bf16) for h in range(heads)], axis=1
     )
     for d in range(ways):
-        loads[d].wait()
         block = jnp.dot(attention, here_ref[d], preferred_element_type=f32)
         if d < ways - 1:
             outs[d][...] = block.astype(bf16)
@@ -374,17 +390,17 @@
     quarter = count // 4
     every = lambda kind, first=0: [(kind, k) for k in range(first, quarter)]
     bulk = every("inner") + every("outer") + every("same", 1) + every("across")
-    *sends, bias, acc_rows = pl.pallas_call(
+    *sends, acc_rows = pl.pallas_call(
         functools.partial(prep_kernel, ops=bulk, block=block, quarter=quarter),
         out_shape=[pltpu.VMEM((payload, kv_width), bf16)] * len(bulk)
-        + [pltpu.VMEM((drafts, rows), f32), pltpu.VMEM((2 * accept, kv_width), bf16)],
-        in_specs=[SMEM, SMEM, VMEM, VMEM, VMEM, VMEM, HBM, HBM],
-        out_specs=[VMEM] * (len(bulk) + 2),
+        + [pltpu.VMEM((2 * accept, kv_width), bf16)],
+        in_specs=[SMEM, SMEM, VMEM, VMEM, VMEM, HBM, HBM],
+        out_specs=[VMEM] * (len(bulk) + 1),
         scratch_shapes=[pltpu.SemaphoreType.DMA((4 * len(bulk),))],
         compiler_params=limit(4),
         cost_estimate=CHEAP,
         name="prep",
-    )(me1, migrating, parents, accepted, draft_k, draft_v, cache_k, cache_v)
+    )(me1, migrating, accepted, draft_k, draft_v, cache_k, cache_v)
     sends = dict(zip(bulk, sends))
     gots = {}
 
@@ -394,7 +410,7 @@
             gots[op] = lax.ppermute(send, "seq", [(i, i ^ deltas(i, *op, quarter)[0]) for i in range(count)])
         return after
 
-    q_mirror, bias = lax.optimization_barrier((q_mirror, bias))
+    q_mirror, acc_rows = lax.optimization_barrier((q_mirror, acc_rows))
     q_both = jnp.concatenate([draft_q, q_mirror], axis=0)
     q_got = to_mates([q_both] * half)
     far = every("across")
@@ -426,30 +442,40 @@
             name="put",
         )(me1, migrating, after, *[gots[op] for op in which], *caches, *filled)
 
-    steps = requests // 2
+    assert requests == 4 and drafts == quarter * rows
     kind = bf16 if rows % 16 == 0 else f32
-    parts = pl.pallas_call(
-        functools.partial(attend_kernel, half=half, count=count, block=block, group=group, steps=steps),
-        out_shape=[pltpu.VMEM((2 * rows, q_width + STATS), bf16)] * half,
-        in_specs=[SMEM] * 3 + [VMEM] * half + [HBM] * 2 + [VMEM] * 3,
-        out_specs=[VMEM] * half,
-        scratch_shapes=[
-            pltpu.VMEM((2 * steps, cache_dev, kv_width), bf16),
-            pltpu.VMEM((2 * steps, cache_dev, kv_width), bf16),
-            pltpu.VMEM((2, half, rows, q_width), kind),
-            pltpu.VMEM((2, half, rows, q_width + STATS), kind),
-            pltpu.SemaphoreType.DMA((2 * steps, 2)),
-        ],
-        compiler_params=limit(20),
-        cost_estimate=CHEAP,
-        name="attend",
-    )(me1, lengths, migrating, q_both, *q_got, cache_k, cache_v, draft_k, draft_v, bias)
-    *filled, done = put(every("inner"), [], parts[0])
+
+    def attend(queries, own):
+        drafted = [draft_k, draft_v, parents] if own else []
+        return pl.pallas_call(
+            functools.partial(attend_kernel, count=count, block=block, group=group, own=own),
+            out_shape=[pltpu.VMEM((2 * rows, q_width + STATS), bf16)] * quarter,
+            in_specs=[SMEM] * 3 + [VMEM] * (quarter + len(drafted)) + [HBM] * 2,
+            out_specs=[VMEM] * quarter,
+            scratch_shapes=[
+                pltpu.VMEM((2, cache_dev, kv_width), bf16),
+                pltpu.VMEM((2, cache_dev, kv_width), bf16),
+                pltpu.VMEM((2, quarter, rows, q_width), kind),
+                pltpu.VMEM((2, quarter, rows, q_width + STATS), kind),
+                pltpu.SemaphoreType.DMA((2, 2)),
+            ],
+            compiler_params=limit(16),
+            cost_estimate=CHEAP,
+            name="attend_own" if own else "attend_next",
+        )(me1, lengths, migrating, *queries, *drafted, cache_k, cache_v)
+
+    q_all = [q_both] + q_got
+    parts = attend(q_all[:quarter], True)
+    q_next, parts = lax.optimization_barrier((q_all[quarter:], parts))
+    later = attend(q_next, False)
+    *filled, done = put(every("inner"), [], later[0])
     done = migrate(far[: quarter // 2], done)
-    parts, done = lax.optimization_barrier((parts, done))
+    later, done = lax.optimization_barrier((later, done))
+    parts = parts + later
     parts_got = to_mates(parts)
     *filled, done = put(every("outer"), filled, done)
     done = migrate(far[quarter // 2 :], done)
+    *filled, done = put([], filled, done, fill=True)
     *filled, done = put(far[: quarter // 2], filled, done)
     done = migrate(every("same", 1), done)
     parts_got, done = lax.optimization_barrier((parts_got, done))
@@ -463,20 +489,28 @@
         name="reduce_other",
     )(parts[0], *parts_got)
     crossed = lax.ppermute(theirs_sum, "seq", across)
-    theirs_sum, done = lax.optimization_barrier((theirs_sum, done))
-    *filled, done = put([], filled, done, fill=True)
     last = far[quarter // 2 :] + every("same", 1)
     width = out_weight.shape[1] // ways
+    weight = pl.pallas_call(
+        weight_kernel,
+        out_shape=pltpu.VMEM((ways, q_width, width), bf16),
+        in_specs=[SMEM, ANY, HBM],
+        out_specs=VMEM,
+        scratch_shapes=[pltpu.SemaphoreType.DMA((ways,))],
+        compiler_params=limit(1),
+        cost_estimate=CHEAP,
+        name="weight",
+    )(tp1, theirs_sum, out_weight)
+    weight, crossed = lax.optimization_barrier((weight, crossed))
     *outs, own = pl.pallas_call(
         functools.partial(project_kernel, heads=heads, ways=ways),
         out_shape=[pltpu.VMEM((rows, width), bf16)] * (ways - 1) + [pltpu.VMEM((rows, width), f32)],
-        in_specs=[SMEM] + [VMEM] * (half + 2) + [HBM],
+        in_specs=[VMEM] * (half + 3),
         out_specs=[VMEM] * ways,
-        scratch_shapes=[pltpu.VMEM((ways, q_width, width), bf16), pltpu.SemaphoreType.DMA((ways,))],
-        compiler_params=limit(12),
+        compiler_params=limit(4),
         cost_estimate=CHEAP,
         name="project",
-    )(tp1, done, parts[0], *parts_got, crossed, out_weight)
+    )(done, parts[0], *parts_got, crossed, weight)
     out_got = [
         lax.ppermute(x, "tp", [(i, i ^ (d + 1)) for i in range(ways)]) for d, x in enumerate(outs)
     ]

time: 76 us -> 73.2 us (0.963)
  starting transfers between devices: 36.5 us -> 27.4 us
  waiting for transfers between devices: 11.8 us -> 15 us
  Pallas kernels: 26.5 us -> 29.5 us
    pallas_call x1 -> x3, Pallas kernels: 7.13 us -> 12.9 us  [the longest x2 9.35 us: attend(): pl.pallas_call(functools.partial(attend_kernel, count=count, block=block,...]
    ppermute x7, starting transfers between devices: 19.6 us -> 14.2 us  [migrate(): lax.ppermute(send, 'seq', [(i, i ^ deltas(i, *op, quarter)[0]) for i in r...]
    ppermute x1, starting transfers between devices: 3.8 us -> 0.07 us  [per_device(): crossed = lax.ppermute(theirs_sum, 'seq', across)]
    ppermute x7, waiting for transfers between devices: 1.37 us -> 4.36 us  [migrate(): lax.ppermute(send, 'seq', [(i, i ^ deltas(i, *op, quarter)[0]) for i in r...]
    pallas_call x1, Pallas kernels: 4.03 us -> 1.83 us  [per_device(): pl.pallas_call(functools.partial(project_kernel, heads=heads, ways=ways),...]
    ppermute x6, waiting for transfers between devices: 6.98 us -> 7.93 us  [to_mates(): lax.ppermute(parts[e], 'seq', beside[e])]
    ppermute x1, waiting for transfers between devices: 3.12 us -> 2.27 us  [per_device(): crossed = lax.ppermute(theirs_sum, 'seq', across)]
  transfers between devices with their start and end apart: 18 -> 18, of which waited for: 7 -> 5; matrix products, arithmetic and copies ran while one was open for 0% -> 0% of each run, Pallas kernels for 34% -> 40%
where the time goes in v4:
time: 73.2 us; the launch traced here: 72.7 us
  Pallas kernels  29.5 us (40%)
  starting transfers between devices  27.4 us (37%)
  waiting for transfers between devices  15 us (20%)
  between operations  0.82 us (1%)
    ppermute x7, starting transfers between devices, migrate(): lax.ppermute(send, 'seq', [(i, i ^ deltas(i, *op, quarter)[0]) for i in r...  14.2 us
    pallas_call x2, Pallas kernels, attend(): pl.pallas_call(functools.partial(attend_kernel, count=count, block=block,...  9.35 us
    ppermute x6, waiting for transfers between devices, to_mates(): lax.ppermute(parts[e], 'seq', beside[e])  7.93 us
    pallas_call x4, Pallas kernels, put(): pl.pallas_call(functools.partial(put_kernel, ops=which, block=block, quar...  7.73 us
    ppermute x6, starting transfers between devices, to_mates(): lax.ppermute(parts[e], 'seq', beside[e])  7.12 us
    ppermute x7, waiting for transfers between devices, migrate(): lax.ppermute(send, 'seq', [(i, i ^ deltas(i, *op, quarter)[0]) for i in r...  4.36 us
    ppermute x1, starting transfers between devices, per_device(): q_mirror = lax.ppermute(draft_q, 'seq', across)  4.1 us
    pallas_call x1, Pallas kernels, per_device(): pl.pallas_call(weight_kernel, out_shape=pltpu.VMEM((ways, q_width, width)...  3.53 us
  transfers between devices with their start and end apart: 18, of which 5 were waited for; matrix products, arithmetic and copies ran while one was open for 0% of the time, Pallas kernels for 40%

profile of v4, /device:TPU:0, one launch (start us, length us, event | category | flops | bytes accessed | tf_op | source)
XLA Modules:
  0.0 72.7 jit_solution(6814371408786398156)
XLA Ops:
  0.6 4.1 %collective-permute-start = (bf16[32,1024]{1,0:T(8,128)(2,1)}, bf16[32,1024]{1,0:T(8,128)(2,1)S(1)}, u32[]{:S(2)}, u32[]{:S(2)}) collective-permute-start(bf16[32,1024]{1,0:T(8,128)(2,1)} %param.10), channel_id=1, source_target_pairs={{0,16},{4,20},{8,24},{12,28},{16,0},{20,4},{24,8},{28,12},{1,17},{... | collective-permute-start | bytes 196616 | tf_op jit(solution)/shard_map/ppermute | solution.py:387
  4.7 2.5 %prep.1 = (bf16[528,256]{1,0:T(8,128)(2,1)S(1)}, bf16[528,256]{1,0:T(8,128)(2,1)S(1)}, bf16[528,256]{1,0:T(8,128)(2,1)S(1)}, bf16[528,256]{1,0:T(8,128)(2,1)S(1)...) custom-call(s32[1]{0:T(128)} %bitcast.me_ref, ...), custom_call_target="tpu_custom_call" | custom-call | flops 1 | bytes 1 | tf_op jit(solution)/shard_map/prep/pallas_call | solution.py:393
  7.3 1.6 %collective-permute-start.1 = (bf16[528,256]{1,0:T(8,128)(2,1)S(1)}, bf16[528,256]{1,0:T(8,128)(2,1)S(1)}, u32[]{:S(2)}, u32[]{:S(2)}) collective-permute-start(bf16[528,256]{1,0:T(8,128)(2,1)S(1)} %get-tuple-element.68), channel_id=1, source_target_pairs={{0,8},{4,12},{8,24},{12,28},{16,0},{20,4},{24,16},{28,20},{1,9},{5... | collective-permute-start | bytes 811016 | tf_op jit(solution)/shard_map/ppermute | solution.py:410
  8.9 1.3 %collective-permute-start.2 = (bf16[528,256]{1,0:T(8,128)(2,1)S(1)}, bf16[528,256]{1,0:T(8,128)(2,1)S(1)}, u32[]{:S(2)}, u32[]{:S(2)}) collective-permute-start(bf16[528,256]{1,0:T(8,128)(2,1)S(1)} %get-tuple-element.69), channel_id=1, source_target_pairs={{0,12},{4,8},{8,28},{12,24},{16,4},{20,0},{24,20},{28,16},{1,13},{... | collective-permute-start | bytes 811016 | tf_op jit(solution)/shard_map/ppermute | solution.py:410
  10.2 0.0 collective-permute-done
  10.2 0.6 collective-permute-start.3
  10.8 1.4 %collective-permute-start.7 = (bf16[64,1024]{1,0:T(8,128)(2,1)S(1)}, bf16[64,1024]{1,0:T(8,128)(2,1)S(1)}, u32[]{:S(2)}, u32[]{:S(2)}) collective-permute-start(bf16[64,1024]{1,0:T(8,128)(2,1)S(1)} %constant_dynamic-update-slice_fusion.rest_0_), channel_id=1, source_target_pairs={{0,12},{4,8},{8,4},{12,0},{16,28},{20,24},{24,20},{28,16},{1,13},{... | collective-permute-start | bytes 393224 | tf_op jit(solution)/shard_map/ppermute | solution.py:384
  12.2 1.6 %collective-permute-start.6 = (bf16[64,1024]{1,0:T(8,128)(2,1)S(1)}, bf16[64,1024]{1,0:T(8,128)(2,1)S(1)}, u32[]{:S(2)}, u32[]{:S(2)}) collective-permute-start(bf16[64,1024]{1,0:T(8,128)(2,1)S(1)} %constant_dynamic-update-slice_fusion.rest_0_), channel_id=1, source_target_pairs={{0,8},{4,12},{8,0},{12,4},{16,24},{20,28},{24,16},{28,20},{1,9},{5... | collective-permute-start | bytes 393224 | tf_op jit(solution)/shard_map/ppermute | solution.py:384
  13.8 1.5 %collective-permute-done.3.rest_1_ = bf16[64,1024]{1,0:T(8,128)(2,1)S(1)} collective-permute-done((bf16[64,1024]{1,0:T(8,128)(2,1)S(1)}, bf16[64,1024]{1,0:T(8,128)(2,1)S(1)}, u32[]{:S(2)}, u32[]{:S(2)}) %collective-permute-start.3) | collective-permute-done | bytes 131104 | tf_op jit(solution)/shard_map/ppermute | solution.py:384
  15.3 9.8 %collective-permute-start.4 = (bf16[528,256]{1,0:T(8,128)(2,1)S(1)}, bf16[528,256]{1,0:T(8,128)(2,1)S(1)}, u32[]{:S(2)}, u32[]{:S(2)}) collective-permute-start(bf16[528,256]{1,0:T(8,128)(2,1)S(1)} %get-tuple-element.73), channel_id=1, source_target_pairs={{0,16},{4,20},{8,0},{12,4},{16,24},{20,28},{24,8},{28,12},{1,17},{... | collective-permute-start | bytes 811016 | tf_op jit(solution)/shard_map/ppermute | solution.py:410
  25.1 5.1 %attend_own.1 = (bf16[64,1152]{1,0:T(8,128)(2,1)S(1)}, bf16[64,1152]{1,0:T(8,128)(2,1)S(1)}) custom-call(s32[1]{0:T(128)} %bitcast.me_ref, s32[4]{0:T(128)} %len_ref.5, s32[4]{0:T(128)} %mig_ref.15, bf16[64,1024]{1,0:T(8,128)(2,1)S(1)} %constant_dynamic-update-slice_fusion.rest_0_, bf16[64,1024]{1,0:T(8,128)(2,1)S(1)} %collective-permute-done.3.rest_1_, ...), custom_call_target="tpu_custom_call" | custom-call | flops 1 | bytes 1 | tf_op jit(solution)/shard_map/attend_own/pallas_call | solution.py:450
  30.2 0.0 collective-permute-done.7.rest_1_
  30.2 0.5 collective-permute-start.5
  30.7 0.0 collective-permute-done.6.rest_0_
  30.7 4.2 %attend_next.1 = (bf16[64,1152]{1,0:T(8,128)(2,1)S(1)}, bf16[64,1152]{1,0:T(8,128)(2,1)S(1)}) custom-call(s32[1]{0:T(128)} %bitcast.me_ref, s32[4]{0:T(128)} %len_ref.5, s32[4]{0:T(128)} %mig_ref.15, bf16[64,1024]{1,0:T(8,128)(2,1)S(1)} %collective-permute-done.6.rest_0_, bf16[64,1024]{1,0:T(8,128)(2,1)S(1)} %collective-permute-done.7.rest_1_, ...), custom_call_target="tpu_custom_call" | custom-call | flops 1 | bytes 1 | tf_op jit(solution)/shard_map/attend_next/pallas_call | solution.py:450
  34.9 0.0 collective-permute-done.1.rest_0_
  34.9 0.0 collective-permute-done.2.rest_1_
  34.9 1.5 %put.4 = (bf16[4,1024,256]{2,1,0:T(8,128)(2,1)}, bf16[4,1024,256]{2,1,0:T(8,128)(2,1)}, f32[8,128]{1,0:T(8,128)S(1)}) custom-call(s32[1]{0:T(128)} %bitcast.me_ref, s32[4]{0:T(128)} %mig_ref.15, bf16[64,1152]{1,0:T(8,128)(2,1)S(1)} %get-tuple-element.103.after_ref, bf16[528,256]{1,0:T(8,128)(2,1)S(1)} %collective-permute-done.1.rest_0_, ...), custom_call_target="tpu_custom_call" | custom-call | flops 1 | bytes 1 | tf_op jit(solution)/shard_map/put/pallas_call | solution.py:433
  36.5 0.1 collective-permute-start.8
  36.5 1.1 %collective-permute-start.11 = (bf16[64,1152]{1,0:T(8,128)(2,1)S(1)}, bf16[64,1152]{1,0:T(8,128)(2,1)S(1)}, u32[]{:S(2)}, u32[]{:S(2)}) collective-permute-start(bf16[64,1152]{1,0:T(8,128)(2,1)S(1)} %get-tuple-element.102), channel_id=1, source_target_pairs={{0,4},{4,0},{8,12},{12,8},{16,20},{20,16},{24,28},{28,24},{1,5},{5... | collective-permute-start | bytes 442376 | tf_op jit(solution)/shard_map/ppermute | solution.py:384
  37.7 2.0 %collective-permute-start.12 = (bf16[64,1152]{1,0:T(8,128)(2,1)S(1)}, bf16[64,1152]{1,0:T(8,128)(2,1)S(1)}, u32[]{:S(2)}, u32[]{:S(2)}) collective-permute-start(bf16[64,1152]{1,0:T(8,128)(2,1)S(1)} %get-tuple-element.103.after_ref), channel_id=1, source_target_pairs={{0,8},{4,12},{8,0},{12,4},{16,24},{20,28},{24,16},{28,20},{1,9},{5... | collective-permute-start | bytes 442376 | tf_op jit(solution)/shard_map/ppermute | solution.py:384
  39.7 0.0 collective-permute-done.4.rest_0_.rest_2_
  39.7 0.4 collective-permute-start.13
  40.1 4.3 %collective-permute-done.5.rest_1_.rest_3_ = bf16[528,256]{1,0:T(8,128)(2,1)S(1)} collective-permute-done((bf16[528,256]{1,0:T(8,128)(2,1)S(1)}, bf16[528,256]{1,0:T(8,128)(2,1)S(1)}, u32[]{:S(2)}, u32[]{:S(2)}) %collective-permute-start.5) | collective-permute-done | bytes 270368 | tf_op jit(solution)/shard_map/ppermute | solution.py:410
  44.5 1.5 %put.5 = (bf16[4,1024,256]{2,1,0:T(8,128)(2,1)}, bf16[4,1024,256]{2,1,0:T(8,128)(2,1)}, f32[8,128]{1,0:T(8,128)S(1)}) custom-call(s32[1]{0:T(128)} %bitcast.me_ref, s32[4]{0:T(128)} %mig_ref.15, f32[8,128]{1,0:T(8,128)S(1)} %get-tuple-element.88.after_ref, ...), custom_call_target="tpu_custom_call", output_to_operand_aliasing={{0}: (5, {}), {1}: (6, {})} | custom-call | flops 1 | bytes 1 | tf_op jit(solution)/shard_map/put/pallas_call | solution.py:433
  46.0 0.1 collective-permute-start.10
  46.1 3.3 %put.6 = (bf16[4,1024,256]{2,1,0:T(8,128)(2,1)}, bf16[4,1024,256]{2,1,0:T(8,128)(2,1)}, f32[8,128]{1,0:T(8,128)S(1)}) custom-call(s32[1]{0:T(128)} %bitcast.me_ref, s32[4]{0:T(128)} %mig_ref.15, f32[8,128]{1,0:T(8,128)S(1)} %get-tuple-element.92.after_ref, bf16[4,1024,256]{2,1,0:T(8,128)(2,1)} %rest_0_.1, ...), custom_call_target="tpu_custom_call", output_to_operand_aliasing={{0}: (5, {}), {1}: (6, {})} | custom-call | flops 1 | bytes 1 | tf_op jit(solution)/shard_map/put/pallas_call | solution.py:433
  49.3 0.0 collective-permute-done.8.rest_0_.rest_5_
  49.4 1.4 %put.7 = (bf16[4,1024,256]{2,1,0:T(8,128)(2,1)}, bf16[4,1024,256]{2,1,0:T(8,128)(2,1)}, f32[8,128]{1,0:T(8,128)S(1)}) custom-call(s32[1]{0:T(128)} %bitcast.me_ref, s32[4]{0:T(128)} %mig_ref.15, f32[8,128]{1,0:T(8,128)S(1)} %get-tuple-element.95.after_ref, ...), custom_call_target="tpu_custom_call", output_to_operand_aliasing={{0}: (4, {}), {1}: (5, {})} | custom-call | flops 1 | bytes 1 | tf_op jit(solution)/shard_map/put/pallas_call | solution.py:433
  50.8 0.9 %collective-permute-start.9 = (bf16[528,256]{1,0:T(8,128)(2,1)S(1)}, bf16[528,256]{1,0:T(8,128)(2,1)S(1)}, u32[]{:S(2)}, u32[]{:S(2)}) collective-permute-start(bf16[528,256]{1,0:T(8,128)(2,1)S(1)} %get-tuple-element.100), channel_id=1, source_target_pairs={{0,4},{4,0},{8,12},{12,8},{16,20},{20,16},{24,28},{28,24},{1,5},{5... | collective-permute-start | bytes 811016 | tf_op jit(solution)/shard_map/ppermute | solution.py:410
  51.7 0.0 collective-permute-done.11.refs_1_
  51.7 0.0 collective-permute-done.12.refs_2_
  51.7 6.4 %collective-permute-done.13.refs_3_ = bf16[64,1152]{1,0:T(8,128)(2,1)S(1)} collective-permute-done((bf16[64,1152]{1,0:T(8,128)(2,1)S(1)}, bf16[64,1152]{1,0:T(8,128)(2,1)S(1)}, u32[]{:S(2)}, u32[]{:S(2)}) %collective-permute-start.13) | collective-permute-done | bytes 147488 | tf_op jit(solution)/shard_map/ppermute | solution.py:384
  58.1 0.4 reduce_other.1.after_ref
  58.6 0.1 collective-permute-start.14
  58.6 3.5 %weight.1.refs_5_ = bf16[4,1024,1024]{2,1,0:T(8,128)(2,1)S(1)} custom-call(s32[1]{0:T(128)} %bitcast.1.tp_ref, bf16[32,1152]{1,0:T(8,128)(2,1)S(1)} %reduce_other.1.after_ref, bf16[1024,4096]{1,0:T(8,128)(2,1)} %w_ref.1), custom_call_target="tpu_custom_call" | custom-call | flops 1 | bytes 1 | tf_op jit(solution)/shard_map/weight/pallas_call | solution.py:494
  62.2 2.3 %collective-permute-done.14.refs_4_ = bf16[32,1152]{1,0:T(8,128)(2,1)S(1)} collective-permute-done((bf16[32,1152]{1,0:T(8,128)(2,1)S(1)}, bf16[32,1152]{1,0:T(8,128)(2,1)S(1)}, u32[]{:S(2)}, u32[]{:S(2)}) %collective-permute-start.14) | collective-permute-done | bytes 73760 | tf_op jit(solution)/shard_map/ppermute | solution.py:491
  64.5 1.8 %project.1 = (bf16[32,1024]{1,0:T(8,128)(2,1)S(1)}, bf16[32,1024]{1,0:T(8,128)(2,1)S(1)}, bf16[32,1024]{1,0:T(8,128)(2,1)S(1)}, f32[32,1024]{1,0:T(8,128)S(1)}) custom-call(f32[8,128]{1,0:T(8,128)S(1)} %get-tuple-element.106.done_ref, bf16[64,1152]{1,0:T(8,128)(2,1)S(1)} %get-tuple-element.107.refs_0_, bf16[64,1152]{1,0:T(8,128)(2,1)S(1)} %collective-permute-done.11.refs_1_, ...), custom_call_target="tpu_custom_call" | custom-call | flops 1 | bytes 1 | tf_op jit(solution)/shard_map/project/pallas_call | solution.py:505
  66.3 0.0 collective-permute-start.15
  66.3 1.6 %collective-permute-start.16 = (bf16[32,1024]{1,0:T(8,128)(2,1)S(1)}, bf16[32,1024]{1,0:T(8,128)(2,1)S(1)}, u32[]{:S(2)}, u32[]{:S(2)}) collective-permute-start(bf16[32,1024]{1,0:T(8,128)(2,1)S(1)} %get-tuple-element.121), channel_id=1, source_target_pairs={{0,2},{1,3},{2,0},{3,1},{4,6},{5,7},{6,4},{7,5},{8,10},{9,11},{10,... | collective-permute-start | bytes 196616 | tf_op jit(solution)/shard_map/ppermute | solution.py:515
  67.9 0.3 collective-permute-start.17
  68.1 0.0 collective-permute-done.10.rest_6_
  68.2 0.0 collective-permute-done.9.rest_4_
  68.2 3.4 %place.1 = (bf16[4,1024,256]{2,1,0:T(8,128)(2,1)}, bf16[4,1024,256]{2,1,0:T(8,128)(2,1)}, f32[8,128]{1,0:T(8,128)S(1)}) custom-call(s32[1]{0:T(128)} %bitcast.me_ref, s32[4]{0:T(128)} %mig_ref.15, s32[4]{0:T(128)} %len_ref.5, s32[4,8]{1,0:T(4,128)} %accepted_ref.3, ...), custom_call_target="tpu_custom_call", output_to_operand_aliasing={{0}: (12, {}), {1}: (13, {})} | custom-call | flops 1 | bytes 1 | tf_op jit(solution)/shard_map/place/pallas_call | solution.py:520
  71.6 0.0 collective-permute-done.15.rest_0_
  71.6 0.0 collective-permute-done.16.rest_1_
  71.6 0.4 collective-permute-done.17.rest_2_
  72.0 0.7 final.1
  (4 shorter events, 0.0 us)
Async XLA Ops:
  0.6 9.6 %collective-permute-start = (bf16[32,1024]{1,0:T(8,128)(2,1)}, bf16[32,1024]{1,0:T(8,128)(2,1)S(1)}, u32[]{:S(2)}, u32[]{:S(2)}) collective-permute-start(bf16[32,1024]{1,0:T(8,128)(2,1)} %param.10), channel_id=1, source_target_pairs={{0,16},{4,20},{8,24},{12,28},{16,0},{20,4},{24,8},{28,12},{1,17},{... | collective-permute-start | bytes 196616 | tf_op jit(solution)/shard_map/ppermute | solution.py:387
  4.7 5.4 %copy-start = (bf16[32,1024]{1,0:T(8,128)(2,1)S(1)}, bf16[32,1024]{1,0:T(8,128)(2,1)}, u32[]{:S(2)}) copy-start(bf16[32,1024]{1,0:T(8,128)(2,1)} %param.10) | copy-start | bytes 196612
  7.3 27.6 %collective-permute-start.1 = (bf16[528,256]{1,0:T(8,128)(2,1)S(1)}, bf16[528,256]{1,0:T(8,128)(2,1)S(1)}, u32[]{:S(2)}, u32[]{:S(2)}) collective-permute-start(bf16[528,256]{1,0:T(8,128)(2,1)S(1)} %get-tuple-element.68), channel_id=1, source_target_pairs={{0,8},{4,12},{8,24},{12,28},{16,0},{20,4},{24,16},{28,20},{1,9},{5... | collective-permute-start | bytes 811016 | tf_op jit(solution)/shard_map/ppermute | solution.py:410
  8.9 26.0 %collective-permute-start.2 = (bf16[528,256]{1,0:T(8,128)(2,1)S(1)}, bf16[528,256]{1,0:T(8,128)(2,1)S(1)}, u32[]{:S(2)}, u32[]{:S(2)}) collective-permute-start(bf16[528,256]{1,0:T(8,128)(2,1)S(1)} %get-tuple-element.69), channel_id=1, source_target_pairs={{0,12},{4,8},{8,28},{12,24},{16,4},{20,0},{24,20},{28,16},{1,13},{... | collective-permute-start | bytes 811016 | tf_op jit(solution)/shard_map/ppermute | solution.py:410
  10.2 5.1 %collective-permute-start.3 = (bf16[64,1024]{1,0:T(8,128)(2,1)S(1)}, bf16[64,1024]{1,0:T(8,128)(2,1)S(1)}, u32[]{:S(2)}, u32[]{:S(2)}) collective-permute-start(bf16[64,1024]{1,0:T(8,128)(2,1)S(1)} %constant_dynamic-update-slice_fusion.rest_0_), channel_id=1, source_target_pairs={{0,4},{4,0},{8,12},{12,8},{16,20},{20,16},{24,28},{28,24},{1,5},{5... | collective-permute-start | bytes 393224 | tf_op jit(solution)/shard_map/ppermute | solution.py:384
  10.8 19.4 %collective-permute-start.7 = (bf16[64,1024]{1,0:T(8,128)(2,1)S(1)}, bf16[64,1024]{1,0:T(8,128)(2,1)S(1)}, u32[]{:S(2)}, u32[]{:S(2)}) collective-permute-start(bf16[64,1024]{1,0:T(8,128)(2,1)S(1)} %constant_dynamic-update-slice_fusion.rest_0_), channel_id=1, source_target_pairs={{0,12},{4,8},{8,4},{12,0},{16,28},{20,24},{24,20},{28,16},{1,13},{... | collective-permute-start | bytes 393224 | tf_op jit(solution)/shard_map/ppermute | solution.py:384
  12.2 18.5 %collective-permute-start.6 = (bf16[64,1024]{1,0:T(8,128)(2,1)S(1)}, bf16[64,1024]{1,0:T(8,128)(2,1)S(1)}, u32[]{:S(2)}, u32[]{:S(2)}) collective-permute-start(bf16[64,1024]{1,0:T(8,128)(2,1)S(1)} %constant_dynamic-update-slice_fusion.rest_0_), channel_id=1, source_target_pairs={{0,8},{4,12},{8,0},{12,4},{16,24},{20,28},{24,16},{28,20},{1,9},{5... | collective-permute-start | bytes 393224 | tf_op jit(solution)/shard_map/ppermute | solution.py:384
  15.3 24.4 %collective-permute-start.4 = (bf16[528,256]{1,0:T(8,128)(2,1)S(1)}, bf16[528,256]{1,0:T(8,128)(2,1)S(1)}, u32[]{:S(2)}, u32[]{:S(2)}) collective-permute-start(bf16[528,256]{1,0:T(8,128)(2,1)S(1)} %get-tuple-element.73), channel_id=1, source_target_pairs={{0,16},{4,20},{8,0},{12,4},{16,24},{20,28},{24,8},{28,12},{1,17},{... | collective-permute-start | bytes 811016 | tf_op jit(solution)/shard_map/ppermute | solution.py:410
  30.2 14.3 %collective-permute-start.5 = (bf16[528,256]{1,0:T(8,128)(2,1)S(1)}, bf16[528,256]{1,0:T(8,128)(2,1)S(1)}, u32[]{:S(2)}, u32[]{:S(2)}) collective-permute-start(bf16[528,256]{1,0:T(8,128)(2,1)S(1)} %get-tuple-element.74), channel_id=1, source_target_pairs={{0,20},{4,16},{8,4},{12,0},{16,28},{20,24},{24,12},{28,8},{1,21},{... | collective-permute-start | bytes 811016 | tf_op jit(solution)/shard_map/ppermute | solution.py:410
  36.5 12.9 %collective-permute-start.8 = (bf16[528,256]{1,0:T(8,128)(2,1)S(1)}, bf16[528,256]{1,0:T(8,128)(2,1)S(1)}, u32[]{:S(2)}, u32[]{:S(2)}) collective-permute-start(bf16[528,256]{1,0:T(8,128)(2,1)S(1)} %get-tuple-element.96), channel_id=1, source_target_pairs={{0,24},{4,28},{8,16},{12,20},{16,8},{20,12},{24,0},{28,4},{1,25},{... | collective-permute-start | bytes 811016 | tf_op jit(solution)/shard_map/ppermute | solution.py:410
  36.5 15.2 %collective-permute-start.11 = (bf16[64,1152]{1,0:T(8,128)(2,1)S(1)}, bf16[64,1152]{1,0:T(8,128)(2,1)S(1)}, u32[]{:S(2)}, u32[]{:S(2)}) collective-permute-start(bf16[64,1152]{1,0:T(8,128)(2,1)S(1)} %get-tuple-element.102), channel_id=1, source_target_pairs={{0,4},{4,0},{8,12},{12,8},{16,20},{20,16},{24,28},{28,24},{1,5},{5... | collective-permute-start | bytes 442376 | tf_op jit(solution)/shard_map/ppermute | solution.py:384
  37.7 14.0 %collective-permute-start.12 = (bf16[64,1152]{1,0:T(8,128)(2,1)S(1)}, bf16[64,1152]{1,0:T(8,128)(2,1)S(1)}, u32[]{:S(2)}, u32[]{:S(2)}) collective-permute-start(bf16[64,1152]{1,0:T(8,128)(2,1)S(1)} %get-tuple-element.103.after_ref), channel_id=1, source_target_pairs={{0,8},{4,12},{8,0},{12,4},{16,24},{20,28},{24,16},{28,20},{1,9},{5... | collective-permute-start | bytes 442376 | tf_op jit(solution)/shard_map/ppermute | solution.py:384
  39.7 18.4 %collective-permute-start.13 = (bf16[64,1152]{1,0:T(8,128)(2,1)S(1)}, bf16[64,1152]{1,0:T(8,128)(2,1)S(1)}, u32[]{:S(2)}, u32[]{:S(2)}) collective-permute-start(bf16[64,1152]{1,0:T(8,128)(2,1)S(1)} %get-tuple-element.104), channel_id=1, source_target_pairs={{0,12},{4,8},{8,4},{12,0},{16,28},{20,24},{24,20},{28,16},{1,13},{... | collective-permute-start | bytes 442376 | tf_op jit(solution)/shard_map/ppermute | solution.py:384
  46.0 22.2 %collective-permute-start.10 = (bf16[528,256]{1,0:T(8,128)(2,1)S(1)}, bf16[528,256]{1,0:T(8,128)(2,1)S(1)}, u32[]{:S(2)}, u32[]{:S(2)}) collective-permute-start(bf16[528,256]{1,0:T(8,128)(2,1)S(1)} %get-tuple-element.101), channel_id=1, source_target_pairs={{0,28},{4,24},{8,20},{12,16},{16,12},{20,8},{24,4},{28,0},{1,29},{... | collective-permute-start | bytes 811016 | tf_op jit(solution)/shard_map/ppermute | solution.py:410
  50.8 17.4 %collective-permute-start.9 = (bf16[528,256]{1,0:T(8,128)(2,1)S(1)}, bf16[528,256]{1,0:T(8,128)(2,1)S(1)}, u32[]{:S(2)}, u32[]{:S(2)}) collective-permute-start(bf16[528,256]{1,0:T(8,128)(2,1)S(1)} %get-tuple-element.100), channel_id=1, source_target_pairs={{0,4},{4,0},{8,12},{12,8},{16,20},{20,16},{24,28},{28,24},{1,5},{5... | collective-permute-start | bytes 811016 | tf_op jit(solution)/shard_map/ppermute | solution.py:410
  58.6 5.9 %collective-permute-start.14 = (bf16[32,1152]{1,0:T(8,128)(2,1)S(1)}, bf16[32,1152]{1,0:T(8,128)(2,1)S(1)}, u32[]{:S(2)}, u32[]{:S(2)}) collective-permute-start(bf16[32,1152]{1,0:T(8,128)(2,1)S(1)} %reduce_other.1.after_ref), channel_id=1, source_target_pairs={{0,16},{4,20},{8,24},{12,28},{16,0},{20,4},{24,8},{28,12},{1,17},{... | collective-permute-start | bytes 221192 | tf_op jit(solution)/shard_map/ppermute | solution.py:491
  66.3 5.3 %collective-permute-start.15 = (bf16[32,1024]{1,0:T(8,128)(2,1)S(1)}, bf16[32,1024]{1,0:T(8,128)(2,1)S(1)}, u32[]{:S(2)}, u32[]{:S(2)}) collective-permute-start(bf16[32,1024]{1,0:T(8,128)(2,1)S(1)} %get-tuple-element.120), channel_id=1, source_target_pairs={{0,1},{1,0},{2,3},{3,2},{4,5},{5,4},{6,7},{7,6},{8,9},{9,8},{10,11... | collective-permute-start | bytes 196616 | tf_op jit(solution)/shard_map/ppermute | solution.py:515
  66.3 5.3 %collective-permute-start.16 = (bf16[32,1024]{1,0:T(8,128)(2,1)S(1)}, bf16[32,1024]{1,0:T(8,128)(2,1)S(1)}, u32[]{:S(2)}, u32[]{:S(2)}) collective-permute-start(bf16[32,1024]{1,0:T(8,128)(2,1)S(1)} %get-tuple-element.121), channel_id=1, source_target_pairs={{0,2},{1,3},{2,0},{3,1},{4,6},{5,7},{6,4},{7,5},{8,10},{9,11},{10,... | collective-permute-start | bytes 196616 | tf_op jit(solution)/shard_map/ppermute | solution.py:515
  67.9 4.1 %collective-permute-start.17 = (bf16[32,1024]{1,0:T(8,128)(2,1)S(1)}, bf16[32,1024]{1,0:T(8,128)(2,1)S(1)}, u32[]{:S(2)}, u32[]{:S(2)}) collective-permute-start(bf16[32,1024]{1,0:T(8,128)(2,1)S(1)} %get-tuple-element.122), channel_id=1, source_target_pairs={{0,3},{1,2},{2,1},{3,0},{4,7},{5,6},{6,5},{7,4},{8,11},{9,10},{10,... | collective-permute-start | bytes 196616 | tf_op jit(solution)/shard_map/ppermute | solution.py:515

commit v5 on v4

--- a/solution.py
+++ b/solution.py
@@ -311,6 +311,14 @@
     copies = block_copies(me, pair, (nk_ref, nv_ref), *zip(*ends), block, sems, back=True)
     for copy in copies:
         copy.start()
+    per_request = count // requests
+    parts = [acc_ref[...].astype(f32)] + [got[4 * block :].astype(f32) for got in gots]
+    helds = []
+    for r in range(requests):
+        held = jnp.where(me // per_request == r, parts[0], 0.0)
+        for owner, rows in zip(sources, parts[1:]):
+            held = held + jnp.where(owner // per_request == r, rows, 0.0)
+        helds.append(held)
     for copy in copies:
         copy.wait()
     span = wins_ref.shape[2]
@@ -324,13 +332,10 @@
             stores.append(pltpu.make_async_copy(b, a, win_sem.at[1, c, r]))
     for copy in loads:
         copy.start()
-    per_request = count // requests
     for copy in loads:
         copy.wait()
     for r in range(requests):
-        held = jnp.where(me // per_request == r, acc_ref[...].astype(f32), 0.0)
-        for owner, got in zip(sources, gots):
-            held = held + jnp.where(owner // per_request == r, got[4 * block :].astype(f32), 0.0)
+        held = helds[r]
         row = lax.broadcasted_iota(i32, (span, 1), 0) + low[r]
         for c in range(2):
             window = wins_ref[c, r].astype(f32)
@@ -338,8 +343,7 @@
                 hit = (row == first[r] + i) & (accepted_ref[r, i] >= 0)
                 window = jnp.where(hit, held[c * accept + i : c * accept + i + 1], window)
             wins_ref[c, r] = window.astype(bf16)
-    for copy in stores:
-        copy.start()
+            stores[c * requests + r].start()
     for copy in stores:
         copy.wait()
 

time: 73.2 us -> 73.2 us (level)
  no operation moved by 1% of the time
where the time goes in v5:
time: 73.2 us; the launch traced here: 72.7 us
  Pallas kernels  29.5 us (40%)
  starting transfers between devices  27.4 us (37%)
  waiting for transfers between devices  15 us (20%)
  between operations  0.82 us (1%)
    ppermute x7, starting transfers between devices, migrate(): lax.ppermute(send, 'seq', [(i, i ^ deltas(i, *op, quarter)[0]) for i in r...  14.2 us
    pallas_call x2, Pallas kernels, attend(): pl.pallas_call(functools.partial(attend_kernel, count=count, block=block,...  9.35 us
    ppermute x6, waiting for transfers between devices, to_mates(): lax.ppermute(parts[e], 'seq', beside[e])  7.93 us
    pallas_call x4, Pallas kernels, put(): pl.pallas_call(functools.partial(put_kernel, ops=which, block=block, quar...  7.73 us
    ppermute x6, starting transfers between devices, to_mates(): lax.ppermute(parts[e], 'seq', beside[e])  7.12 us
    ppermute x7, waiting for transfers between devices, migrate(): lax.ppermute(send, 'seq', [(i, i ^ deltas(i, *op, quarter)[0]) for i in r...  4.36 us
    ppermute x1, starting transfers between devices, per_device(): q_mirror = lax.ppermute(draft_q, 'seq', across)  4.1 us
    pallas_call x1, Pallas kernels, per_device(): pl.pallas_call(weight_kernel, out_shape=pltpu.VMEM((ways, q_width, width)...  3.53 us
  transfers between devices with their start and end apart: 18, of which 5 were waited for; matrix products, arithmetic and copies ran while one was open for 0% of the time, Pallas kernels for 40%

profile of v5, /device:TPU:0, one launch (start us, length us, event | category | flops | bytes accessed | tf_op | source)
XLA Modules:
  0.0 72.7 jit_solution(2162749851400199536)
XLA Ops:
  0.6 4.1 %collective-permute-start = (bf16[32,1024]{1,0:T(8,128)(2,1)}, bf16[32,1024]{1,0:T(8,128)(2,1)S(1)}, u32[]{:S(2)}, u32[]{:S(2)}) collective-permute-start(bf16[32,1024]{1,0:T(8,128)(2,1)} %param.10), channel_id=1, source_target_pairs={{0,16},{4,20},{8,24},{12,28},{16,0},{20,4},{24,8},{28,12},{1,17},{... | collective-permute-start | bytes 196616 | tf_op jit(solution)/shard_map/ppermute | solution.py:391
  4.7 2.5 %prep.1 = (bf16[528,256]{1,0:T(8,128)(2,1)S(1)}, bf16[528,256]{1,0:T(8,128)(2,1)S(1)}, bf16[528,256]{1,0:T(8,128)(2,1)S(1)}, bf16[528,256]{1,0:T(8,128)(2,1)S(1)...) custom-call(s32[1]{0:T(128)} %bitcast.me_ref, ...), custom_call_target="tpu_custom_call" | custom-call | flops 1 | bytes 1 | tf_op jit(solution)/shard_map/prep/pallas_call | solution.py:397
  7.3 1.6 %collective-permute-start.1 = (bf16[528,256]{1,0:T(8,128)(2,1)S(1)}, bf16[528,256]{1,0:T(8,128)(2,1)S(1)}, u32[]{:S(2)}, u32[]{:S(2)}) collective-permute-start(bf16[528,256]{1,0:T(8,128)(2,1)S(1)} %get-tuple-element.68), channel_id=1, source_target_pairs={{0,8},{4,12},{8,24},{12,28},{16,0},{20,4},{24,16},{28,20},{1,9},{5... | collective-permute-start | bytes 811016 | tf_op jit(solution)/shard_map/ppermute | solution.py:414
  8.9 1.3 %collective-permute-start.2 = (bf16[528,256]{1,0:T(8,128)(2,1)S(1)}, bf16[528,256]{1,0:T(8,128)(2,1)S(1)}, u32[]{:S(2)}, u32[]{:S(2)}) collective-permute-start(bf16[528,256]{1,0:T(8,128)(2,1)S(1)} %get-tuple-element.69), channel_id=1, source_target_pairs={{0,12},{4,8},{8,28},{12,24},{16,4},{20,0},{24,20},{28,16},{1,13},{... | collective-permute-start | bytes 811016 | tf_op jit(solution)/shard_map/ppermute | solution.py:414
  10.2 0.0 collective-permute-done
  10.2 0.6 collective-permute-start.3
  10.8 1.4 %collective-permute-start.7 = (bf16[64,1024]{1,0:T(8,128)(2,1)S(1)}, bf16[64,1024]{1,0:T(8,128)(2,1)S(1)}, u32[]{:S(2)}, u32[]{:S(2)}) collective-permute-start(bf16[64,1024]{1,0:T(8,128)(2,1)S(1)} %constant_dynamic-update-slice_fusion.rest_0_), channel_id=1, source_target_pairs={{0,12},{4,8},{8,4},{12,0},{16,28},{20,24},{24,20},{28,16},{1,13},{... | collective-permute-start | bytes 393224 | tf_op jit(solution)/shard_map/ppermute | solution.py:388
  12.2 1.6 %collective-permute-start.6 = (bf16[64,1024]{1,0:T(8,128)(2,1)S(1)}, bf16[64,1024]{1,0:T(8,128)(2,1)S(1)}, u32[]{:S(2)}, u32[]{:S(2)}) collective-permute-start(bf16[64,1024]{1,0:T(8,128)(2,1)S(1)} %constant_dynamic-update-slice_fusion.rest_0_), channel_id=1, source_target_pairs={{0,8},{4,12},{8,0},{12,4},{16,24},{20,28},{24,16},{28,20},{1,9},{5... | collective-permute-start | bytes 393224 | tf_op jit(solution)/shard_map/ppermute | solution.py:388
  13.8 1.5 %collective-permute-done.3.rest_1_ = bf16[64,1024]{1,0:T(8,128)(2,1)S(1)} collective-permute-done((bf16[64,1024]{1,0:T(8,128)(2,1)S(1)}, bf16[64,1024]{1,0:T(8,128)(2,1)S(1)}, u32[]{:S(2)}, u32[]{:S(2)}) %collective-permute-start.3) | collective-permute-done | bytes 131104 | tf_op jit(solution)/shard_map/ppermute | solution.py:388
  15.3 9.8 %collective-permute-start.4 = (bf16[528,256]{1,0:T(8,128)(2,1)S(1)}, bf16[528,256]{1,0:T(8,128)(2,1)S(1)}, u32[]{:S(2)}, u32[]{:S(2)}) collective-permute-start(bf16[528,256]{1,0:T(8,128)(2,1)S(1)} %get-tuple-element.73), channel_id=1, source_target_pairs={{0,16},{4,20},{8,0},{12,4},{16,24},{20,28},{24,8},{28,12},{1,17},{... | collective-permute-start | bytes 811016 | tf_op jit(solution)/shard_map/ppermute | solution.py:414
  25.1 5.1 %attend_own.1 = (bf16[64,1152]{1,0:T(8,128)(2,1)S(1)}, bf16[64,1152]{1,0:T(8,128)(2,1)S(1)}) custom-call(s32[1]{0:T(128)} %bitcast.me_ref, s32[4]{0:T(128)} %len_ref.5, s32[4]{0:T(128)} %mig_ref.15, bf16[64,1024]{1,0:T(8,128)(2,1)S(1)} %constant_dynamic-update-slice_fusion.rest_0_, bf16[64,1024]{1,0:T(8,128)(2,1)S(1)} %collective-permute-done.3.rest_1_, ...), custom_call_target="tpu_custom_call" | custom-call | flops 1 | bytes 1 | tf_op jit(solution)/shard_map/attend_own/pallas_call | solution.py:454
  30.2 0.0 collective-permute-done.7.rest_1_
  30.2 0.5 collective-permute-start.5
  30.7 0.0 collective-permute-done.6.rest_0_
  30.7 4.2 %attend_next.1 = (bf16[64,1152]{1,0:T(8,128)(2,1)S(1)}, bf16[64,1152]{1,0:T(8,128)(2,1)S(1)}) custom-call(s32[1]{0:T(128)} %bitcast.me_ref, s32[4]{0:T(128)} %len_ref.5, s32[4]{0:T(128)} %mig_ref.15, bf16[64,1024]{1,0:T(8,128)(2,1)S(1)} %collective-permute-done.6.rest_0_, bf16[64,1024]{1,0:T(8,128)(2,1)S(1)} %collective-permute-done.7.rest_1_, ...), custom_call_target="tpu_custom_call" | custom-call | flops 1 | bytes 1 | tf_op jit(solution)/shard_map/attend_next/pallas_call | solution.py:454
  34.9 0.0 collective-permute-done.1.rest_0_
  34.9 0.0 collective-permute-done.2.rest_1_
  34.9 1.5 %put.4 = (bf16[4,1024,256]{2,1,0:T(8,128)(2,1)}, bf16[4,1024,256]{2,1,0:T(8,128)(2,1)}, f32[8,128]{1,0:T(8,128)S(1)}) custom-call(s32[1]{0:T(128)} %bitcast.me_ref, s32[4]{0:T(128)} %mig_ref.15, bf16[64,1152]{1,0:T(8,128)(2,1)S(1)} %get-tuple-element.103.after_ref, bf16[528,256]{1,0:T(8,128)(2,1)S(1)} %collective-permute-done.1.rest_0_, ...), custom_call_target="tpu_custom_call" | custom-call | flops 1 | bytes 1 | tf_op jit(solution)/shard_map/put/pallas_call | solution.py:437
  36.5 0.1 collective-permute-start.8
  36.5 1.1 %collective-permute-start.11 = (bf16[64,1152]{1,0:T(8,128)(2,1)S(1)}, bf16[64,1152]{1,0:T(8,128)(2,1)S(1)}, u32[]{:S(2)}, u32[]{:S(2)}) collective-permute-start(bf16[64,1152]{1,0:T(8,128)(2,1)S(1)} %get-tuple-element.102), channel_id=1, source_target_pairs={{0,4},{4,0},{8,12},{12,8},{16,20},{20,16},{24,28},{28,24},{1,5},{5... | collective-permute-start | bytes 442376 | tf_op jit(solution)/shard_map/ppermute | solution.py:388
  37.7 2.0 %collective-permute-start.12 = (bf16[64,1152]{1,0:T(8,128)(2,1)S(1)}, bf16[64,1152]{1,0:T(8,128)(2,1)S(1)}, u32[]{:S(2)}, u32[]{:S(2)}) collective-permute-start(bf16[64,1152]{1,0:T(8,128)(2,1)S(1)} %get-tuple-element.103.after_ref), channel_id=1, source_target_pairs={{0,8},{4,12},{8,0},{12,4},{16,24},{20,28},{24,16},{28,20},{1,9},{5... | collective-permute-start | bytes 442376 | tf_op jit(solution)/shard_map/ppermute | solution.py:388
  39.7 0.0 collective-permute-done.4.rest_0_.rest_2_
  39.7 0.4 collective-permute-start.13
  40.1 4.3 %collective-permute-done.5.rest_1_.rest_3_ = bf16[528,256]{1,0:T(8,128)(2,1)S(1)} collective-permute-done((bf16[528,256]{1,0:T(8,128)(2,1)S(1)}, bf16[528,256]{1,0:T(8,128)(2,1)S(1)}, u32[]{:S(2)}, u32[]{:S(2)}) %collective-permute-start.5) | collective-permute-done | bytes 270368 | tf_op jit(solution)/shard_map/ppermute | solution.py:414
  44.5 1.5 %put.5 = (bf16[4,1024,256]{2,1,0:T(8,128)(2,1)}, bf16[4,1024,256]{2,1,0:T(8,128)(2,1)}, f32[8,128]{1,0:T(8,128)S(1)}) custom-call(s32[1]{0:T(128)} %bitcast.me_ref, s32[4]{0:T(128)} %mig_ref.15, f32[8,128]{1,0:T(8,128)S(1)} %get-tuple-element.88.after_ref, ...), custom_call_target="tpu_custom_call", output_to_operand_aliasing={{0}: (5, {}), {1}: (6, {})} | custom-call | flops 1 | bytes 1 | tf_op jit(solution)/shard_map/put/pallas_call | solution.py:437
  46.0 0.1 collective-permute-start.10
  46.1 3.3 %put.6 = (bf16[4,1024,256]{2,1,0:T(8,128)(2,1)}, bf16[4,1024,256]{2,1,0:T(8,128)(2,1)}, f32[8,128]{1,0:T(8,128)S(1)}) custom-call(s32[1]{0:T(128)} %bitcast.me_ref, s32[4]{0:T(128)} %mig_ref.15, f32[8,128]{1,0:T(8,128)S(1)} %get-tuple-element.92.after_ref, bf16[4,1024,256]{2,1,0:T(8,128)(2,1)} %rest_0_.1, ...), custom_call_target="tpu_custom_call", output_to_operand_aliasing={{0}: (5, {}), {1}: (6, {})} | custom-call | flops 1 | bytes 1 | tf_op jit(solution)/shard_map/put/pallas_call | solution.py:437
  49.3 0.0 collective-permute-done.8.rest_0_.rest_5_
  49.4 1.4 %put.7 = (bf16[4,1024,256]{2,1,0:T(8,128)(2,1)}, bf16[4,1024,256]{2,1,0:T(8,128)(2,1)}, f32[8,128]{1,0:T(8,128)S(1)}) custom-call(s32[1]{0:T(128)} %bitcast.me_ref, s32[4]{0:T(128)} %mig_ref.15, f32[8,128]{1,0:T(8,128)S(1)} %get-tuple-element.95.after_ref, ...), custom_call_target="tpu_custom_call", output_to_operand_aliasing={{0}: (4, {}), {1}: (5, {})} | custom-call | flops 1 | bytes 1 | tf_op jit(solution)/shard_map/put/pallas_call | solution.py:437
  50.8 0.9 %collective-permute-start.9 = (bf16[528,256]{1,0:T(8,128)(2,1)S(1)}, bf16[528,256]{1,0:T(8,128)(2,1)S(1)}, u32[]{:S(2)}, u32[]{:S(2)}) collective-permute-start(bf16[528,256]{1,0:T(8,128)(2,1)S(1)} %get-tuple-element.100), channel_id=1, source_target_pairs={{0,4},{4,0},{8,12},{12,8},{16,20},{20,16},{24,28},{28,24},{1,5},{5... | collective-permute-start | bytes 811016 | tf_op jit(solution)/shard_map/ppermute | solution.py:414
  51.7 0.0 collective-permute-done.11.refs_1_
  51.7 0.0 collective-permute-done.12.refs_2_
  51.7 6.4 %collective-permute-done.13.refs_3_ = bf16[64,1152]{1,0:T(8,128)(2,1)S(1)} collective-permute-done((bf16[64,1152]{1,0:T(8,128)(2,1)S(1)}, bf16[64,1152]{1,0:T(8,128)(2,1)S(1)}, u32[]{:S(2)}, u32[]{:S(2)}) %collective-permute-start.13) | collective-permute-done | bytes 147488 | tf_op jit(solution)/shard_map/ppermute | solution.py:388
  58.1 0.4 reduce_other.1.after_ref
  58.6 0.1 collective-permute-start.14
  58.6 3.5 %weight.1.refs_5_ = bf16[4,1024,1024]{2,1,0:T(8,128)(2,1)S(1)} custom-call(s32[1]{0:T(128)} %bitcast.1.tp_ref, bf16[32,1152]{1,0:T(8,128)(2,1)S(1)} %reduce_other.1.after_ref, bf16[1024,4096]{1,0:T(8,128)(2,1)} %w_ref.1), custom_call_target="tpu_custom_call" | custom-call | flops 1 | bytes 1 | tf_op jit(solution)/shard_map/weight/pallas_call | solution.py:498
  62.2 2.3 %collective-permute-done.14.refs_4_ = bf16[32,1152]{1,0:T(8,128)(2,1)S(1)} collective-permute-done((bf16[32,1152]{1,0:T(8,128)(2,1)S(1)}, bf16[32,1152]{1,0:T(8,128)(2,1)S(1)}, u32[]{:S(2)}, u32[]{:S(2)}) %collective-permute-start.14) | collective-permute-done | bytes 73760 | tf_op jit(solution)/shard_map/ppermute | solution.py:495
  64.5 1.8 %project.1 = (bf16[32,1024]{1,0:T(8,128)(2,1)S(1)}, bf16[32,1024]{1,0:T(8,128)(2,1)S(1)}, bf16[32,1024]{1,0:T(8,128)(2,1)S(1)}, f32[32,1024]{1,0:T(8,128)S(1)}) custom-call(f32[8,128]{1,0:T(8,128)S(1)} %get-tuple-element.106.done_ref, bf16[64,1152]{1,0:T(8,128)(2,1)S(1)} %get-tuple-element.107.refs_0_, bf16[64,1152]{1,0:T(8,128)(2,1)S(1)} %collective-permute-done.11.refs_1_, ...), custom_call_target="tpu_custom_call" | custom-call | flops 1 | bytes 1 | tf_op jit(solution)/shard_map/project/pallas_call | solution.py:509
  66.3 0.0 collective-permute-start.15
  66.3 1.6 %collective-permute-start.16 = (bf16[32,1024]{1,0:T(8,128)(2,1)S(1)}, bf16[32,1024]{1,0:T(8,128)(2,1)S(1)}, u32[]{:S(2)}, u32[]{:S(2)}) collective-permute-start(bf16[32,1024]{1,0:T(8,128)(2,1)S(1)} %get-tuple-element.121), channel_id=1, source_target_pairs={{0,2},{1,3},{2,0},{3,1},{4,6},{5,7},{6,4},{7,5},{8,10},{9,11},{10,... | collective-permute-start | bytes 196616 | tf_op jit(solution)/shard_map/ppermute | solution.py:519
  67.9 0.3 collective-permute-start.17
  68.1 0.0 collective-permute-done.10.rest_6_
  68.2 0.0 collective-permute-done.9.rest_4_
  68.2 3.4 %place.1 = (bf16[4,1024,256]{2,1,0:T(8,128)(2,1)}, bf16[4,1024,256]{2,1,0:T(8,128)(2,1)}, f32[8,128]{1,0:T(8,128)S(1)}) custom-call(s32[1]{0:T(128)} %bitcast.me_ref, s32[4]{0:T(128)} %mig_ref.15, s32[4]{0:T(128)} %len_ref.5, s32[4,8]{1,0:T(4,128)} %accepted_ref.3, ...), custom_call_target="tpu_custom_call", output_to_operand_aliasing={{0}: (12, {}), {1}: (13, {})} | custom-call | flops 1 | bytes 1 | tf_op jit(solution)/shard_map/place/pallas_call | solution.py:524
  71.5 0.0 collective-permute-done.15.rest_0_
  71.6 0.0 collective-permute-done.16.rest_1_
  71.6 0.5 collective-permute-done.17.rest_2_
  72.0 0.7 final.1
  (4 shorter events, 0.0 us)
Async XLA Ops:
  0.6 9.6 %collective-permute-start = (bf16[32,1024]{1,0:T(8,128)(2,1)}, bf16[32,1024]{1,0:T(8,128)(2,1)S(1)}, u32[]{:S(2)}, u32[]{:S(2)}) collective-permute-start(bf16[32,1024]{1,0:T(8,128)(2,1)} %param.10), channel_id=1, source_target_pairs={{0,16},{4,20},{8,24},{12,28},{16,0},{20,4},{24,8},{28,12},{1,17},{... | collective-permute-start | bytes 196616 | tf_op jit(solution)/shard_map/ppermute | solution.py:391
  4.7 5.4 %copy-start = (bf16[32,1024]{1,0:T(8,128)(2,1)S(1)}, bf16[32,1024]{1,0:T(8,128)(2,1)}, u32[]{:S(2)}) copy-start(bf16[32,1024]{1,0:T(8,128)(2,1)} %param.10) | copy-start | bytes 196612
  7.3 27.6 %collective-permute-start.1 = (bf16[528,256]{1,0:T(8,128)(2,1)S(1)}, bf16[528,256]{1,0:T(8,128)(2,1)S(1)}, u32[]{:S(2)}, u32[]{:S(2)}) collective-permute-start(bf16[528,256]{1,0:T(8,128)(2,1)S(1)} %get-tuple-element.68), channel_id=1, source_target_pairs={{0,8},{4,12},{8,24},{12,28},{16,0},{20,4},{24,16},{28,20},{1,9},{5... | collective-permute-start | bytes 811016 | tf_op jit(solution)/shard_map/ppermute | solution.py:414
  8.9 26.0 %collective-permute-start.2 = (bf16[528,256]{1,0:T(8,128)(2,1)S(1)}, bf16[528,256]{1,0:T(8,128)(2,1)S(1)}, u32[]{:S(2)}, u32[]{:S(2)}) collective-permute-start(bf16[528,256]{1,0:T(8,128)(2,1)S(1)} %get-tuple-element.69), channel_id=1, source_target_pairs={{0,12},{4,8},{8,28},{12,24},{16,4},{20,0},{24,20},{28,16},{1,13},{... | collective-permute-start | bytes 811016 | tf_op jit(solution)/shard_map/ppermute | solution.py:414
  10.2 5.1 %collective-permute-start.3 = (bf16[64,1024]{1,0:T(8,128)(2,1)S(1)}, bf16[64,1024]{1,0:T(8,128)(2,1)S(1)}, u32[]{:S(2)}, u32[]{:S(2)}) collective-permute-start(bf16[64,1024]{1,0:T(8,128)(2,1)S(1)} %constant_dynamic-update-slice_fusion.rest_0_), channel_id=1, source_target_pairs={{0,4},{4,0},{8,12},{12,8},{16,20},{20,16},{24,28},{28,24},{1,5},{5... | collective-permute-start | bytes 393224 | tf_op jit(solution)/shard_map/ppermute | solution.py:388
  10.8 19.4 %collective-permute-start.7 = (bf16[64,1024]{1,0:T(8,128)(2,1)S(1)}, bf16[64,1024]{1,0:T(8,128)(2,1)S(1)}, u32[]{:S(2)}, u32[]{:S(2)}) collective-permute-start(bf16[64,1024]{1,0:T(8,128)(2,1)S(1)} %constant_dynamic-update-slice_fusion.rest_0_), channel_id=1, source_target_pairs={{0,12},{4,8},{8,4},{12,0},{16,28},{20,24},{24,20},{28,16},{1,13},{... | collective-permute-start | bytes 393224 | tf_op jit(solution)/shard_map/ppermute | solution.py:388
  12.2 18.5 %collective-permute-start.6 = (bf16[64,1024]{1,0:T(8,128)(2,1)S(1)}, bf16[64,1024]{1,0:T(8,128)(2,1)S(1)}, u32[]{:S(2)}, u32[]{:S(2)}) collective-permute-start(bf16[64,1024]{1,0:T(8,128)(2,1)S(1)} %constant_dynamic-update-slice_fusion.rest_0_), channel_id=1, source_target_pairs={{0,8},{4,12},{8,0},{12,4},{16,24},{20,28},{24,16},{28,20},{1,9},{5... | collective-permute-start | bytes 393224 | tf_op jit(solution)/shard_map/ppermute | solution.py:388
  15.3 24.4 %collective-permute-start.4 = (bf16[528,256]{1,0:T(8,128)(2,1)S(1)}, bf16[528,256]{1,0:T(8,128)(2,1)S(1)}, u32[]{:S(2)}, u32[]{:S(2)}) collective-permute-start(bf16[528,256]{1,0:T(8,128)(2,1)S(1)} %get-tuple-element.73), channel_id=1, source_target_pairs={{0,16},{4,20},{8,0},{12,4},{16,24},{20,28},{24,8},{28,12},{1,17},{... | collective-permute-start | bytes 811016 | tf_op jit(solution)/shard_map/ppermute | solution.py:414
  30.2 14.3 %collective-permute-start.5 = (bf16[528,256]{1,0:T(8,128)(2,1)S(1)}, bf16[528,256]{1,0:T(8,128)(2,1)S(1)}, u32[]{:S(2)}, u32[]{:S(2)}) collective-permute-start(bf16[528,256]{1,0:T(8,128)(2,1)S(1)} %get-tuple-element.74), channel_id=1, source_target_pairs={{0,20},{4,16},{8,4},{12,0},{16,28},{20,24},{24,12},{28,8},{1,21},{... | collective-permute-start | bytes 811016 | tf_op jit(solution)/shard_map/ppermute | solution.py:414
  36.5 12.9 %collective-permute-start.8 = (bf16[528,256]{1,0:T(8,128)(2,1)S(1)}, bf16[528,256]{1,0:T(8,128)(2,1)S(1)}, u32[]{:S(2)}, u32[]{:S(2)}) collective-permute-start(bf16[528,256]{1,0:T(8,128)(2,1)S(1)} %get-tuple-element.96), channel_id=1, source_target_pairs={{0,24},{4,28},{8,16},{12,20},{16,8},{20,12},{24,0},{28,4},{1,25},{... | collective-permute-start | bytes 811016 | tf_op jit(solution)/shard_map/ppermute | solution.py:414
  36.5 15.2 %collective-permute-start.11 = (bf16[64,1152]{1,0:T(8,128)(2,1)S(1)}, bf16[64,1152]{1,0:T(8,128)(2,1)S(1)}, u32[]{:S(2)}, u32[]{:S(2)}) collective-permute-start(bf16[64,1152]{1,0:T(8,128)(2,1)S(1)} %get-tuple-element.102), channel_id=1, source_target_pairs={{0,4},{4,0},{8,12},{12,8},{16,20},{20,16},{24,28},{28,24},{1,5},{5... | collective-permute-start | bytes 442376 | tf_op jit(solution)/shard_map/ppermute | solution.py:388
  37.7 14.0 %collective-permute-start.12 = (bf16[64,1152]{1,0:T(8,128)(2,1)S(1)}, bf16[64,1152]{1,0:T(8,128)(2,1)S(1)}, u32[]{:S(2)}, u32[]{:S(2)}) collective-permute-start(bf16[64,1152]{1,0:T(8,128)(2,1)S(1)} %get-tuple-element.103.after_ref), channel_id=1, source_target_pairs={{0,8},{4,12},{8,0},{12,4},{16,24},{20,28},{24,16},{28,20},{1,9},{5... | collective-permute-start | bytes 442376 | tf_op jit(solution)/shard_map/ppermute | solution.py:388
  39.7 18.4 %collective-permute-start.13 = (bf16[64,1152]{1,0:T(8,128)(2,1)S(1)}, bf16[64,1152]{1,0:T(8,128)(2,1)S(1)}, u32[]{:S(2)}, u32[]{:S(2)}) collective-permute-start(bf16[64,1152]{1,0:T(8,128)(2,1)S(1)} %get-tuple-element.104), channel_id=1, source_target_pairs={{0,12},{4,8},{8,4},{12,0},{16,28},{20,24},{24,20},{28,16},{1,13},{... | collective-permute-start | bytes 442376 | tf_op jit(solution)/shard_map/ppermute | solution.py:388
  46.0 22.2 %collective-permute-start.10 = (bf16[528,256]{1,0:T(8,128)(2,1)S(1)}, bf16[528,256]{1,0:T(8,128)(2,1)S(1)}, u32[]{:S(2)}, u32[]{:S(2)}) collective-permute-start(bf16[528,256]{1,0:T(8,128)(2,1)S(1)} %get-tuple-element.101), channel_id=1, source_target_pairs={{0,28},{4,24},{8,20},{12,16},{16,12},{20,8},{24,4},{28,0},{1,29},{... | collective-permute-start | bytes 811016 | tf_op jit(solution)/shard_map/ppermute | solution.py:414
  50.8 17.4 %collective-permute-start.9 = (bf16[528,256]{1,0:T(8,128)(2,1)S(1)}, bf16[528,256]{1,0:T(8,128)(2,1)S(1)}, u32[]{:S(2)}, u32[]{:S(2)}) collective-permute-start(bf16[528,256]{1,0:T(8,128)(2,1)S(1)} %get-tuple-element.100), channel_id=1, source_target_pairs={{0,4},{4,0},{8,12},{12,8},{16,20},{20,16},{24,28},{28,24},{1,5},{5... | collective-permute-start | bytes 811016 | tf_op jit(solution)/shard_map/ppermute | solution.py:414
  58.6 5.9 %collective-permute-start.14 = (bf16[32,1152]{1,0:T(8,128)(2,1)S(1)}, bf16[32,1152]{1,0:T(8,128)(2,1)S(1)}, u32[]{:S(2)}, u32[]{:S(2)}) collective-permute-start(bf16[32,1152]{1,0:T(8,128)(2,1)S(1)} %reduce_other.1.after_ref), channel_id=1, source_target_pairs={{0,16},{4,20},{8,24},{12,28},{16,0},{20,4},{24,8},{28,12},{1,17},{... | collective-permute-start | bytes 221192 | tf_op jit(solution)/shard_map/ppermute | solution.py:495
  66.3 5.3 %collective-permute-start.15 = (bf16[32,1024]{1,0:T(8,128)(2,1)S(1)}, bf16[32,1024]{1,0:T(8,128)(2,1)S(1)}, u32[]{:S(2)}, u32[]{:S(2)}) collective-permute-start(bf16[32,1024]{1,0:T(8,128)(2,1)S(1)} %get-tuple-element.120), channel_id=1, source_target_pairs={{0,1},{1,0},{2,3},{3,2},{4,5},{5,4},{6,7},{7,6},{8,9},{9,8},{10,11... | collective-permute-start | bytes 196616 | tf_op jit(solution)/shard_map/ppermute | solution.py:519
  66.3 5.3 %collective-permute-start.16 = (bf16[32,1024]{1,0:T(8,128)(2,1)S(1)}, bf16[32,1024]{1,0:T(8,128)(2,1)S(1)}, u32[]{:S(2)}, u32[]{:S(2)}) collective-permute-start(bf16[32,1024]{1,0:T(8,128)(2,1)S(1)} %get-tuple-element.121), channel_id=1, source_target_pairs={{0,2},{1,3},{2,0},{3,1},{4,6},{5,7},{6,4},{7,5},{8,10},{9,11},{10,... | collective-permute-start | bytes 196616 | tf_op jit(solution)/shard_map/ppermute | solution.py:519
  67.9 4.1 %collective-permute-start.17 = (bf16[32,1024]{1,0:T(8,128)(2,1)S(1)}, bf16[32,1024]{1,0:T(8,128)(2,1)S(1)}, u32[]{:S(2)}, u32[]{:S(2)}) collective-permute-start(bf16[32,1024]{1,0:T(8,128)(2,1)S(1)} %get-tuple-element.122), channel_id=1, source_target_pairs={{0,3},{1,2},{2,1},{3,0},{4,7},{5,6},{6,5},{7,4},{8,11},{9,10},{10,... | collective-permute-start | bytes 196616 | tf_op jit(solution)/shard_map/ppermute | solution.py:519

commit v6 on v5

--- a/solution.py
+++ b/solution.py
@@ -259,6 +259,10 @@
     out_ref[...] = total.astype(bf16)
 
 
+def note_kernel(*refs):
+    refs[-1][...] = jnp.zeros_like(refs[-1])
+
+
 def put_kernel(me_ref, mig_ref, after_ref, *rest, ops, block, quarter, first, fill):
     gots = rest[: len(ops)]
     rest = rest[len(ops) :]
@@ -472,12 +476,20 @@
     parts = attend(q_all[:quarter], True)
     q_next, parts = lax.optimization_barrier((q_all[quarter:], parts))
     later = attend(q_next, False)
-    *filled, done = put(every("inner"), [], later[0])
+    done = pl.pallas_call(
+        note_kernel,
+        out_shape=token,
+        in_specs=[ANY] * (1 + quarter),
+        out_specs=VMEM,
+        compiler_params=limit(1),
+        cost_estimate=CHEAP,
+        name="note",
+    )(later[0], *[gots[op] for op in every("inner")])
     done = migrate(far[: quarter // 2], done)
     later, done = lax.optimization_barrier((later, done))
     parts = parts + later
     parts_got = to_mates(parts)
-    *filled, done = put(every("outer"), filled, done)
+    *filled, done = put(every("inner") + every("outer"), [], done)
     done = migrate(far[quarter // 2 :], done)
     *filled, done = put([], filled, done, fill=True)
     *filled, done = put(far[: quarter // 2], filled, done)

time: 73.2 us -> 73.2 us (level)
  Pallas kernels: 29.5 us -> 28.2 us
  waiting for transfers between devices: 15 us -> 16.2 us
    ppermute x7, waiting for transfers between devices: 4.36 us -> 7.41 us  [migrate(): lax.ppermute(send, 'seq', [(i, i ^ deltas(i, *op, quarter)[0]) for i in r...]
    ppermute x6, waiting for transfers between devices: 7.93 us -> 6.11 us  [to_mates(): lax.ppermute(parts[e], 'seq', beside[e])]
    pallas_call x4 -> x3, Pallas kernels: 7.73 us -> 6.44 us  [put(): pl.pallas_call(functools.partial(put_kernel, ops=which, block=block, quar...]
  transfers between devices with their start and end apart: 18 -> 18, of which waited for: 5 -> 5; matrix products, arithmetic and copies ran while one was open for 0% -> 0% of each run, Pallas kernels for 40% -> 38%
where the time goes in v6:
time: 73.2 us; the launch traced here: 72.7 us
  Pallas kernels  28.2 us (39%)
  starting transfers between devices  27.4 us (37%)
  waiting for transfers between devices  16.2 us (22%)
  between operations  0.82 us (1%)
    ppermute x7, starting transfers between devices, migrate(): lax.ppermute(send, 'seq', [(i, i ^ deltas(i, *op, quarter)[0]) for i in r...  14.3 us
    pallas_call x2, Pallas kernels, attend(): pl.pallas_call(functools.partial(attend_kernel, count=count, block=block,...  9.35 us
    ppermute x7, waiting for transfers between devices, migrate(): lax.ppermute(send, 'seq', [(i, i ^ deltas(i, *op, quarter)[0]) for i in r...  7.41 us
    ppermute x6, starting transfers between devices, to_mates(): lax.ppermute(parts[e], 'seq', beside[e])  7.12 us
    pallas_call x3, Pallas kernels, put(): pl.pallas_call(functools.partial(put_kernel, ops=which, block=block, quar...  6.44 us
    ppermute x6, waiting for transfers between devices, to_mates(): lax.ppermute(parts[e], 'seq', beside[e])  6.11 us
    ppermute x1, starting transfers between devices, per_device(): q_mirror = lax.ppermute(draft_q, 'seq', across)  4.1 us
    pallas_call x1, Pallas kernels, per_device(): pl.pallas_call(weight_kernel, out_shape=pltpu.VMEM((ways, q_width, width)...  3.53 us
  transfers between devices with their start and end apart: 18, of which 5 were waited for; matrix products, arithmetic and copies ran while one was open for 0% of the time, Pallas kernels for 38%

profile of v6, /device:TPU:0, one launch (start us, length us, event | category | flops | bytes accessed | tf_op | source)
XLA Modules:
  0.0 72.7 jit_solution(2361612088960896864)
XLA Ops:
  0.6 4.1 %collective-permute-start = (bf16[32,1024]{1,0:T(8,128)(2,1)}, bf16[32,1024]{1,0:T(8,128)(2,1)S(1)}, u32[]{:S(2)}, u32[]{:S(2)}) collective-permute-start(bf16[32,1024]{1,0:T(8,128)(2,1)} %param.10), channel_id=1, source_target_pairs={{0,16},{4,20},{8,24},{12,28},{16,0},{20,4},{24,8},{28,12},{1,17},{... | collective-permute-start | bytes 196616 | tf_op jit(solution)/shard_map/ppermute | solution.py:395
  4.7 2.5 %prep.1 = (bf16[528,256]{1,0:T(8,128)(2,1)S(1)}, bf16[528,256]{1,0:T(8,128)(2,1)S(1)}, bf16[528,256]{1,0:T(8,128)(2,1)S(1)}, bf16[528,256]{1,0:T(8,128)(2,1)S(1)...) custom-call(s32[1]{0:T(128)} %bitcast.me_ref, ...), custom_call_target="tpu_custom_call" | custom-call | flops 1 | bytes 1 | tf_op jit(solution)/shard_map/prep/pallas_call | solution.py:401
  7.3 1.6 %collective-permute-start.1 = (bf16[528,256]{1,0:T(8,128)(2,1)S(1)}, bf16[528,256]{1,0:T(8,128)(2,1)S(1)}, u32[]{:S(2)}, u32[]{:S(2)}) collective-permute-start(bf16[528,256]{1,0:T(8,128)(2,1)S(1)} %get-tuple-element.65), channel_id=1, source_target_pairs={{0,8},{4,12},{8,24},{12,28},{16,0},{20,4},{24,16},{28,20},{1,9},{5... | collective-permute-start | bytes 811016 | tf_op jit(solution)/shard_map/ppermute | solution.py:418
  8.9 1.3 %collective-permute-start.2 = (bf16[528,256]{1,0:T(8,128)(2,1)S(1)}, bf16[528,256]{1,0:T(8,128)(2,1)S(1)}, u32[]{:S(2)}, u32[]{:S(2)}) collective-permute-start(bf16[528,256]{1,0:T(8,128)(2,1)S(1)} %get-tuple-element.66), channel_id=1, source_target_pairs={{0,12},{4,8},{8,28},{12,24},{16,4},{20,0},{24,20},{28,16},{1,13},{... | collective-permute-start | bytes 811016 | tf_op jit(solution)/shard_map/ppermute | solution.py:418
  10.2 0.0 copy-done
  10.2 0.0 collective-permute-done
  10.2 0.6 collective-permute-start.3
  10.8 1.4 %collective-permute-start.7 = (bf16[64,1024]{1,0:T(8,128)(2,1)S(1)}, bf16[64,1024]{1,0:T(8,128)(2,1)S(1)}, u32[]{:S(2)}, u32[]{:S(2)}) collective-permute-start(bf16[64,1024]{1,0:T(8,128)(2,1)S(1)} %constant_dynamic-update-slice_fusion.rest_0_), channel_id=1, source_target_pairs={{0,12},{4,8},{8,4},{12,0},{16,28},{20,24},{24,20},{28,16},{1,13},{... | collective-permute-start | bytes 393224 | tf_op jit(solution)/shard_map/ppermute | solution.py:392
  12.2 1.6 %collective-permute-start.6 = (bf16[64,1024]{1,0:T(8,128)(2,1)S(1)}, bf16[64,1024]{1,0:T(8,128)(2,1)S(1)}, u32[]{:S(2)}, u32[]{:S(2)}) collective-permute-start(bf16[64,1024]{1,0:T(8,128)(2,1)S(1)} %constant_dynamic-update-slice_fusion.rest_0_), channel_id=1, source_target_pairs={{0,8},{4,12},{8,0},{12,4},{16,24},{20,28},{24,16},{28,20},{1,9},{5... | collective-permute-start | bytes 393224 | tf_op jit(solution)/shard_map/ppermute | solution.py:392
  13.8 1.5 %collective-permute-done.3.rest_1_ = bf16[64,1024]{1,0:T(8,128)(2,1)S(1)} collective-permute-done((bf16[64,1024]{1,0:T(8,128)(2,1)S(1)}, bf16[64,1024]{1,0:T(8,128)(2,1)S(1)}, u32[]{:S(2)}, u32[]{:S(2)}) %collective-permute-start.3) | collective-permute-done | bytes 131104 | tf_op jit(solution)/shard_map/ppermute | solution.py:392
  15.3 9.8 %collective-permute-start.4 = (bf16[528,256]{1,0:T(8,128)(2,1)S(1)}, bf16[528,256]{1,0:T(8,128)(2,1)S(1)}, u32[]{:S(2)}, u32[]{:S(2)}) collective-permute-start(bf16[528,256]{1,0:T(8,128)(2,1)S(1)} %get-tuple-element.70), channel_id=1, source_target_pairs={{0,16},{4,20},{8,0},{12,4},{16,24},{20,28},{24,8},{28,12},{1,17},{... | collective-permute-start | bytes 811016 | tf_op jit(solution)/shard_map/ppermute | solution.py:418
  25.1 5.1 %attend_own.1 = (bf16[64,1152]{1,0:T(8,128)(2,1)S(1)}, bf16[64,1152]{1,0:T(8,128)(2,1)S(1)}) custom-call(s32[1]{0:T(128)} %bitcast.me_ref, s32[4]{0:T(128)} %len_ref.5, s32[4]{0:T(128)} %mig_ref.13, bf16[64,1024]{1,0:T(8,128)(2,1)S(1)} %constant_dynamic-update-slice_fusion.rest_0_, bf16[64,1024]{1,0:T(8,128)(2,1)S(1)} %collective-permute-done.3.rest_1_, ...), custom_call_target="tpu_custom_call" | custom-call | flops 1 | bytes 1 | tf_op jit(solution)/shard_map/attend_own/pallas_call | solution.py:458
  30.2 0.0 collective-permute-done.7.rest_1_
  30.2 0.5 collective-permute-start.5
  30.7 0.0 collective-permute-done.6.rest_0_
  30.7 4.2 %attend_next.1 = (bf16[64,1152]{1,0:T(8,128)(2,1)S(1)}, bf16[64,1152]{1,0:T(8,128)(2,1)S(1)}) custom-call(s32[1]{0:T(128)} %bitcast.me_ref, s32[4]{0:T(128)} %len_ref.5, s32[4]{0:T(128)} %mig_ref.13, bf16[64,1024]{1,0:T(8,128)(2,1)S(1)} %collective-permute-done.6.rest_0_, bf16[64,1024]{1,0:T(8,128)(2,1)S(1)} %collective-permute-done.7.rest_1_, ...), custom_call_target="tpu_custom_call" | custom-call | flops 1 | bytes 1 | tf_op jit(solution)/shard_map/attend_next/pallas_call | solution.py:458
  34.9 0.0 collective-permute-done.1.refs_1_.rest_0_
  34.9 0.0 collective-permute-done.2.refs_2_.rest_1_
  34.9 0.1 collective-permute-start.8
  35.0 1.1 %collective-permute-start.11 = (bf16[64,1152]{1,0:T(8,128)(2,1)S(1)}, bf16[64,1152]{1,0:T(8,128)(2,1)S(1)}, u32[]{:S(2)}, u32[]{:S(2)}) collective-permute-start(bf16[64,1152]{1,0:T(8,128)(2,1)S(1)} %get-tuple-element.96), channel_id=1, source_target_pairs={{0,4},{4,0},{8,12},{12,8},{16,20},{20,16},{24,28},{28,24},{1,5},{5... | collective-permute-start | bytes 442376 | tf_op jit(solution)/shard_map/ppermute | solution.py:392
  36.2 2.0 %collective-permute-start.12 = (bf16[64,1152]{1,0:T(8,128)(2,1)S(1)}, bf16[64,1152]{1,0:T(8,128)(2,1)S(1)}, u32[]{:S(2)}, u32[]{:S(2)}) collective-permute-start(bf16[64,1152]{1,0:T(8,128)(2,1)S(1)} %get-tuple-element.97.refs_0_), channel_id=1, source_target_pairs={{0,8},{4,12},{8,0},{12,4},{16,24},{20,28},{24,16},{28,20},{1,9},{5... | collective-permute-start | bytes 442376 | tf_op jit(solution)/shard_map/ppermute | solution.py:392
  38.2 0.0 collective-permute-done.4.rest_2_
  38.2 0.4 collective-permute-start.13
  38.6 7.4 %collective-permute-done.5.rest_3_ = bf16[528,256]{1,0:T(8,128)(2,1)S(1)} collective-permute-done((bf16[528,256]{1,0:T(8,128)(2,1)S(1)}, bf16[528,256]{1,0:T(8,128)(2,1)S(1)}, u32[]{:S(2)}, u32[]{:S(2)}) %collective-permute-start.5) | collective-permute-done | bytes 270368 | tf_op jit(solution)/shard_map/ppermute | solution.py:418
  46.0 1.8 %put.3 = (bf16[4,1024,256]{2,1,0:T(8,128)(2,1)}, bf16[4,1024,256]{2,1,0:T(8,128)(2,1)}, f32[8,128]{1,0:T(8,128)S(1)}) custom-call(s32[1]{0:T(128)} %bitcast.me_ref, s32[4]{0:T(128)} %mig_ref.13, f32[8,128]{1,0:T(8,128)S(1)} %note.1.after_ref, bf16[528,256]{1,0:T(8,128)(2,1)S(1)} %collective-permute-done.1.refs_1_.rest_0_, ...), custom_call_target="tpu_custom_call" | custom-call | flops 1 | bytes 1 | tf_op jit(solution)/shard_map/put/pallas_call | solution.py:441
  47.8 0.1 collective-permute-start.10
  47.8 3.3 %put.4 = (bf16[4,1024,256]{2,1,0:T(8,128)(2,1)}, bf16[4,1024,256]{2,1,0:T(8,128)(2,1)}, f32[8,128]{1,0:T(8,128)S(1)}) custom-call(s32[1]{0:T(128)} %bitcast.me_ref, s32[4]{0:T(128)} %mig_ref.13, f32[8,128]{1,0:T(8,128)S(1)} %get-tuple-element.86.after_ref, bf16[4,1024,256]{2,1,0:T(8,128)(2,1)} %rest_0_.1, ...), custom_call_target="tpu_custom_call", output_to_operand_aliasing={{0}: (5, {}), {1}: (6, {})} | custom-call | flops 1 | bytes 1 | tf_op jit(solution)/shard_map/put/pallas_call | solution.py:441
  51.1 0.0 collective-permute-done.8.rest_0_.rest_5_
  51.1 1.4 %put.5 = (bf16[4,1024,256]{2,1,0:T(8,128)(2,1)}, bf16[4,1024,256]{2,1,0:T(8,128)(2,1)}, f32[8,128]{1,0:T(8,128)S(1)}) custom-call(s32[1]{0:T(128)} %bitcast.me_ref, s32[4]{0:T(128)} %mig_ref.13, f32[8,128]{1,0:T(8,128)S(1)} %get-tuple-element.89.after_ref, ...), custom_call_target="tpu_custom_call", output_to_operand_aliasing={{0}: (4, {}), {1}: (5, {})} | custom-call | flops 1 | bytes 1 | tf_op jit(solution)/shard_map/put/pallas_call | solution.py:441
  52.5 1.0 %collective-permute-start.9 = (bf16[528,256]{1,0:T(8,128)(2,1)S(1)}, bf16[528,256]{1,0:T(8,128)(2,1)S(1)}, u32[]{:S(2)}, u32[]{:S(2)}) collective-permute-start(bf16[528,256]{1,0:T(8,128)(2,1)S(1)} %get-tuple-element.94), channel_id=1, source_target_pairs={{0,4},{4,0},{8,12},{12,8},{16,20},{20,16},{24,28},{28,24},{1,5},{5... | collective-permute-start | bytes 811016 | tf_op jit(solution)/shard_map/ppermute | solution.py:418
  53.5 0.0 collective-permute-done.11.refs_1_
  53.5 0.0 collective-permute-done.12.refs_2_
  53.5 4.6 %collective-permute-done.13.refs_3_ = bf16[64,1152]{1,0:T(8,128)(2,1)S(1)} collective-permute-done((bf16[64,1152]{1,0:T(8,128)(2,1)S(1)}, bf16[64,1152]{1,0:T(8,128)(2,1)S(1)}, u32[]{:S(2)}, u32[]{:S(2)}) %collective-permute-start.13) | collective-permute-done | bytes 147488 | tf_op jit(solution)/shard_map/ppermute | solution.py:392
  58.1 0.4 reduce_other.1.after_ref
  58.6 0.1 collective-permute-start.14
  58.7 3.5 %weight.1.refs_5_ = bf16[4,1024,1024]{2,1,0:T(8,128)(2,1)S(1)} custom-call(s32[1]{0:T(128)} %bitcast.1.tp_ref, bf16[32,1152]{1,0:T(8,128)(2,1)S(1)} %reduce_other.1.after_ref, bf16[1024,4096]{1,0:T(8,128)(2,1)} %w_ref.1), custom_call_target="tpu_custom_call" | custom-call | flops 1 | bytes 1 | tf_op jit(solution)/shard_map/weight/pallas_call | solution.py:510
  62.2 2.2 %collective-permute-done.14.refs_4_ = bf16[32,1152]{1,0:T(8,128)(2,1)S(1)} collective-permute-done((bf16[32,1152]{1,0:T(8,128)(2,1)S(1)}, bf16[32,1152]{1,0:T(8,128)(2,1)S(1)}, u32[]{:S(2)}, u32[]{:S(2)}) %collective-permute-start.14) | collective-permute-done | bytes 73760 | tf_op jit(solution)/shard_map/ppermute | solution.py:507
  64.5 1.8 %project.1 = (bf16[32,1024]{1,0:T(8,128)(2,1)S(1)}, bf16[32,1024]{1,0:T(8,128)(2,1)S(1)}, bf16[32,1024]{1,0:T(8,128)(2,1)S(1)}, f32[32,1024]{1,0:T(8,128)S(1)}) custom-call(f32[8,128]{1,0:T(8,128)S(1)} %get-tuple-element.100.done_ref, bf16[64,1152]{1,0:T(8,128)(2,1)S(1)} %get-tuple-element.101.refs_0_, bf16[64,1152]{1,0:T(8,128)(2,1)S(1)} %collective-permute-done.11.refs_1_, ...), custom_call_target="tpu_custom_call" | custom-call | flops 1 | bytes 1 | tf_op jit(solution)/shard_map/project/pallas_call | solution.py:521
  66.3 0.0 collective-permute-start.15
  66.3 1.6 %collective-permute-start.16 = (bf16[32,1024]{1,0:T(8,128)(2,1)S(1)}, bf16[32,1024]{1,0:T(8,128)(2,1)S(1)}, u32[]{:S(2)}, u32[]{:S(2)}) collective-permute-start(bf16[32,1024]{1,0:T(8,128)(2,1)S(1)} %get-tuple-element.115), channel_id=1, source_target_pairs={{0,2},{1,3},{2,0},{3,1},{4,6},{5,7},{6,4},{7,5},{8,10},{9,11},{10,... | collective-permute-start | bytes 196616 | tf_op jit(solution)/shard_map/ppermute | solution.py:531
  67.9 0.3 collective-permute-start.17
  68.1 0.0 collective-permute-done.10.rest_6_
  68.2 0.0 collective-permute-done.9.rest_4_
  68.2 3.4 %place.1 = (bf16[4,1024,256]{2,1,0:T(8,128)(2,1)}, bf16[4,1024,256]{2,1,0:T(8,128)(2,1)}, f32[8,128]{1,0:T(8,128)S(1)}) custom-call(s32[1]{0:T(128)} %bitcast.me_ref, s32[4]{0:T(128)} %mig_ref.13, s32[4]{0:T(128)} %len_ref.5, s32[4,8]{1,0:T(4,128)} %accepted_ref.3, ...), custom_call_target="tpu_custom_call", output_to_operand_aliasing={{0}: (12, {}), {1}: (13, {})} | custom-call | flops 1 | bytes 1 | tf_op jit(solution)/shard_map/place/pallas_call | solution.py:536
  71.5 0.0 collective-permute-done.15.rest_0_
  71.6 0.0 collective-permute-done.16.rest_1_
  71.6 0.5 collective-permute-done.17.rest_2_
  72.0 0.7 final.1
  (4 shorter events, 0.0 us)
Async XLA Ops:
  0.6 9.6 %collective-permute-start = (bf16[32,1024]{1,0:T(8,128)(2,1)}, bf16[32,1024]{1,0:T(8,128)(2,1)S(1)}, u32[]{:S(2)}, u32[]{:S(2)}) collective-permute-start(bf16[32,1024]{1,0:T(8,128)(2,1)} %param.10), channel_id=1, source_target_pairs={{0,16},{4,20},{8,24},{12,28},{16,0},{20,4},{24,8},{28,12},{1,17},{... | collective-permute-start | bytes 196616 | tf_op jit(solution)/shard_map/ppermute | solution.py:395
  4.7 5.4 %copy-start = (bf16[32,1024]{1,0:T(8,128)(2,1)S(1)}, bf16[32,1024]{1,0:T(8,128)(2,1)}, u32[]{:S(2)}) copy-start(bf16[32,1024]{1,0:T(8,128)(2,1)} %param.10) | copy-start | bytes 196612
  7.3 27.6 %collective-permute-start.1 = (bf16[528,256]{1,0:T(8,128)(2,1)S(1)}, bf16[528,256]{1,0:T(8,128)(2,1)S(1)}, u32[]{:S(2)}, u32[]{:S(2)}) collective-permute-start(bf16[528,256]{1,0:T(8,128)(2,1)S(1)} %get-tuple-element.65), channel_id=1, source_target_pairs={{0,8},{4,12},{8,24},{12,28},{16,0},{20,4},{24,16},{28,20},{1,9},{5... | collective-permute-start | bytes 811016 | tf_op jit(solution)/shard_map/ppermute | solution.py:418
  8.9 26.0 %collective-permute-start.2 = (bf16[528,256]{1,0:T(8,128)(2,1)S(1)}, bf16[528,256]{1,0:T(8,128)(2,1)S(1)}, u32[]{:S(2)}, u32[]{:S(2)}) collective-permute-start(bf16[528,256]{1,0:T(8,128)(2,1)S(1)} %get-tuple-element.66), channel_id=1, source_target_pairs={{0,12},{4,8},{8,28},{12,24},{16,4},{20,0},{24,20},{28,16},{1,13},{... | collective-permute-start | bytes 811016 | tf_op jit(solution)/shard_map/ppermute | solution.py:418
  10.2 5.1 %collective-permute-start.3 = (bf16[64,1024]{1,0:T(8,128)(2,1)S(1)}, bf16[64,1024]{1,0:T(8,128)(2,1)S(1)}, u32[]{:S(2)}, u32[]{:S(2)}) collective-permute-start(bf16[64,1024]{1,0:T(8,128)(2,1)S(1)} %constant_dynamic-update-slice_fusion.rest_0_), channel_id=1, source_target_pairs={{0,4},{4,0},{8,12},{12,8},{16,20},{20,16},{24,28},{28,24},{1,5},{5... | collective-permute-start | bytes 393224 | tf_op jit(solution)/shard_map/ppermute | solution.py:392
  10.8 19.4 %collective-permute-start.7 = (bf16[64,1024]{1,0:T(8,128)(2,1)S(1)}, bf16[64,1024]{1,0:T(8,128)(2,1)S(1)}, u32[]{:S(2)}, u32[]{:S(2)}) collective-permute-start(bf16[64,1024]{1,0:T(8,128)(2,1)S(1)} %constant_dynamic-update-slice_fusion.rest_0_), channel_id=1, source_target_pairs={{0,12},{4,8},{8,4},{12,0},{16,28},{20,24},{24,20},{28,16},{1,13},{... | collective-permute-start | bytes 393224 | tf_op jit(solution)/shard_map/ppermute | solution.py:392
  12.2 18.5 %collective-permute-start.6 = (bf16[64,1024]{1,0:T(8,128)(2,1)S(1)}, bf16[64,1024]{1,0:T(8,128)(2,1)S(1)}, u32[]{:S(2)}, u32[]{:S(2)}) collective-permute-start(bf16[64,1024]{1,0:T(8,128)(2,1)S(1)} %constant_dynamic-update-slice_fusion.rest_0_), channel_id=1, source_target_pairs={{0,8},{4,12},{8,0},{12,4},{16,24},{20,28},{24,16},{28,20},{1,9},{5... | collective-permute-start | bytes 393224 | tf_op jit(solution)/shard_map/ppermute | solution.py:392
  15.3 22.9 %collective-permute-start.4 = (bf16[528,256]{1,0:T(8,128)(2,1)S(1)}, bf16[528,256]{1,0:T(8,128)(2,1)S(1)}, u32[]{:S(2)}, u32[]{:S(2)}) collective-permute-start(bf16[528,256]{1,0:T(8,128)(2,1)S(1)} %get-tuple-element.70), channel_id=1, source_target_pairs={{0,16},{4,20},{8,0},{12,4},{16,24},{20,28},{24,8},{28,12},{1,17},{... | collective-permute-start | bytes 811016 | tf_op jit(solution)/shard_map/ppermute | solution.py:418
  30.2 15.8 %collective-permute-start.5 = (bf16[528,256]{1,0:T(8,128)(2,1)S(1)}, bf16[528,256]{1,0:T(8,128)(2,1)S(1)}, u32[]{:S(2)}, u32[]{:S(2)}) collective-permute-start(bf16[528,256]{1,0:T(8,128)(2,1)S(1)} %get-tuple-element.71), channel_id=1, source_target_pairs={{0,20},{4,16},{8,4},{12,0},{16,28},{20,24},{24,12},{28,8},{1,21},{... | collective-permute-start | bytes 811016 | tf_op jit(solution)/shard_map/ppermute | solution.py:418
  34.9 16.2 %collective-permute-start.8 = (bf16[528,256]{1,0:T(8,128)(2,1)S(1)}, bf16[528,256]{1,0:T(8,128)(2,1)S(1)}, u32[]{:S(2)}, u32[]{:S(2)}) collective-permute-start(bf16[528,256]{1,0:T(8,128)(2,1)S(1)} %get-tuple-element.90), channel_id=1, source_target_pairs={{0,24},{4,28},{8,16},{12,20},{16,8},{20,12},{24,0},{28,4},{1,25},{... | collective-permute-start | bytes 811016 | tf_op jit(solution)/shard_map/ppermute | solution.py:418
  35.0 18.5 %collective-permute-start.11 = (bf16[64,1152]{1,0:T(8,128)(2,1)S(1)}, bf16[64,1152]{1,0:T(8,128)(2,1)S(1)}, u32[]{:S(2)}, u32[]{:S(2)}) collective-permute-start(bf16[64,1152]{1,0:T(8,128)(2,1)S(1)} %get-tuple-element.96), channel_id=1, source_target_pairs={{0,4},{4,0},{8,12},{12,8},{16,20},{20,16},{24,28},{28,24},{1,5},{5... | collective-permute-start | bytes 442376 | tf_op jit(solution)/shard_map/ppermute | solution.py:392
  36.2 17.4 %collective-permute-start.12 = (bf16[64,1152]{1,0:T(8,128)(2,1)S(1)}, bf16[64,1152]{1,0:T(8,128)(2,1)S(1)}, u32[]{:S(2)}, u32[]{:S(2)}) collective-permute-start(bf16[64,1152]{1,0:T(8,128)(2,1)S(1)} %get-tuple-element.97.refs_0_), channel_id=1, source_target_pairs={{0,8},{4,12},{8,0},{12,4},{16,24},{20,28},{24,16},{28,20},{1,9},{5... | collective-permute-start | bytes 442376 | tf_op jit(solution)/shard_map/ppermute | solution.py:392
  38.2 20.0 %collective-permute-start.13 = (bf16[64,1152]{1,0:T(8,128)(2,1)S(1)}, bf16[64,1152]{1,0:T(8,128)(2,1)S(1)}, u32[]{:S(2)}, u32[]{:S(2)}) collective-permute-start(bf16[64,1152]{1,0:T(8,128)(2,1)S(1)} %get-tuple-element.98), channel_id=1, source_target_pairs={{0,12},{4,8},{8,4},{12,0},{16,28},{20,24},{24,20},{28,16},{1,13},{... | collective-permute-start | bytes 442376 | tf_op jit(solution)/shard_map/ppermute | solution.py:392
  47.8 20.4 %collective-permute-start.10 = (bf16[528,256]{1,0:T(8,128)(2,1)S(1)}, bf16[528,256]{1,0:T(8,128)(2,1)S(1)}, u32[]{:S(2)}, u32[]{:S(2)}) collective-permute-start(bf16[528,256]{1,0:T(8,128)(2,1)S(1)} %get-tuple-element.95), channel_id=1, source_target_pairs={{0,28},{4,24},{8,20},{12,16},{16,12},{20,8},{24,4},{28,0},{1,29},{... | collective-permute-start | bytes 811016 | tf_op jit(solution)/shard_map/ppermute | solution.py:418
  52.5 15.6 %collective-permute-start.9 = (bf16[528,256]{1,0:T(8,128)(2,1)S(1)}, bf16[528,256]{1,0:T(8,128)(2,1)S(1)}, u32[]{:S(2)}, u32[]{:S(2)}) collective-permute-start(bf16[528,256]{1,0:T(8,128)(2,1)S(1)} %get-tuple-element.94), channel_id=1, source_target_pairs={{0,4},{4,0},{8,12},{12,8},{16,20},{20,16},{24,28},{28,24},{1,5},{5... | collective-permute-start | bytes 811016 | tf_op jit(solution)/shard_map/ppermute | solution.py:418
  58.6 5.9 %collective-permute-start.14 = (bf16[32,1152]{1,0:T(8,128)(2,1)S(1)}, bf16[32,1152]{1,0:T(8,128)(2,1)S(1)}, u32[]{:S(2)}, u32[]{:S(2)}) collective-permute-start(bf16[32,1152]{1,0:T(8,128)(2,1)S(1)} %reduce_other.1.after_ref), channel_id=1, source_target_pairs={{0,16},{4,20},{8,24},{12,28},{16,0},{20,4},{24,8},{28,12},{1,17},{... | collective-permute-start | bytes 221192 | tf_op jit(solution)/shard_map/ppermute | solution.py:507
  66.3 5.3 %collective-permute-start.15 = (bf16[32,1024]{1,0:T(8,128)(2,1)S(1)}, bf16[32,1024]{1,0:T(8,128)(2,1)S(1)}, u32[]{:S(2)}, u32[]{:S(2)}) collective-permute-start(bf16[32,1024]{1,0:T(8,128)(2,1)S(1)} %get-tuple-element.114), channel_id=1, source_target_pairs={{0,1},{1,0},{2,3},{3,2},{4,5},{5,4},{6,7},{7,6},{8,9},{9,8},{10,11... | collective-permute-start | bytes 196616 | tf_op jit(solution)/shard_map/ppermute | solution.py:531
  66.3 5.3 %collective-permute-start.16 = (bf16[32,1024]{1,0:T(8,128)(2,1)S(1)}, bf16[32,1024]{1,0:T(8,128)(2,1)S(1)}, u32[]{:S(2)}, u32[]{:S(2)}) collective-permute-start(bf16[32,1024]{1,0:T(8,128)(2,1)S(1)} %get-tuple-element.115), channel_id=1, source_target_pairs={{0,2},{1,3},{2,0},{3,1},{4,6},{5,7},{6,4},{7,5},{8,10},{9,11},{10,... | collective-permute-start | bytes 196616 | tf_op jit(solution)/shard_map/ppermute | solution.py:531
  67.9 4.1 %collective-permute-start.17 = (bf16[32,1024]{1,0:T(8,128)(2,1)S(1)}, bf16[32,1024]{1,0:T(8,128)(2,1)S(1)}, u32[]{:S(2)}, u32[]{:S(2)}) collective-permute-start(bf16[32,1024]{1,0:T(8,128)(2,1)S(1)} %get-tuple-element.116), channel_id=1, source_target_pairs={{0,3},{1,2},{2,1},{3,0},{4,7},{5,6},{6,5},{7,4},{8,11},{9,10},{10,... | collective-permute-start | bytes 196616 | tf_op jit(solution)/shard_map/ppermute | solution.py:531
